TPU v7x, 32 devices: a whole 2x2x4 slice. The times are simulated.
32 devices in a mesh: scan: 4 (over x, core), pix: 8 (over z, y).
Axes of the slice: x: 2, y: 2, z: 4, core: 2. Of those that a mesh axis runs over, the one named last changes fastest.
Arguments:
- raw_frames: float32 [1536, 128, 128], P(('scan', 'pix')), may hold values from 0.2 to 5
- gain_map: float32 [128, 128], replicated, may hold values from 0.5 to 1.5
- coupling: float32 [128, 128], replicated, may hold values from 0.05 to 0.25
- factor_w: float32 [1536, 256], P(('scan', 'pix')), may hold values from 0.01 to 0.25
- factor_h: float32 [256, 16384], P('scan', 'pix'), may hold values from 0.01 to 0.25
Outputs:
- w_factor: float32 [1536, 256], P(('scan', 'pix'))
- h_factor: float32 [256, 16384], P('scan', 'pix')
All inputs are finite; a program needn't handle non-finite values.
Results may differ from a plain program's by a relative error of at most 0.0003.
Values may be sent and summed in bfloat16 or wider, within the bound.
No kernel may reach another device: no remote copies, remote signals or barrier semaphores. Data moves between devices by JAX's collectives and lax.ppermute only.
A program may use at most 64 MiB of HBM per device.

v0:
```python
import functools

import jax
import jax.numpy as jnp
from jax import lax
from jax.experimental import pallas as pl
from jax.experimental.pallas import tpu as pltpu
from jax.sharding import PartitionSpec as P

SWEEPS = 4
ITERS = 2
BF16, F16, F32 = jnp.bfloat16, jnp.float16, jnp.float32


def stencil_body(me_ref, raw_ref, gain_ref, couple_ref, w_ref, *refs):
    out_refs, (gain_s, near_s, stage) = refs[:-3], refs[-3:]
    rows, cols = gain_ref.shape
    parts, frames, pixels = stage.shape
    groups = frames // 8
    band = rows // parts

    @pl.when(pl.program_id(0) == 0)
    def _():
        inverse = 1.0 / (1.0 + 4.0 * couple_ref[...])
        gain_s[...] = gain_ref[...] * inverse
        near_s[...] = couple_ref[...] * inverse

    lane = lax.broadcasted_iota(jnp.int32, (8, cols), 1)
    has_left = jnp.where(lane == 0, 0.0, 1.0)
    has_right = jnp.where(lane == cols - 1, 0.0, 1.0)
    zero = jnp.zeros((8, cols), F32)

    def every(ref, row):
        return ref[pl.ds(row, 8, stride=0), :]

    def advance(state, row, end=False):
        levels, scaled, weight = state
        if end:
            w_new = zero
            enter = [zero] * groups
            s_new = [zero] * groups
        else:
            w_new = every(near_s, row)
            gain = every(gain_ref, row)
            gain_scaled = every(gain_s, row)
            raws = [raw_ref[pl.ds(g * 8 * rows + row, 8, stride=rows), :] for g in range(groups)]
            enter = [raw * gain for raw in raws]
            s_new = [raw * gain_scaled for raw in raws]
        out, new_levels = [], []
        for g in range(groups):
            new = enter[g]
            mine = []
            for k in range(SWEEPS):
                older, newer = levels[g][k]
                side = pltpu.roll(newer, 1, 1) * has_left + pltpu.roll(newer, cols - 1, 1) * has_right
                value = scaled[g][k] + weight[k] * ((older + side) + new)
                mine.append((newer, new))
                new = value
            out.append(new)
            new_levels.append(mine)
        scaled = [[s_new[g]] + scaled[g][: SWEEPS - 1] for g in range(groups)]
        return (new_levels, scaled, [w_new] + weight[: SWEEPS - 1]), out

    frame = lax.broadcasted_iota(jnp.int32, (frames, cols), 0) + frames * pl.program_id(0)
    phase = frame.astype(F32) * 0.6180340 + lax.broadcasted_iota(jnp.int32, (frames, cols), 1).astype(F32) * 0.7548777
    shift = (phase - jnp.floor(phase) - 0.5) * 0.005

    def one_band(part, state, error, first=False, last=False):
        for i in range(band):
            state, out = advance(state, part * band + SWEEPS + i, end=last and i + SWEEPS >= band)
            value = jnp.concatenate(out, axis=0)
            value = value + (value * shift if first and i == 0 else error)
            rounded = value.astype(BF16)
            error = value - rounded.astype(F32)
            stage[part, :, i * cols : (i + 1) * cols] = rounded
        return state, error

    state = (
        [[(zero, zero)] * SWEEPS for _ in range(groups)],
        [[zero] * SWEEPS for _ in range(groups)],
        [zero] * SWEEPS,
    )
    for row in range(SWEEPS):
        state, _ = advance(state, row)
    carry = one_band(0, state, None, first=True)
    carry = lax.fori_loop(1, parts - 1, lambda part, c: one_band(part, *c), carry)
    one_band(parts - 1, *carry, last=True)
    w_mine = w_ref[...].astype(BF16)
    for r, out_ref in enumerate(out_refs):
        out_ref[:, :pixels] = stage[jnp.bitwise_xor(me_ref[0], r)]
        out_ref[:, pixels:] = w_mine


def correct(raw_frames, gain_map, coupling, w_local, me, parts, start, count):
    frames, rows, cols = raw_frames.shape
    rank = w_local.shape[1]
    group = 16
    pixels = rows * cols // parts
    first = start // group
    return pl.pallas_call(
        stencil_body,
        out_shape=[jax.ShapeDtypeStruct((count, pixels + rank), BF16)] * parts,
        grid_spec=pltpu.PrefetchScalarGridSpec(
            num_scalar_prefetch=1,
            grid=(count // group,),
            in_specs=[
                pl.BlockSpec((group * rows, cols), lambda i, m: (i + first, 0)),
                pl.BlockSpec((rows, cols), lambda i, m: (0, 0)),
                pl.BlockSpec((rows, cols), lambda i, m: (0, 0)),
                pl.BlockSpec((group, rank), lambda i, m: (i + first, 0)),
            ],
            out_specs=[pl.BlockSpec((group, pixels + rank), lambda i, m: (i, 0))] * parts,
            scratch_shapes=[pltpu.VMEM((rows, cols), F32)] * 2 + [pltpu.VMEM((parts, group, pixels), BF16)],
        ),
        cost_estimate=pl.CostEstimate(
            flops=count * rows * cols * SWEEPS * 9,
            bytes_accessed=count * rows * cols * 6,
            transcendentals=0,
        ),
        name="charge_sharing",
    )(me[None].astype(jnp.int32), raw_frames.reshape(frames * rows, cols), gain_map, coupling, w_local)


TILE = 256


def ratio_tile(data_refs, w, h_refs, at, tile):
    h_tile = jnp.concatenate([ref[:, at : at + tile] for ref in h_refs], axis=0)
    product = jnp.dot(w, h_tile, preferred_element_type=F32)
    values = jnp.concatenate([ref[:, at : at + tile] for ref in data_refs], axis=0).astype(F32)
    return (values / product).astype(BF16), h_tile


def rows_of(data_refs, pixels):
    return jnp.concatenate([ref[:, pixels:] for ref in data_refs], axis=0)


def w_term_body(*refs):
    *data_refs, h_one, h_two, out_ref = refs
    pixels = h_one.shape[1]
    w = rows_of(data_refs, pixels)
    tile = min(TILE, pixels)
    total = None
    for at in range(0, pixels, tile):
        ratio, h_tile = ratio_tile(data_refs, w, (h_one, h_two), at, tile)
        term = lax.dot_general(ratio, h_tile, (((1,), (1,)), ((), ())), preferred_element_type=F32)
        total = term if total is None else total + term
    out_ref[...] = total


def tiles_body(*refs):
    *data_refs, out_ref = refs
    pixels = out_ref.shape[1]
    row = 0
    for ref in data_refs:
        out_ref[row : row + ref.shape[0], :] = ref[:, :pixels]
        row += ref.shape[0]


VMEM = pl.BlockSpec(memory_space=pltpu.VMEM)


def term(body, out_shape, args, flops):
    single = not isinstance(out_shape, list)
    return pl.pallas_call(
        body,
        out_shape=out_shape,
        in_specs=[VMEM] * len(args),
        out_specs=VMEM if single else [VMEM] * len(out_shape),
        cost_estimate=pl.CostEstimate(flops=flops, bytes_accessed=sum(a.size * 2 for a in args), transcendentals=0),
    )(*args)


def relative(blocks, index, bits):
    for bit in range(bits):
        flip = (index >> bit) & 1
        blocks = [jnp.where(flip == 1, blocks[j ^ (1 << bit)], blocks[j]) for j in range(len(blocks))]
    return blocks


def halves(value):
    high = value.astype(F16)
    return high, (value - high.astype(F32)).astype(F16)


def with_sums(block, sums):
    high, low = halves(sums)
    return jnp.concatenate([block.astype(F16), high[None], low[None], jnp.zeros((14, len(sums)), F16)], axis=0)


def chunks_of(frames):
    return [(0, frames - 16), (frames - 16, 16)] if frames > 16 else [(0, frames)]


def groups_of(n_pix):
    near = list(range(n_pix // 2))
    far = list(range(n_pix - 1, n_pix // 2 - 1, -1))
    return [near] + [far[i : i + 2] for i in range(0, len(far), 2)]


def local(raw_frames, gain_map, coupling, factor_w, factor_h, n_scan, n_pix):
    scan_bits = n_scan.bit_length() - 1
    scan = lax.axis_index("scan")
    me = lax.axis_index("pix")
    row_count, rank = factor_w.shape
    comp_rows, pixels = factor_h.shape
    half = rank // 2
    x_bits = [1 << b for b in range(1, scan_bits)]
    far = list(range(2, n_pix, 2))
    even = [0] + far
    odd = [r + 1 for r in even]
    scale = 1.0 / (pixels // 8)

    def over_pix(value, bit):
        return lax.ppermute(value, "pix", [(i, i ^ bit) for i in range(n_pix)])

    def over_scan(value, bit):
        return lax.ppermute(value, "scan", [(i, i ^ bit) for i in range(n_scan)])

    comp_order = [2 * j + c for c in range(2) for j in range(n_scan // 2)]

    def to_local(w):
        blocks = relative([w[:, comp_rows * j : comp_rows * (j + 1)] for j in range(n_scan)], scan, scan_bits)
        return jnp.concatenate([blocks[j] for j in comp_order], axis=1)

    def to_global(w):
        at = {j: w[:, comp_rows * i : comp_rows * (i + 1)] for i, j in enumerate(comp_order)}
        return jnp.concatenate(relative([at[j] for j in range(n_scan)], scan, scan_bits), axis=1)

    w_local = to_local(factor_w)

    tile = {r: [] for r in range(n_pix)}
    for start, count in chunks_of(raw_frames.shape[0]):
        messages = correct(raw_frames, gain_map, coupling, w_local, me, n_pix, start, count)
        for r in range(n_pix - 1, 0, -1):
            tile[r].append(over_pix(messages[r], r))
        tile[0].append(messages[0])

    h_own = factor_h
    for bit in x_bits:
        h_own = jnp.concatenate([h_own, over_scan(h_own, bit)], 0)

    def blocks(which):
        return [part for r in which for part in tile[r]]

    for rounds in range(ITERS):
        h_mine = h_own.astype(BF16)
        h_pair = [h_mine, over_scan(h_mine, 1)]
        h_part = jnp.concatenate([jnp.sum(h.astype(F32), axis=1) for h in h_pair])

        def numerator_of(values, w_round):
            h_block = jnp.concatenate(h_pair, axis=0)
            product = jnp.dot(w_round, h_block, preferred_element_type=F32)
            ratio = (values.astype(F32) / product).astype(BF16)
            return lax.dot_general(ratio, h_block, (((1,), (1,)), ((), ())), preferred_element_type=F32)

        if rounds == 0:
            backs = []
            for group in groups_of(n_pix):
                rows = row_count * len(group)
                out = jax.ShapeDtypeStruct((rows, rank), F32)
                partial = term(w_term_body, out, blocks(group) + h_pair, 4 * rows * rank * pixels) * scale
                for j, r in enumerate(group):
                    block = partial[row_count * j : row_count * (j + 1)]
                    if r == 0:
                        numerator = block
                    else:
                        backs.append(over_pix(with_sums(block, h_part * scale), r))
            everything = functools.reduce(lambda a, b: a + b, [b.astype(F32) for b in backs])
            numerator = numerator + everything[:row_count]
            h_sums = h_part * scale + everything[row_count] + everything[row_count + 1]
        else:
            rows = row_count * len(even)
            away = numerator_of(data_all[rows:], w_odd)
            back = over_pix(with_sums(away / h_part - 1.0, h_part), 1)
            near = numerator_of(data_all[:rows], w_even)
            weight = back[rows].astype(F32) + back[rows + 1].astype(F32)
            near = near + (back[:rows].astype(F32) + 1.0) * weight
            h_two = h_part + weight
            numerator, h_sums = near[:row_count], h_two
            for i, r in enumerate(far):
                mean = near[row_count * (i + 1) : row_count * (i + 2)] / h_two - 1.0
                back = over_pix(with_sums(mean, h_two), r)
                weight = back[row_count].astype(F32) + back[row_count + 1].astype(F32)
                numerator = numerator + (back[:row_count].astype(F32) + 1.0) * weight
                h_sums = h_sums + weight
        w_local = w_local * numerator / h_sums

        w_mine = w_local.astype(BF16)
        w_even = jnp.concatenate([w_mine] + [over_pix(w_mine, r) for r in far], axis=0)
        w_odd = over_pix(w_even, 1)
        if rounds == 0:
            shape = jax.ShapeDtypeStruct((row_count * n_pix, pixels), BF16)
            data_all = term(tiles_body, shape, blocks(even + odd), 0)
        w_all = jnp.concatenate([w_even, w_odd], axis=0)
        w_part = jnp.sum(w_all.astype(F32), axis=0)
        last = rounds == ITERS - 1
        w_sums = w_part[:half] + over_scan(w_part[half:], 1)
        product = jnp.dot(w_all, jnp.concatenate(h_pair, axis=0), preferred_element_type=F32)
        ratio = (data_all.astype(F32) / product).astype(BF16)

        def numerator_rows(w):
            return lax.dot_general(w, ratio, (((0,), (0,)), ((), ())), preferred_element_type=F32)

        other = over_scan(numerator_rows(w_all[:, half:]), 1)
        total = numerator_rows(w_all[:, :half]) + other
        for bit in x_bits[::-1]:
            count = total.shape[0] // comp_rows
            step = bit >> 1
            if last:
                keep = [i for i in range(count) if not i & step]
                send = [i | step for i in keep]
            else:
                keep = list(range(count))
                send = [i ^ step for i in keep]

            def pick(value, which):
                if list(which) == list(range(which[0], which[0] + len(which))):
                    return value[comp_rows * which[0] : comp_rows * (which[-1] + 1)]
                return jnp.concatenate([value[comp_rows * i : comp_rows * (i + 1)] for i in which], axis=0)

            sums = pick(w_sums, send)
            weight = over_scan(sums, bit)
            message = (pick(total, send) / sums[:, None] - 1.0).astype(F16)
            back = over_scan(message, bit).astype(F32) + 1.0
            total = pick(total, keep) + back * weight[:, None]
            w_sums = pick(w_sums, keep) + weight
        h_own = h_own[: total.shape[0]] * total / w_sums[:, None]
    return (to_global(w_local), h_own)


def solution(mesh):
    n_pix = mesh.shape["pix"]

    def layer(*args):
        return local(*args, n_scan=mesh.shape["scan"], n_pix=n_pix)

    return jax.shard_map(
        layer,
        mesh=mesh,
        in_specs=(
            P(("scan", "pix"), None, None),
            P(),
            P(),
            P(("scan", "pix"), None),
            P("scan", "pix"),
        ),
        out_specs=(P(("scan", "pix"), None), P("scan", "pix")),
        check_vma=False,
    )
```

profile of v0, /device:TPU:0, one launch (start us, length us, event | category | flops | bytes accessed | tf_op | source)
XLA Modules:
  0.0 188.8 jit_solution(9212032556162931245)
XLA Ops:
  0.6 3.0 %collective-permute-start.6 = (f32[64,2048]{1,0:T(8,128)}, f32[64,2048]{1,0:T(8,128)S(1)}, u32[]{:S(2)}, u32[]{:S(2)}) collective-permute-start(f32[64,2048]{1,0:T(8,128)} %param.9), channel_id=1, source_target_pairs={{0,16},{8,24},{16,0},{24,8},{1,17},{9,25},{17,1},{25,9},{2,18},{10... | collective-permute-start | bytes 1572872 | tf_op jit(solution)/shard_map/ppermute | solution.py:218
  4.8 11.0 %collective-permute-done.6 = f32[64,2048]{1,0:T(8,128)S(1)} collective-permute-done((f32[64,2048]{1,0:T(8,128)}, f32[64,2048]{1,0:T(8,128)S(1)}, u32[]{:S(2)}, u32[]{:S(2)}) %collective-permute-start.6) | collective-permute-done | bytes 524320 | tf_op jit(solution)/shard_map/ppermute | solution.py:218
  16.9 5.4 %charge_sharing.3 = (bf16[16,2304]{1,0:T(8,128)(2,1)}, bf16[16,2304]{1,0:T(8,128)(2,1)}, bf16[16,2304]{1,0:T(8,128)(2,1)}, bf16[16,2304]{1,0:T(8,128)(2,1)}, bf1...) custom-call(s32[1]{0:T(128)} %bitcast.me_ref, ...), custom_call_target="tpu_custom_call" | custom-call | flops 9437184 | bytes 1572864 | tf_op jit(solution)/shard_map/charge_sharing/pallas_call | solution.py:100
  22.3 1.8 collective-permute-start.1
  24.1 1.6 collective-permute-start.3
  25.7 8.8 %charge_sharing.2 = (bf16[32,2304]{1,0:T(8,128)(2,1)}, bf16[32,2304]{1,0:T(8,128)(2,1)}, bf16[32,2304]{1,0:T(8,128)(2,1)}, bf16[32,2304]{1,0:T(8,128)(2,1)}, bf1...) custom-call(s32[1]{0:T(128)} %bitcast.me_ref, ...), custom_call_target="tpu_custom_call" | custom-call | flops 18874368 | bytes 3145728 | tf_op jit(solution)/shard_map/charge_sharing/pallas_call | solution.py:100
  35.3 2.8 %collective-permute-start.4 = (bf16[32,2304]{1,0:T(8,128)(2,1)}, bf16[32,2304]{1,0:T(8,128)(2,1)S(1)}, u32[]{:S(2)}, u32[]{:S(2)}) collective-permute-start(bf16[32,2304]{1,0:T(8,128)(2,1)} %get-tuple-element.24), channel_id=1, source_target_pairs={{0,3},{1,2},{2,1},{3,0},{4,7},{5,6},{6,5},{7,4},{8,11},{9,10},{10,... | collective-permute-start | bytes 442376 | tf_op jit(solution)/shard_map/ppermute | solution.py:215
  38.3 8.1 %collective-permute-done.5.refs_7_.refs_11_ = bf16[16,2304]{1,0:T(8,128)(2,1)S(1)} collective-permute-done((bf16[16,2304]{1,0:T(8,128)(2,1)S(1)}, bf16[16,2304]{1,0:T(8,128)(2,1)S(1)}, u32[]{:S(2)}, u32[]{:S(2)}) %collective-permute-start.5) | collective-permute-done | bytes 73760 | tf_op jit(solution)/shard_map/ppermute | solution.py:215
  46.4 2.4 %collective-permute-start.11 = (bf16[32,2304]{1,0:T(8,128)(2,1)}, bf16[32,2304]{1,0:T(8,128)(2,1)S(1)}, u32[]{:S(2)}, u32[]{:S(2)}) collective-permute-start(bf16[32,2304]{1,0:T(8,128)(2,1)} %get-tuple-element.26), channel_id=1, source_target_pairs={{0,7},{1,6},{2,5},{3,4},{4,3},{5,2},{6,1},{7,0},{8,15},{9,14},{10,... | collective-permute-start | bytes 442376 | tf_op jit(solution)/shard_map/ppermute | solution.py:215
  49.2 3.5 %collective-permute-start.19 = (bf16[32,2304]{1,0:T(8,128)(2,1)}, bf16[32,2304]{1,0:T(8,128)(2,1)S(1)}, u32[]{:S(2)}, u32[]{:S(2)}) collective-permute-start(bf16[32,2304]{1,0:T(8,128)(2,1)} %get-tuple-element.32), channel_id=1, source_target_pairs={{0,4},{1,5},{2,6},{3,7},{4,0},{5,1},{6,2},{7,3},{8,12},{9,13},{10,... | collective-permute-start | bytes 442376 | tf_op jit(solution)/shard_map/ppermute | solution.py:215
  52.9 2.7 %collective-permute-start.20 = (bf16[16,2304]{1,0:T(8,128)(2,1)}, bf16[16,2304]{1,0:T(8,128)(2,1)S(1)}, u32[]{:S(2)}, u32[]{:S(2)}) collective-permute-start(bf16[16,2304]{1,0:T(8,128)(2,1)} %get-tuple-element.33), channel_id=1, source_target_pairs={{0,4},{1,5},{2,6},{3,7},{4,0},{5,1},{6,2},{7,3},{8,12},{9,13},{10,... | collective-permute-start | bytes 221192 | tf_op jit(solution)/shard_map/ppermute | solution.py:215
  55.6 3.1 %shard_map.68 = f32[192,256]{1,0:T(8,128)} custom-call(bf16[32,2304]{1,0:T(8,128)(2,1)} %get-tuple-element.18.refs_0_, bf16[16,2304]{1,0:T(8,128)(2,1)} %get-tuple-element.19.refs_1_, bf16[32,2304]{1,0:T(8,128)(2,1)} %copy-done.4, bf16[16,2304]{1,0:T(8,128)(2,1)} %copy-done.11, bf16[32,2304]{1,0:T(8,128)(2,1)} %copy-done.5, bf16[16,2304]{1,0:T(8,128)(2,1)} %copy-done.12, ...), custom_call_target="tpu_custom_call" | custom-call | flops 402653184 | bytes 1933312 | tf_op jit(solution)/shard_map/pallas_call | solution.py:165
  59.7 13.9 %collective-permute-done.18.refs_1_.refs_13_ = bf16[16,2304]{1,0:T(8,128)(2,1)S(1)} collective-permute-done((bf16[16,2304]{1,0:T(8,128)(2,1)}, bf16[16,2304]{1,0:T(8,128)(2,1)S(1)}, u32[]{:S(2)}, u32[]{:S(2)}) %collective-permute-start.18) | collective-permute-done | bytes 73760 | tf_op jit(solution)/shard_map/ppermute | solution.py:215
  73.6 3.4 %collective-permute-start.13 = (bf16[32,2304]{1,0:T(8,128)(2,1)S(1)}, bf16[32,2304]{1,0:T(8,128)(2,1)S(1)}, u32[]{:S(2)}, u32[]{:S(2)}) collective-permute-start(bf16[32,2304]{1,0:T(8,128)(2,1)S(1)} %copy-done.19), channel_id=1, source_target_pairs={{0,6},{1,7},{2,4},{3,5},{4,2},{5,3},{6,0},{7,1},{8,14},{9,15},{10,... | collective-permute-start | bytes 442376 | tf_op jit(solution)/shard_map/ppermute | solution.py:215
  76.9 1.6 collective-permute-start.12
  78.5 2.7 %collective-permute-start.14 = (bf16[16,2304]{1,0:T(8,128)(2,1)S(1)}, bf16[16,2304]{1,0:T(8,128)(2,1)S(1)}, u32[]{:S(2)}, u32[]{:S(2)}) collective-permute-start(bf16[16,2304]{1,0:T(8,128)(2,1)S(1)} %copy-done.20), channel_id=1, source_target_pairs={{0,6},{1,7},{2,4},{3,5},{4,2},{5,3},{6,0},{7,1},{8,14},{9,15},{10,... | collective-permute-start | bytes 221192 | tf_op jit(solution)/shard_map/ppermute | solution.py:215
  81.9 3.0 %shard_map.70 = f32[96,256]{1,0:T(8,128)} custom-call(bf16[32,2304]{1,0:T(8,128)(2,1)} %copy-done.8, bf16[16,2304]{1,0:T(8,128)(2,1)} %copy-done.14, bf16[32,2304]{1,0:T(8,128)(2,1)} %copy-done.9, bf16[16,2304]{1,0:T(8,128)(2,1)} %copy-done.15, bf16[128,2048]{1,0:T(8,128)(2,1)} %copy-done, bf16[128,2048]{1,0:T(8,128)(2,1)} %copy-done.2), custom_call_target="tpu_custom_call" | custom-call | flops 201326592 | bytes 1490944 | tf_op jit(solution)/shard_map/pallas_call | solution.py:165
  87.2 3.0 %shard_map.69 = f32[96,256]{1,0:T(8,128)} custom-call(bf16[32,2304]{1,0:T(8,128)(2,1)} %copy-done.7, bf16[16,2304]{1,0:T(8,128)(2,1)} %copy-done.16, bf16[32,2304]{1,0:T(8,128)(2,1)} %copy-done.10, bf16[16,2304]{1,0:T(8,128)(2,1)} %copy-done.17, bf16[128,2048]{1,0:T(8,128)(2,1)} %copy-done, bf16[128,2048]{1,0:T(8,128)(2,1)} %copy-done.2), custom_call_target="tpu_custom_call" | custom-call | flops 201326592 | bytes 1490944 | tf_op jit(solution)/shard_map/pallas_call | solution.py:165
  91.4 2.0 %collective-permute-start.10 = (f16[64,256]{1,0:T(8,128)(2,1)S(1)}, f16[64,256]{1,0:T(8,128)(2,1)S(1)}, u32[]{:S(2)}, u32[]{:S(2)}) collective-permute-start(f16[64,256]{1,0:T(8,128)(2,1)S(1)} %get-tuple-element.79), channel_id=1, source_target_pairs={{0,3},{1,2},{2,1},{3,0},{4,7},{5,6},{6,5},{7,4},{8,11},{9,10},{10,... | collective-permute-start | bytes 98312 | tf_op jit(solution)/shard_map/ppermute | solution.py:215
  93.4 3.2 %collective-permute-start.15 = (f16[64,256]{1,0:T(8,128)(2,1)S(1)}, f16[64,256]{1,0:T(8,128)(2,1)S(1)}, u32[]{:S(2)}, u32[]{:S(2)}) collective-permute-start(f16[64,256]{1,0:T(8,128)(2,1)S(1)} %get-tuple-element.80), channel_id=1, source_target_pairs={{0,7},{1,6},{2,5},{3,4},{4,3},{5,2},{6,1},{7,0},{8,15},{9,14},{10,... | collective-permute-start | bytes 98312 | tf_op jit(solution)/shard_map/ppermute | solution.py:215
  96.5 1.3 collective-permute-start.8
  98.8 2.8 %collective-permute-start.21 = (f16[64,256]{1,0:T(8,128)(2,1)S(1)}, f16[64,256]{1,0:T(8,128)(2,1)S(1)}, u32[]{:S(2)}, u32[]{:S(2)}) collective-permute-start(f16[64,256]{1,0:T(8,128)(2,1)S(1)} %get-tuple-element.82), channel_id=1, source_target_pairs={{0,5},{1,4},{2,7},{3,6},{4,1},{5,0},{6,3},{7,2},{8,13},{9,12},{10,... | collective-permute-start | bytes 98312 | tf_op jit(solution)/shard_map/ppermute | solution.py:215
  102.3 1.4 collective-permute-done.16
  103.7 1.2 collective-permute-done.21
  104.9 1.5 collective-permute-done.22
  107.6 1.4 collective-permute-start.24
  109.0 2.1 %collective-permute-start.25 = (bf16[48,256]{1,0:T(8,128)(2,1)S(1)}, bf16[48,256]{1,0:T(8,128)(2,1)S(1)}, u32[]{:S(2)}, u32[]{:S(2)}) collective-permute-start(bf16[48,256]{1,0:T(8,128)(2,1)S(1)} %get-tuple-element.48), channel_id=1, source_target_pairs={{0,6},{1,7},{2,4},{3,5},{4,2},{5,3},{6,0},{7,1},{8,14},{9,15},{10,... | collective-permute-start | bytes 73736 | tf_op jit(solution)/shard_map/ppermute | solution.py:215
  111.1 2.8 %shard_map.71 = bf16[384,2048]{1,0:T(8,128)(2,1)} custom-call(bf16[32,2304]{1,0:T(8,128)(2,1)} %get-tuple-element.18.refs_0_, bf16[16,2304]{1,0:T(8,128)(2,1)} %get-tuple-element.19.refs_1_, bf16[32,2304]{1,0:T(8,128)(2,1)} %copy-done.5, bf16[16,2304]{1,0:T(8,128)(2,1)} %copy-done.12, bf16[32,2304]{1,0:T(8,128)(2,1)} %copy-done.9, ...), custom_call_target="tpu_custom_call" | custom-call | bytes 1769472 | tf_op jit(solution)/shard_map/pallas_call | solution.py:165
  115.8 3.5 %collective-permute-done.26 = bf16[192,256]{1,0:T(8,128)(2,1)S(1)} collective-permute-done((bf16[192,256]{1,0:T(8,128)(2,1)S(1)}, bf16[192,256]{1,0:T(8,128)(2,1)S(1)}, u32[]{:S(2)}, u32[]{:S(2)}) %collective-permute-start.26) | collective-permute-done | bytes 98336 | tf_op jit(solution)/shard_map/ppermute | solution.py:215
  119.3 2.0 %fusion = bf16[384,2048]{1,0:T(8,128)(2,1)S(1)} fusion(bf16[384,2048]{1,0:T(8,128)(2,1)} %shard_map.71, bf16[384,256]{1,0:T(8,128)(2,1)S(1)} %constant_dynamic-update-slice_fusion.2, bf16[128,2048]{1,0:T(8,128)(2,1)S(1)} %copy-done.3, bf16[128,2048]{1,0:T(8,128)(2,1)S(1)} %copy-done.1), kind=kOutput, calls=%fused_computation.2 | convolution fusion | flops 407109632 | bytes 4390912 | tf_op jit(solution)/shard_map/dot_general | solution.py:299
  122.5 2.0 %collective-permute-done.28 = f32[128]{0:T(128)S(1)} collective-permute-done((f32[128]{0:T(128)S(1)}, f32[128]{0:T(128)S(1)}, u32[]{:S(2)}, u32[]{:S(2)}) %collective-permute-start.28) | collective-permute-done | bytes 544 | tf_op jit(solution)/shard_map/ppermute | solution.py:218
  125.5 1.6 collective-permute-start.29
  127.6 12.0 %collective-permute-done.30 = f32[128]{0:T(128)S(1)} collective-permute-done((f32[128]{0:T(128)S(1)}, f32[128]{0:T(128)S(1)}, u32[]{:S(2)}, u32[]{:S(2)}) %collective-permute-start.30) | collective-permute-done | bytes 544 | tf_op jit(solution)/shard_map/ppermute | solution.py:218
  140.1 1.9 %collective-permute-done.31 = bf16[128,2048]{1,0:T(8,128)(2,1)S(1)} collective-permute-done((bf16[128,2048]{1,0:T(8,128)(2,1)S(1)}, bf16[128,2048]{1,0:T(8,128)(2,1)S(1)}, u32[]{:S(2)}, u32[]{:S(2)}) %collective-permute-start.31) | collective-permute-done | bytes 524320 | tf_op jit(solution)/shard_map/ppermute | solution.py:218
  142.2 1.9 fusion.3
  145.3 3.9 %collective-permute-done.32 = f16[208,256]{1,0:T(8,128)(2,1)S(1)} collective-permute-done((f16[208,256]{1,0:T(8,128)(2,1)S(1)}, f16[208,256]{1,0:T(8,128)(2,1)S(1)}, u32[]{:S(2)}, u32[]{:S(2)}) %collective-permute-start.32) | collective-permute-done | bytes 106528 | tf_op jit(solution)/shard_map/ppermute | solution.py:215
  149.2 1.9 convolution_add_fusion.2
  151.3 2.6 %collective-permute-start.34 = (f16[64,256]{1,0:T(8,128)(2,1)S(1)}, f16[64,256]{1,0:T(8,128)(2,1)S(1)}, u32[]{:S(2)}, u32[]{:S(2)}) collective-permute-start(f16[64,256]{1,0:T(8,128)(2,1)S(1)} %get-tuple-element.76), channel_id=1, source_target_pairs={{0,4},{1,5},{2,6},{3,7},{4,0},{5,1},{6,2},{7,3},{8,12},{9,13},{10,... | collective-permute-start | bytes 98312 | tf_op jit(solution)/shard_map/ppermute | solution.py:215
  153.9 1.8 collective-permute-start.35
  156.1 3.4 %collective-permute-done.35 = f16[64,256]{1,0:T(8,128)(2,1)S(1)} collective-permute-done((f16[64,256]{1,0:T(8,128)(2,1)S(1)}, f16[64,256]{1,0:T(8,128)(2,1)S(1)}, u32[]{:S(2)}, u32[]{:S(2)}) %collective-permute-start.35) | collective-permute-done | bytes 32800 | tf_op jit(solution)/shard_map/ppermute | solution.py:215
  159.7 2.3 %collective-permute-start.37 = (bf16[48,256]{1,0:T(8,128)(2,1)S(1)}, bf16[48,256]{1,0:T(8,128)(2,1)S(1)}, u32[]{:S(2)}, u32[]{:S(2)}) collective-permute-start(bf16[48,256]{1,0:T(8,128)(2,1)S(1)} %get-tuple-element.35), channel_id=1, source_target_pairs={{0,4},{1,5},{2,6},{3,7},{4,0},{5,1},{6,2},{7,3},{8,12},{9,13},{10,... | collective-permute-start | bytes 73736 | tf_op jit(solution)/shard_map/ppermute | solution.py:215
  162.0 2.1 %collective-permute-start.38 = (bf16[48,256]{1,0:T(8,128)(2,1)S(1)}, bf16[48,256]{1,0:T(8,128)(2,1)S(1)}, u32[]{:S(2)}, u32[]{:S(2)}) collective-permute-start(bf16[48,256]{1,0:T(8,128)(2,1)S(1)} %get-tuple-element.35), channel_id=1, source_target_pairs={{0,6},{1,7},{2,4},{3,5},{4,2},{5,3},{6,0},{7,1},{8,14},{9,15},{10,... | collective-permute-start | bytes 73736 | tf_op jit(solution)/shard_map/ppermute | solution.py:215
  164.5 3.1 %collective-permute-done.38 = bf16[48,256]{1,0:T(8,128)(2,1)S(1)} collective-permute-done((bf16[48,256]{1,0:T(8,128)(2,1)S(1)}, bf16[48,256]{1,0:T(8,128)(2,1)S(1)}, u32[]{:S(2)}, u32[]{:S(2)}) %collective-permute-start.38) | collective-permute-done | bytes 24608 | tf_op jit(solution)/shard_map/ppermute | solution.py:215
  168.9 3.5 %collective-permute-done.39 = bf16[192,256]{1,0:T(8,128)(2,1)S(1)} collective-permute-done((bf16[192,256]{1,0:T(8,128)(2,1)S(1)}, bf16[192,256]{1,0:T(8,128)(2,1)S(1)}, u32[]{:S(2)}, u32[]{:S(2)}) %collective-permute-start.39) | collective-permute-done | bytes 98336 | tf_op jit(solution)/shard_map/ppermute | solution.py:215
  172.4 2.0 %fusion.1 = bf16[384,2048]{1,0:T(8,128)(2,1)S(1)} fusion(bf16[384,2048]{1,0:T(8,128)(2,1)} %shard_map.71, bf16[384,256]{1,0:T(8,128)(2,1)S(1)} %constant_dynamic-update-slice_fusion.7, bf16[128,2048]{1,0:T(8,128)(2,1)S(1)} %collective-permute-done.31, bf16[128,2048]{1,0:T(8,128)(2,1)S(1)} %get-tuple-element.45), kind=kOutput, calls=%fused_computation.3 | convolution fusion | flops 407109632 | bytes 4390912 | tf_op jit(solution)/shard_map/dot_general | solution.py:299
  175.6 1.9 %collective-permute-done.41 = f32[128]{0:T(128)S(1)} collective-permute-done((f32[128]{0:T(128)S(1)}, f32[128]{0:T(128)S(1)}, u32[]{:S(2)}, u32[]{:S(2)}) %collective-permute-start.41) | collective-permute-done | bytes 544 | tf_op jit(solution)/shard_map/ppermute | solution.py:218
  177.6 1.5 collective-permute-start.43
  181.2 6.7 %collective-permute-done.42 = f16[64,2048]{1,0:T(8,128)(2,1)S(1)} collective-permute-done((f16[64,2048]{1,0:T(8,128)(2,1)S(1)}, f16[64,2048]{1,0:T(8,128)(2,1)S(1)}, u32[]{:S(2)}, u32[]{:S(2)}) %collective-permute-start.42) | collective-permute-done | bytes 262176 | tf_op jit(solution)/shard_map/ppermute | solution.py:218
  (154 shorter events, 24.8 us)
Async XLA Ops:
  0.6 15.2 %collective-permute-start.6 = (f32[64,2048]{1,0:T(8,128)}, f32[64,2048]{1,0:T(8,128)S(1)}, u32[]{:S(2)}, u32[]{:S(2)}) collective-permute-start(f32[64,2048]{1,0:T(8,128)} %param.9), channel_id=1, source_target_pairs={{0,16},{8,24},{16,0},{24,8},{1,17},{9,25},{17,1},{25,9},{2,18},{10... | collective-permute-start | bytes 1572872 | tf_op jit(solution)/shard_map/ppermute | solution.py:218
  16.0 36.9 %collective-permute-start.7 = (bf16[128,2048]{1,0:T(8,128)(2,1)S(1)}, bf16[128,2048]{1,0:T(8,128)(2,1)S(1)}, u32[]{:S(2)}, u32[]{:S(2)}) collective-permute-start(bf16[128,2048]{1,0:T(8,128)(2,1)S(1)} %get-tuple-element.51.refs_8_.refs_4_), channel_id=1, source_target_pairs={{0,8},{8,0},{16,24},{24,16},{1,9},{9,1},{17,25},{25,17},{2,10},{10... | collective-permute-start | bytes 1572872 | tf_op jit(solution)/shard_map/ppermute | solution.py:218
  22.3 13.0 %collective-permute-start.1 = (bf16[16,2304]{1,0:T(8,128)(2,1)}, bf16[16,2304]{1,0:T(8,128)(2,1)S(1)}, u32[]{:S(2)}, u32[]{:S(2)}) collective-permute-start(bf16[16,2304]{1,0:T(8,128)(2,1)} %get-tuple-element.21), channel_id=1, source_target_pairs={{0,1},{1,0},{2,3},{3,2},{4,5},{5,4},{6,7},{7,6},{8,9},{9,8},{10,11... | collective-permute-start | bytes 221192 | tf_op jit(solution)/shard_map/ppermute | solution.py:215
  24.1 14.0 %collective-permute-start.3 = (bf16[16,2304]{1,0:T(8,128)(2,1)}, bf16[16,2304]{1,0:T(8,128)(2,1)S(1)}, u32[]{:S(2)}, u32[]{:S(2)}) collective-permute-start(bf16[16,2304]{1,0:T(8,128)(2,1)} %get-tuple-element.23), channel_id=1, source_target_pairs={{0,2},{1,3},{2,0},{3,1},{4,6},{5,7},{6,4},{7,5},{8,10},{9,11},{10,... | collective-permute-start | bytes 221192 | tf_op jit(solution)/shard_map/ppermute | solution.py:215
  34.5 44.0 %copy-start.20 = (bf16[16,2304]{1,0:T(8,128)(2,1)S(1)}, bf16[16,2304]{1,0:T(8,128)(2,1)}, u32[]{:S(2)}) copy-start(bf16[16,2304]{1,0:T(8,128)(2,1)} %get-tuple-element.29) | copy-start | bytes 221188
  34.5 14.3 %collective-permute-start = (bf16[32,2304]{1,0:T(8,128)(2,1)}, bf16[32,2304]{1,0:T(8,128)(2,1)S(1)}, u32[]{:S(2)}, u32[]{:S(2)}) collective-permute-start(bf16[32,2304]{1,0:T(8,128)(2,1)} %get-tuple-element.20), channel_id=1, source_target_pairs={{0,1},{1,0},{2,3},{3,2},{4,5},{5,4},{6,7},{7,6},{8,9},{9,8},{10,11... | collective-permute-start | bytes 442376 | tf_op jit(solution)/shard_map/ppermute | solution.py:215
  35.1 14.1 %collective-permute-start.2 = (bf16[32,2304]{1,0:T(8,128)(2,1)}, bf16[32,2304]{1,0:T(8,128)(2,1)S(1)}, u32[]{:S(2)}, u32[]{:S(2)}) collective-permute-start(bf16[32,2304]{1,0:T(8,128)(2,1)} %get-tuple-element.22), channel_id=1, source_target_pairs={{0,2},{1,3},{2,0},{3,1},{4,6},{5,7},{6,4},{7,5},{8,10},{9,11},{10,... | collective-permute-start | bytes 442376 | tf_op jit(solution)/shard_map/ppermute | solution.py:215
  35.3 20.3 %copy-start.11 = (bf16[16,2304]{1,0:T(8,128)(2,1)}, bf16[16,2304]{1,0:T(8,128)(2,1)S(1)}, u32[]{:S(2)}) copy-start(bf16[16,2304]{1,0:T(8,128)(2,1)S(1)} %collective-permute-done.1.refs_3_.refs_9_) | copy-start | bytes 221188
  35.3 17.4 %collective-permute-start.4 = (bf16[32,2304]{1,0:T(8,128)(2,1)}, bf16[32,2304]{1,0:T(8,128)(2,1)S(1)}, u32[]{:S(2)}, u32[]{:S(2)}) collective-permute-start(bf16[32,2304]{1,0:T(8,128)(2,1)} %get-tuple-element.24), channel_id=1, source_target_pairs={{0,3},{1,2},{2,1},{3,0},{4,7},{5,6},{6,5},{7,4},{8,11},{9,10},{10,... | collective-permute-start | bytes 442376 | tf_op jit(solution)/shard_map/ppermute | solution.py:215
  38.0 17.5 %copy-start.12 = (bf16[16,2304]{1,0:T(8,128)(2,1)}, bf16[16,2304]{1,0:T(8,128)(2,1)S(1)}, u32[]{:S(2)}) copy-start(bf16[16,2304]{1,0:T(8,128)(2,1)S(1)} %collective-permute-done.3.refs_5_.refs_3_) | copy-start | bytes 221188
  38.1 8.3 %collective-permute-start.5 = (bf16[16,2304]{1,0:T(8,128)(2,1)S(1)}, bf16[16,2304]{1,0:T(8,128)(2,1)S(1)}, u32[]{:S(2)}, u32[]{:S(2)}) collective-permute-start(bf16[16,2304]{1,0:T(8,128)(2,1)S(1)} %copy-done.21), channel_id=1, source_target_pairs={{0,3},{1,2},{2,1},{3,0},{4,7},{5,6},{6,5},{7,4},{8,11},{9,10},{10,... | collective-permute-start | bytes 221192 | tf_op jit(solution)/shard_map/ppermute | solution.py:215
  46.4 39.5 %collective-permute-start.11 = (bf16[32,2304]{1,0:T(8,128)(2,1)}, bf16[32,2304]{1,0:T(8,128)(2,1)S(1)}, u32[]{:S(2)}, u32[]{:S(2)}) collective-permute-start(bf16[32,2304]{1,0:T(8,128)(2,1)} %get-tuple-element.26), channel_id=1, source_target_pairs={{0,7},{1,6},{2,5},{3,4},{4,3},{5,2},{6,1},{7,0},{8,15},{9,14},{10,... | collective-permute-start | bytes 442376 | tf_op jit(solution)/shard_map/ppermute | solution.py:215
  48.8 29.7 %collective-permute-start.17 = (bf16[32,2304]{1,0:T(8,128)(2,1)}, bf16[32,2304]{1,0:T(8,128)(2,1)S(1)}, u32[]{:S(2)}, u32[]{:S(2)}) collective-permute-start(bf16[32,2304]{1,0:T(8,128)(2,1)} %get-tuple-element.30), channel_id=1, source_target_pairs={{0,5},{1,4},{2,7},{3,6},{4,1},{5,0},{6,3},{7,2},{8,13},{9,12},{10,... | collective-permute-start | bytes 442376 | tf_op jit(solution)/shard_map/ppermute | solution.py:215
  49.2 32.0 %collective-permute-start.19 = (bf16[32,2304]{1,0:T(8,128)(2,1)}, bf16[32,2304]{1,0:T(8,128)(2,1)S(1)}, u32[]{:S(2)}, u32[]{:S(2)}) collective-permute-start(bf16[32,2304]{1,0:T(8,128)(2,1)} %get-tuple-element.32), channel_id=1, source_target_pairs={{0,4},{1,5},{2,6},{3,7},{4,0},{5,1},{6,2},{7,3},{8,12},{9,13},{10,... | collective-permute-start | bytes 442376 | tf_op jit(solution)/shard_map/ppermute | solution.py:215
  52.7 20.9 %collective-permute-start.18 = (bf16[16,2304]{1,0:T(8,128)(2,1)}, bf16[16,2304]{1,0:T(8,128)(2,1)S(1)}, u32[]{:S(2)}, u32[]{:S(2)}) collective-permute-start(bf16[16,2304]{1,0:T(8,128)(2,1)} %get-tuple-element.31), channel_id=1, source_target_pairs={{0,5},{1,4},{2,7},{3,6},{4,1},{5,0},{6,3},{7,2},{8,13},{9,12},{10,... | collective-permute-start | bytes 221192 | tf_op jit(solution)/shard_map/ppermute | solution.py:215
  52.9 20.7 %copy-start.19 = (bf16[32,2304]{1,0:T(8,128)(2,1)S(1)}, bf16[32,2304]{1,0:T(8,128)(2,1)}, u32[]{:S(2)}) copy-start(bf16[32,2304]{1,0:T(8,128)(2,1)} %get-tuple-element.28) | copy-start | bytes 442372
  52.9 24.1 %collective-permute-start.20 = (bf16[16,2304]{1,0:T(8,128)(2,1)}, bf16[16,2304]{1,0:T(8,128)(2,1)S(1)}, u32[]{:S(2)}, u32[]{:S(2)}) collective-permute-start(bf16[16,2304]{1,0:T(8,128)(2,1)} %get-tuple-element.33), channel_id=1, source_target_pairs={{0,4},{1,5},{2,6},{3,7},{4,0},{5,1},{6,2},{7,3},{8,12},{9,13},{10,... | collective-permute-start | bytes 221192 | tf_op jit(solution)/shard_map/ppermute | solution.py:215
  73.6 12.3 %collective-permute-start.13 = (bf16[32,2304]{1,0:T(8,128)(2,1)S(1)}, bf16[32,2304]{1,0:T(8,128)(2,1)S(1)}, u32[]{:S(2)}, u32[]{:S(2)}) collective-permute-start(bf16[32,2304]{1,0:T(8,128)(2,1)S(1)} %copy-done.19), channel_id=1, source_target_pairs={{0,6},{1,7},{2,4},{3,5},{4,2},{5,3},{6,0},{7,1},{8,14},{9,15},{10,... | collective-permute-start | bytes 442376 | tf_op jit(solution)/shard_map/ppermute | solution.py:215
  76.9 8.9 %collective-permute-start.12 = (bf16[16,2304]{1,0:T(8,128)(2,1)}, bf16[16,2304]{1,0:T(8,128)(2,1)S(1)}, u32[]{:S(2)}, u32[]{:S(2)}) collective-permute-start(bf16[16,2304]{1,0:T(8,128)(2,1)} %get-tuple-element.27), channel_id=1, source_target_pairs={{0,7},{1,6},{2,5},{3,4},{4,3},{5,2},{6,1},{7,0},{8,15},{9,14},{10,... | collective-permute-start | bytes 221192 | tf_op jit(solution)/shard_map/ppermute | solution.py:215
  78.5 7.3 %collective-permute-start.14 = (bf16[16,2304]{1,0:T(8,128)(2,1)S(1)}, bf16[16,2304]{1,0:T(8,128)(2,1)S(1)}, u32[]{:S(2)}, u32[]{:S(2)}) collective-permute-start(bf16[16,2304]{1,0:T(8,128)(2,1)S(1)} %copy-done.20), channel_id=1, source_target_pairs={{0,6},{1,7},{2,4},{3,5},{4,2},{5,3},{6,0},{7,1},{8,14},{9,15},{10,... | collective-permute-start | bytes 221192 | tf_op jit(solution)/shard_map/ppermute | solution.py:215
  91.4 7.4 %collective-permute-start.10 = (f16[64,256]{1,0:T(8,128)(2,1)S(1)}, f16[64,256]{1,0:T(8,128)(2,1)S(1)}, u32[]{:S(2)}, u32[]{:S(2)}) collective-permute-start(f16[64,256]{1,0:T(8,128)(2,1)S(1)} %get-tuple-element.79), channel_id=1, source_target_pairs={{0,3},{1,2},{2,1},{3,0},{4,7},{5,6},{6,5},{7,4},{8,11},{9,10},{10,... | collective-permute-start | bytes 98312 | tf_op jit(solution)/shard_map/ppermute | solution.py:215
  93.4 8.2 %collective-permute-start.15 = (f16[64,256]{1,0:T(8,128)(2,1)S(1)}, f16[64,256]{1,0:T(8,128)(2,1)S(1)}, u32[]{:S(2)}, u32[]{:S(2)}) collective-permute-start(f16[64,256]{1,0:T(8,128)(2,1)S(1)} %get-tuple-element.80), channel_id=1, source_target_pairs={{0,7},{1,6},{2,5},{3,4},{4,3},{5,2},{6,1},{7,0},{8,15},{9,14},{10,... | collective-permute-start | bytes 98312 | tf_op jit(solution)/shard_map/ppermute | solution.py:215
  96.5 5.7 %collective-permute-start.8 = (f16[64,256]{1,0:T(8,128)(2,1)S(1)}, f16[64,256]{1,0:T(8,128)(2,1)S(1)}, u32[]{:S(2)}, u32[]{:S(2)}) collective-permute-start(f16[64,256]{1,0:T(8,128)(2,1)S(1)} %get-tuple-element.77), channel_id=1, source_target_pairs={{0,1},{1,0},{2,3},{3,2},{4,5},{5,4},{6,7},{7,6},{8,9},{9,8},{10,11... | collective-permute-start | bytes 98312 | tf_op jit(solution)/shard_map/ppermute | solution.py:215
  97.9 4.4 %collective-permute-start.9 = (f16[64,256]{1,0:T(8,128)(2,1)S(1)}, f16[64,256]{1,0:T(8,128)(2,1)S(1)}, u32[]{:S(2)}, u32[]{:S(2)}) collective-permute-start(f16[64,256]{1,0:T(8,128)(2,1)S(1)} %get-tuple-element.78), channel_id=1, source_target_pairs={{0,2},{1,3},{2,0},{3,1},{4,6},{5,7},{6,4},{7,5},{8,10},{9,11},{10,... | collective-permute-start | bytes 98312 | tf_op jit(solution)/shard_map/ppermute | solution.py:215
  97.9 5.8 %collective-permute-start.16 = (f16[64,256]{1,0:T(8,128)(2,1)S(1)}, f16[64,256]{1,0:T(8,128)(2,1)S(1)}, u32[]{:S(2)}, u32[]{:S(2)}) collective-permute-start(f16[64,256]{1,0:T(8,128)(2,1)S(1)} %get-tuple-element.81), channel_id=1, source_target_pairs={{0,6},{1,7},{2,4},{3,5},{4,2},{5,3},{6,0},{7,1},{8,14},{9,15},{10,... | collective-permute-start | bytes 98312 | tf_op jit(solution)/shard_map/ppermute | solution.py:215
  98.8 6.1 %collective-permute-start.21 = (f16[64,256]{1,0:T(8,128)(2,1)S(1)}, f16[64,256]{1,0:T(8,128)(2,1)S(1)}, u32[]{:S(2)}, u32[]{:S(2)}) collective-permute-start(f16[64,256]{1,0:T(8,128)(2,1)S(1)} %get-tuple-element.82), channel_id=1, source_target_pairs={{0,5},{1,4},{2,7},{3,6},{4,1},{5,0},{6,3},{7,2},{8,13},{9,12},{10,... | collective-permute-start | bytes 98312 | tf_op jit(solution)/shard_map/ppermute | solution.py:215
  101.6 4.8 %collective-permute-start.22 = (f16[64,256]{1,0:T(8,128)(2,1)S(1)}, f16[64,256]{1,0:T(8,128)(2,1)S(1)}, u32[]{:S(2)}, u32[]{:S(2)}) collective-permute-start(f16[64,256]{1,0:T(8,128)(2,1)S(1)} %get-tuple-element.83), channel_id=1, source_target_pairs={{0,4},{1,5},{2,6},{3,7},{4,0},{5,1},{6,2},{7,3},{8,12},{9,13},{10,... | collective-permute-start | bytes 98312 | tf_op jit(solution)/shard_map/ppermute | solution.py:215
  106.6 7.3 %collective-permute-start.23 = (bf16[48,256]{1,0:T(8,128)(2,1)S(1)}, bf16[48,256]{1,0:T(8,128)(2,1)S(1)}, u32[]{:S(2)}, u32[]{:S(2)}) collective-permute-start(bf16[48,256]{1,0:T(8,128)(2,1)S(1)} %get-tuple-element.48), channel_id=1, source_target_pairs={{0,2},{1,3},{2,0},{3,1},{4,6},{5,7},{6,4},{7,5},{8,10},{9,11},{10,... | collective-permute-start | bytes 73736 | tf_op jit(solution)/shard_map/ppermute | solution.py:215
  107.6 6.3 %collective-permute-start.24 = (bf16[48,256]{1,0:T(8,128)(2,1)S(1)}, bf16[48,256]{1,0:T(8,128)(2,1)S(1)}, u32[]{:S(2)}, u32[]{:S(2)}) collective-permute-start(bf16[48,256]{1,0:T(8,128)(2,1)S(1)} %get-tuple-element.48), channel_id=1, source_target_pairs={{0,4},{1,5},{2,6},{3,7},{4,0},{5,1},{6,2},{7,3},{8,12},{9,13},{10,... | collective-permute-start | bytes 73736 | tf_op jit(solution)/shard_map/ppermute | solution.py:215
  109.0 5.6 %collective-permute-start.25 = (bf16[48,256]{1,0:T(8,128)(2,1)S(1)}, bf16[48,256]{1,0:T(8,128)(2,1)S(1)}, u32[]{:S(2)}, u32[]{:S(2)}) collective-permute-start(bf16[48,256]{1,0:T(8,128)(2,1)S(1)} %get-tuple-element.48), channel_id=1, source_target_pairs={{0,6},{1,7},{2,4},{3,5},{4,2},{5,3},{6,0},{7,1},{8,14},{9,15},{10,... | collective-permute-start | bytes 73736 | tf_op jit(solution)/shard_map/ppermute | solution.py:215
  114.6 4.7 %collective-permute-start.26 = (bf16[192,256]{1,0:T(8,128)(2,1)S(1)}, bf16[192,256]{1,0:T(8,128)(2,1)S(1)}, u32[]{:S(2)}, u32[]{:S(2)}) collective-permute-start(bf16[192,256]{1,0:T(8,128)(2,1)S(1)} %pad_maximum_fusion.26), channel_id=1, source_target_pairs={{0,1},{1,0},{2,3},{3,2},{4,5},{5,4},{6,7},{7,6},{8,9},{9,8},{10,11... | collective-permute-start | bytes 294920 | tf_op jit(solution)/shard_map/ppermute | solution.py:215
  121.8 2.9 %collective-permute-start.27 = (f32[128,2048]{1,0:T(8,128)S(1)}, f32[128,2048]{1,0:T(8,128)S(1)}, u32[]{:S(2)}, u32[]{:S(2)}) collective-permute-start(f32[128,2048]{1,0:T(8,128)S(1)} %fusion.16), channel_id=1, source_target_pairs={{0,8},{8,0},{16,24},{24,16},{1,9},{9,1},{17,25},{25,17},{2,10},{10... | collective-permute-start | bytes 3145736 | tf_op jit(solution)/shard_map/ppermute | solution.py:218
  122.0 2.6 %collective-permute-start.28 = (f32[128]{0:T(128)S(1)}, f32[128]{0:T(128)S(1)}, u32[]{:S(2)}, u32[]{:S(2)}) collective-permute-start(f32[128]{0:T(128)S(1)} %slice.190), channel_id=1, source_target_pairs={{0,8},{8,0},{16,24},{24,16},{1,9},{9,1},{17,25},{25,17},{2,10},{10... | collective-permute-start | bytes 1544 | tf_op jit(solution)/shard_map/ppermute | solution.py:218
  125.5 14.1 %collective-permute-start.29 = (f16[128,2048]{1,0:T(8,128)(2,1)S(1)}, f16[128,2048]{1,0:T(8,128)(2,1)S(1)}, u32[]{:S(2)}, u32[]{:S(2)}) collective-permute-start(f16[128,2048]{1,0:T(8,128)(2,1)S(1)} %fusion.8), channel_id=1, source_target_pairs={{0,16},{8,24},{16,0},{24,8},{1,17},{9,25},{17,1},{25,9},{2,18},{10... | collective-permute-start | bytes 1572872 | tf_op jit(solution)/shard_map/ppermute | solution.py:218
  127.1 12.6 %collective-permute-start.30 = (f32[128]{0:T(128)S(1)}, f32[128]{0:T(128)S(1)}, u32[]{:S(2)}, u32[]{:S(2)}) collective-permute-start(f32[128]{0:T(128)S(1)} %pad_maximum_fusion.38), channel_id=1, source_target_pairs={{0,16},{8,24},{16,0},{24,8},{1,17},{9,25},{17,1},{25,9},{2,18},{10... | collective-permute-start | bytes 1544 | tf_op jit(solution)/shard_map/ppermute | solution.py:218
  140.1 2.0 %collective-permute-start.31 = (bf16[128,2048]{1,0:T(8,128)(2,1)S(1)}, bf16[128,2048]{1,0:T(8,128)(2,1)S(1)}, u32[]{:S(2)}, u32[]{:S(2)}) collective-permute-start(bf16[128,2048]{1,0:T(8,128)(2,1)S(1)} %get-tuple-element.45), channel_id=1, source_target_pairs={{0,8},{8,0},{16,24},{24,16},{1,9},{9,1},{17,25},{25,17},{2,10},{10... | collective-permute-start | bytes 1572872 | tf_op jit(solution)/shard_map/ppermute | solution.py:218
  144.1 5.1 %collective-permute-start.32 = (f16[208,256]{1,0:T(8,128)(2,1)S(1)}, f16[208,256]{1,0:T(8,128)(2,1)S(1)}, u32[]{:S(2)}, u32[]{:S(2)}) collective-permute-start(f16[208,256]{1,0:T(8,128)(2,1)S(1)} %pad_maximum_fusion.11), channel_id=1, source_target_pairs={{0,1},{1,0},{2,3},{3,2},{4,5},{5,4},{6,7},{7,6},{8,9},{9,8},{10,11... | collective-permute-start | bytes 319496 | tf_op jit(solution)/shard_map/ppermute | solution.py:215
  151.2 4.5 %collective-permute-start.33 = (f16[64,256]{1,0:T(8,128)(2,1)S(1)}, f16[64,256]{1,0:T(8,128)(2,1)S(1)}, u32[]{:S(2)}, u32[]{:S(2)}) collective-permute-start(f16[64,256]{1,0:T(8,128)(2,1)S(1)} %get-tuple-element.75), channel_id=1, source_target_pairs={{0,2},{1,3},{2,0},{3,1},{4,6},{5,7},{6,4},{7,5},{8,10},{9,11},{10,... | collective-permute-start | bytes 98312 | tf_op jit(solution)/shard_map/ppermute | solution.py:215
  151.3 4.9 %collective-permute-start.34 = (f16[64,256]{1,0:T(8,128)(2,1)S(1)}, f16[64,256]{1,0:T(8,128)(2,1)S(1)}, u32[]{:S(2)}, u32[]{:S(2)}) collective-permute-start(f16[64,256]{1,0:T(8,128)(2,1)S(1)} %get-tuple-element.76), channel_id=1, source_target_pairs={{0,4},{1,5},{2,6},{3,7},{4,0},{5,1},{6,2},{7,3},{8,12},{9,13},{10,... | collective-permute-start | bytes 98312 | tf_op jit(solution)/shard_map/ppermute | solution.py:215
  153.9 5.7 %collective-permute-start.35 = (f16[64,256]{1,0:T(8,128)(2,1)S(1)}, f16[64,256]{1,0:T(8,128)(2,1)S(1)}, u32[]{:S(2)}, u32[]{:S(2)}) collective-permute-start(f16[64,256]{1,0:T(8,128)(2,1)S(1)} %get-tuple-element.74), channel_id=1, source_target_pairs={{0,6},{1,7},{2,4},{3,5},{4,2},{5,3},{6,0},{7,1},{8,14},{9,15},{10,... | collective-permute-start | bytes 98312 | tf_op jit(solution)/shard_map/ppermute | solution.py:215
  159.6 4.5 %collective-permute-start.36 = (bf16[48,256]{1,0:T(8,128)(2,1)S(1)}, bf16[48,256]{1,0:T(8,128)(2,1)S(1)}, u32[]{:S(2)}, u32[]{:S(2)}) collective-permute-start(bf16[48,256]{1,0:T(8,128)(2,1)S(1)} %get-tuple-element.35), channel_id=1, source_target_pairs={{0,2},{1,3},{2,0},{3,1},{4,6},{5,7},{6,4},{7,5},{8,10},{9,11},{10,... | collective-permute-start | bytes 73736 | tf_op jit(solution)/shard_map/ppermute | solution.py:215
  159.7 4.8 %collective-permute-start.37 = (bf16[48,256]{1,0:T(8,128)(2,1)S(1)}, bf16[48,256]{1,0:T(8,128)(2,1)S(1)}, u32[]{:S(2)}, u32[]{:S(2)}) collective-permute-start(bf16[48,256]{1,0:T(8,128)(2,1)S(1)} %get-tuple-element.35), channel_id=1, source_target_pairs={{0,4},{1,5},{2,6},{3,7},{4,0},{5,1},{6,2},{7,3},{8,12},{9,13},{10,... | collective-permute-start | bytes 73736 | tf_op jit(solution)/shard_map/ppermute | solution.py:215
  162.0 5.6 %collective-permute-start.38 = (bf16[48,256]{1,0:T(8,128)(2,1)S(1)}, bf16[48,256]{1,0:T(8,128)(2,1)S(1)}, u32[]{:S(2)}, u32[]{:S(2)}) collective-permute-start(bf16[48,256]{1,0:T(8,128)(2,1)S(1)} %get-tuple-element.35), channel_id=1, source_target_pairs={{0,6},{1,7},{2,4},{3,5},{4,2},{5,3},{6,0},{7,1},{8,14},{9,15},{10,... | collective-permute-start | bytes 73736 | tf_op jit(solution)/shard_map/ppermute | solution.py:215
  167.7 4.7 %collective-permute-start.39 = (bf16[192,256]{1,0:T(8,128)(2,1)S(1)}, bf16[192,256]{1,0:T(8,128)(2,1)S(1)}, u32[]{:S(2)}, u32[]{:S(2)}) collective-permute-start(bf16[192,256]{1,0:T(8,128)(2,1)S(1)} %pad_maximum_fusion.27), channel_id=1, source_target_pairs={{0,1},{1,0},{2,3},{3,2},{4,5},{5,4},{6,7},{7,6},{8,9},{9,8},{10,11... | collective-permute-start | bytes 294920 | tf_op jit(solution)/shard_map/ppermute | solution.py:215
  174.8 4.3 %collective-permute-start.40 = (f32[128,2048]{1,0:T(8,128)S(1)}, f32[128,2048]{1,0:T(8,128)S(1)}, u32[]{:S(2)}, u32[]{:S(2)}) collective-permute-start(f32[128,2048]{1,0:T(8,128)S(1)} %fusion.13), channel_id=1, source_target_pairs={{0,8},{8,0},{16,24},{24,16},{1,9},{9,1},{17,25},{25,17},{2,10},{10... | collective-permute-start | bytes 3145736 | tf_op jit(solution)/shard_map/ppermute | solution.py:218
  175.0 2.6 %collective-permute-start.41 = (f32[128]{0:T(128)S(1)}, f32[128]{0:T(128)S(1)}, u32[]{:S(2)}, u32[]{:S(2)}) collective-permute-start(f32[128]{0:T(128)S(1)} %slice.220), channel_id=1, source_target_pairs={{0,8},{8,0},{16,24},{24,16},{1,9},{9,1},{17,25},{25,17},{2,10},{10... | collective-permute-start | bytes 1544 | tf_op jit(solution)/shard_map/ppermute | solution.py:218
  177.6 3.6 %collective-permute-start.43 = (f32[64]{0:T(128)S(1)}, f32[64]{0:T(128)S(1)}, u32[]{:S(2)}, u32[]{:S(2)}) collective-permute-start(f32[64]{0:T(128)S(1)} %slice.221), channel_id=1, source_target_pairs={{0,16},{8,24},{16,0},{24,8},{1,17},{9,25},{17,1},{25,9},{2,18},{10... | collective-permute-start | bytes 776 | tf_op jit(solution)/shard_map/ppermute | solution.py:218
  179.8 8.1 %collective-permute-start.42 = (f16[64,2048]{1,0:T(8,128)(2,1)S(1)}, f16[64,2048]{1,0:T(8,128)(2,1)S(1)}, u32[]{:S(2)}, u32[]{:S(2)}) collective-permute-start(f16[64,2048]{1,0:T(8,128)(2,1)S(1)} %fusion.10), channel_id=1, source_target_pairs={{0,16},{8,24},{16,0},{24,8},{1,17},{9,25},{17,1},{25,9},{2,18},{10... | collective-permute-start | bytes 786440 | tf_op jit(solution)/shard_map/ppermute | solution.py:218
  (18 other events, 102.8 us)
where the time goes:
time: 189 us
  waiting for transfers between devices  81 us (43%)
  starting transfers between devices  60.3 us (32%)
  Pallas kernels  26.1 us (14%)
  matrix products  9.58 us (5%)
  other arithmetic  7.21 us (4%)
  local copies, waits for them, and re-layouts  3.5 us (2%)
    ppermute x33, starting transfers between devices, over_pix(): return lax.ppermute(value, 'pix', [(i, i ^ bit) for i in range(n_pix)])  51.7 us
    ppermute x33, waiting for transfers between devices, over_pix(): return lax.ppermute(value, 'pix', [(i, i ^ bit) for i in range(n_pix)])  45.3 us
    ppermute x11, waiting for transfers between devices, over_scan(): return lax.ppermute(value, 'scan', [(i, i ^ bit) for i in range(n_scan)])  35.7 us
    pallas_call x2, Pallas kernels, correct(): pl.pallas_call(stencil_body, out_shape=[jax.ShapeDtypeStruct((count, pixe...  14.2 us
    pallas_call x4, Pallas kernels, term(): pl.pallas_call(body, out_shape=out_shape, in_specs=[VMEM] * len(args), ou...  11.9 us
    ppermute x11, starting transfers between devices, over_scan(): return lax.ppermute(value, 'scan', [(i, i ^ bit) for i in range(n_scan)])  8.61 us
    dot_general x2, matrix products, local(): jnp.dot(w_all, jnp.concatenate(h_pair, axis=0), preferred_element_type=F32)  3.98 us
  transfers between devices with their start and end apart: 44, of which 20 were waited for; matrix products, arithmetic and copies ran while one was open for 3% of the time, Pallas kernels for 12%

commit v1 on v0

--- a/solution.py
+++ b/solution.py
@@ -12,8 +12,21 @@
 BF16, F16, F32 = jnp.bfloat16, jnp.float16, jnp.float32
 
 
-def stencil_body(me_ref, raw_ref, gain_ref, couple_ref, w_ref, *refs):
-    out_refs, (gain_s, near_s, stage) = refs[:-3], refs[-3:]
+def relative(blocks, index):
+    for bit in range(len(blocks).bit_length() - 1):
+        flip = (index >> bit) & 1
+        blocks = [jnp.where(flip == 1, blocks[j ^ (1 << bit)], blocks[j]) for j in range(len(blocks))]
+    return blocks
+
+
+def reordered(w, index, order):
+    width = w.shape[1] // len(order)
+    blocks = relative([w[:, width * j : width * (j + 1)] for j in range(len(order))], index)
+    return jnp.concatenate([blocks[j] for j in order], axis=1)
+
+
+def stencil_body(me_ref, raw_ref, gain_ref, couple_ref, *refs, start, order, near):
+    refs, (gain_s, near_s, stage) = refs[:-3], refs[-3:]
     rows, cols = gain_ref.shape
     parts, frames, pixels = stage.shape
     groups = frames // 8
@@ -61,7 +74,7 @@
         scaled = [[s_new[g]] + scaled[g][: SWEEPS - 1] for g in range(groups)]
         return (new_levels, scaled, [w_new] + weight[: SWEEPS - 1]), out
 
-    frame = lax.broadcasted_iota(jnp.int32, (frames, cols), 0) + frames * pl.program_id(0)
+    frame = lax.broadcasted_iota(jnp.int32, (frames, cols), 0) + frames * pl.program_id(0) + start
     phase = frame.astype(F32) * 0.6180340 + lax.broadcasted_iota(jnp.int32, (frames, cols), 1).astype(F32) * 0.7548777
     shift = (phase - jnp.floor(phase) - 0.5) * 0.005
 
@@ -85,21 +98,46 @@
     carry = one_band(0, state, None, first=True)
     carry = lax.fori_loop(1, parts - 1, lambda part, c: one_band(part, *c), carry)
     one_band(parts - 1, *carry, last=True)
-    w_mine = w_ref[...].astype(BF16)
+
+    def mine(r):
+        return stage[jnp.bitwise_xor(me_ref[0], r)]
+
+    if near is None:
+        for r, out_ref in enumerate(refs):
+            out_ref[...] = mine(r)
+        return
+    early, w_ref, out_refs = refs[:near], refs[near], refs[near + 1 :]
+    w_mine = reordered(w_ref[...], me_ref[1], order).astype(BF16)
+    rank = w_mine.shape[1]
     for r, out_ref in enumerate(out_refs):
-        out_ref[:, :pixels] = stage[jnp.bitwise_xor(me_ref[0], r)]
-        out_ref[:, pixels:] = w_mine
-
-
-def correct(raw_frames, gain_map, coupling, w_local, me, parts, start, count):
+        if r < near:
+            before = early[r].shape[0]
+            out_ref[:before, :pixels] = early[r][...]
+            out_ref[before:, :pixels] = mine(r)
+            out_ref[:, pixels:] = w_mine
+        else:
+            out_ref[:, :pixels] = mine(r)
+            for i in range(w_mine.shape[0] // frames):
+                out_ref[:, pixels + rank * i : pixels + rank * (i + 1)] = w_mine[frames * i : frames * (i + 1)]
+
+
+def correct(raw_frames, gain_map, coupling, at, parts, start, count, early=None, factor_w=None, order=None):
     frames, rows, cols = raw_frames.shape
-    rank = w_local.shape[1]
     group = 16
     pixels = rows * cols // parts
     first = start // group
+    if early is None:
+        extra, near = [], None
+        shapes = [(count, pixels)] * parts
+        out_specs = [pl.BlockSpec((group, pixels), lambda i, m: (i, 0))] * parts
+    else:
+        rank = factor_w.shape[1]
+        extra, near = [*early, factor_w], len(early)
+        shapes = [(frames, pixels + rank)] * near + [(group, pixels + rank * (frames // group))] * (parts - near)
+        out_specs = [pl.BlockSpec(shape, lambda i, m: (0, 0)) for shape in shapes]
     return pl.pallas_call(
-        stencil_body,
-        out_shape=[jax.ShapeDtypeStruct((count, pixels + rank), BF16)] * parts,
+        functools.partial(stencil_body, start=start, order=order, near=near),
+        out_shape=[jax.ShapeDtypeStruct(shape, BF16) for shape in shapes],
         grid_spec=pltpu.PrefetchScalarGridSpec(
             num_scalar_prefetch=1,
             grid=(count // group,),
@@ -107,9 +145,9 @@
                 pl.BlockSpec((group * rows, cols), lambda i, m: (i + first, 0)),
                 pl.BlockSpec((rows, cols), lambda i, m: (0, 0)),
                 pl.BlockSpec((rows, cols), lambda i, m: (0, 0)),
-                pl.BlockSpec((group, rank), lambda i, m: (i + first, 0)),
-            ],
-            out_specs=[pl.BlockSpec((group, pixels + rank), lambda i, m: (i, 0))] * parts,
+            ]
+            + [pl.BlockSpec(x.shape, lambda i, m: (0, 0)) for x in extra],
+            out_specs=out_specs,
             scratch_shapes=[pltpu.VMEM((rows, cols), F32)] * 2 + [pltpu.VMEM((parts, group, pixels), BF16)],
         ),
         cost_estimate=pl.CostEstimate(
@@ -118,10 +156,11 @@
             transcendentals=0,
         ),
         name="charge_sharing",
-    )(me[None].astype(jnp.int32), raw_frames.reshape(frames * rows, cols), gain_map, coupling, w_local)
+    )(at, raw_frames.reshape(frames * rows, cols), gain_map, coupling, *extra)
 
 
 TILE = 256
+PARTS = 2
 
 
 def ratio_tile(data_refs, w, h_refs, at, tile):
@@ -131,18 +170,17 @@
     return (values / product).astype(BF16), h_tile
 
 
-def rows_of(data_refs, pixels):
-    return jnp.concatenate([ref[:, pixels:] for ref in data_refs], axis=0)
-
-
 def w_term_body(*refs):
     *data_refs, h_one, h_two, out_ref = refs
     pixels = h_one.shape[1]
-    w = rows_of(data_refs, pixels)
+    rank = out_ref.shape[1]
+    w = jnp.concatenate([ref[:, at : at + rank] for ref in data_refs for at in range(pixels, ref.shape[1], rank)], axis=0)
     tile = min(TILE, pixels)
+    ones = jnp.ones((16, tile), BF16)
     total = None
     for at in range(0, pixels, tile):
         ratio, h_tile = ratio_tile(data_refs, w, (h_one, h_two), at, tile)
+        ratio = jnp.concatenate([ratio, ones], axis=0)
         term = lax.dot_general(ratio, h_tile, (((1,), (1,)), ((), ())), preferred_element_type=F32)
         total = term if total is None else total + term
     out_ref[...] = total
@@ -160,22 +198,15 @@
 VMEM = pl.BlockSpec(memory_space=pltpu.VMEM)
 
 
-def term(body, out_shape, args, flops):
-    single = not isinstance(out_shape, list)
+def term(body, shape, dtype, args, flops):
     return pl.pallas_call(
         body,
-        out_shape=out_shape,
+        out_shape=pltpu.VMEM(shape, dtype),
         in_specs=[VMEM] * len(args),
-        out_specs=VMEM if single else [VMEM] * len(out_shape),
+        out_specs=VMEM,
         cost_estimate=pl.CostEstimate(flops=flops, bytes_accessed=sum(a.size * 2 for a in args), transcendentals=0),
-    )(*args)
-
-
-def relative(blocks, index, bits):
-    for bit in range(bits):
-        flip = (index >> bit) & 1
-        blocks = [jnp.where(flip == 1, blocks[j ^ (1 << bit)], blocks[j]) for j in range(len(blocks))]
-    return blocks
+        compiler_params=pltpu.CompilerParams(vmem_limit_bytes=8 << 20),
+    )(*[pltpu.with_memory_space_constraint(a, pltpu.VMEM) for a in args])
 
 
 def halves(value):
@@ -188,14 +219,8 @@
     return jnp.concatenate([block.astype(F16), high[None], low[None], jnp.zeros((14, len(sums)), F16)], axis=0)
 
 
-def chunks_of(frames):
-    return [(0, frames - 16), (frames - 16, 16)] if frames > 16 else [(0, frames)]
-
-
 def groups_of(n_pix):
-    near = list(range(n_pix // 2))
-    far = list(range(n_pix - 1, n_pix // 2 - 1, -1))
-    return [near] + [far[i : i + 2] for i in range(0, len(far), 2)]
+    return [list(range(n_pix // 2)), list(range(n_pix - 1, n_pix // 2 - 1, -1))]
 
 
 def local(raw_frames, gain_map, coupling, factor_w, factor_h, n_scan, n_pix):
@@ -218,62 +243,79 @@
         return lax.ppermute(value, "scan", [(i, i ^ bit) for i in range(n_scan)])
 
     comp_order = [2 * j + c for c in range(2) for j in range(n_scan // 2)]
-
-    def to_local(w):
-        blocks = relative([w[:, comp_rows * j : comp_rows * (j + 1)] for j in range(n_scan)], scan, scan_bits)
-        return jnp.concatenate([blocks[j] for j in comp_order], axis=1)
+    back_order = [comp_order.index(j) for j in range(n_scan)]
 
     def to_global(w):
-        at = {j: w[:, comp_rows * i : comp_rows * (i + 1)] for i, j in enumerate(comp_order)}
-        return jnp.concatenate(relative([at[j] for j in range(n_scan)], scan, scan_bits), axis=1)
-
-    w_local = to_local(factor_w)
-
+        at = [w[:, comp_rows * i : comp_rows * (i + 1)] for i in back_order]
+        return jnp.concatenate(relative(at, scan), axis=1)
+
+    w_local = reordered(factor_w, scan, comp_order)
+
+    close = n_pix // 2
+    frames = raw_frames.shape[0]
     tile = {r: [] for r in range(n_pix)}
-    for start, count in chunks_of(raw_frames.shape[0]):
-        messages = correct(raw_frames, gain_map, coupling, w_local, me, n_pix, start, count)
-        for r in range(n_pix - 1, 0, -1):
-            tile[r].append(over_pix(messages[r], r))
-        tile[0].append(messages[0])
-
-    h_own = factor_h
+    at = jnp.stack([me, scan]).astype(jnp.int32)
+    early = correct(raw_frames, gain_map, coupling, at, n_pix, 0, frames - 16)
+    late = correct(raw_frames, gain_map, coupling, at, n_pix, frames - 16, 16, early[:close], factor_w, comp_order)
+    for c, messages in enumerate([early, late]):
+        for r in range(1, n_pix):
+            if c or r >= close:
+                tile[r].append(over_pix(messages[r], r))
+    tile[0].append(late[0])
+
     for bit in x_bits:
-        h_own = jnp.concatenate([h_own, over_scan(h_own, bit)], 0)
+        factor_h = jnp.concatenate([factor_h, over_scan(factor_h, bit)], 0)
+    width = pixels // PARTS
+    parts = [slice(width * c, width * (c + 1)) for c in range(PARTS)]
+    h_mine = factor_h.astype(BF16)
+    h_other = over_scan(h_mine, 1)
+    h_own = [factor_h[:, part] for part in parts]
+    h_pairs = [[h_mine[:, part], h_other[:, part]] for part in parts]
 
     def blocks(which):
         return [part for r in which for part in tile[r]]
 
     for rounds in range(ITERS):
-        h_mine = h_own.astype(BF16)
-        h_pair = [h_mine, over_scan(h_mine, 1)]
-        h_part = jnp.concatenate([jnp.sum(h.astype(F32), axis=1) for h in h_pair])
+        if rounds:
+            h_part = sum(jnp.concatenate([jnp.sum(h.astype(F32), axis=1) for h in pair]) for pair in h_pairs)
+
+        def ratio_of(values, w_round, pair):
+            product = jnp.dot(w_round, jnp.concatenate(pair, axis=0), preferred_element_type=F32)
+            return (values.astype(F32) / product).astype(BF16)
 
         def numerator_of(values, w_round):
-            h_block = jnp.concatenate(h_pair, axis=0)
-            product = jnp.dot(w_round, h_block, preferred_element_type=F32)
-            ratio = (values.astype(F32) / product).astype(BF16)
-            return lax.dot_general(ratio, h_block, (((1,), (1,)), ((), ())), preferred_element_type=F32)
+            terms = []
+            for part, pair in zip(parts, h_pairs):
+                ratio = ratio_of(values[:, part], w_round, pair)
+                h_block = jnp.concatenate(pair, axis=0)
+                terms.append(lax.dot_general(ratio, h_block, (((1,), (1,)), ((), ())), preferred_element_type=F32))
+            return sum(terms)
 
         if rounds == 0:
-            backs = []
+            backs, h_here = [], [h_mine, h_other]
             for group in groups_of(n_pix):
                 rows = row_count * len(group)
-                out = jax.ShapeDtypeStruct((rows, rank), F32)
-                partial = term(w_term_body, out, blocks(group) + h_pair, 4 * rows * rank * pixels) * scale
+                shape = (rows + 16, rank)
+                partial = term(w_term_body, shape, F32, blocks(group) + h_here, 4 * rows * rank * pixels) * scale
+                h_sums = partial[rows]
+                messages = {}
                 for j, r in enumerate(group):
                     block = partial[row_count * j : row_count * (j + 1)]
                     if r == 0:
                         numerator = block
                     else:
-                        backs.append(over_pix(with_sums(block, h_part * scale), r))
+                        messages[r] = with_sums(block, h_sums)
+                h_here, messages = lax.optimization_barrier((h_here, messages))
+                for r, message in messages.items():
+                    backs.append(over_pix(message, r))
             everything = functools.reduce(lambda a, b: a + b, [b.astype(F32) for b in backs])
             numerator = numerator + everything[:row_count]
-            h_sums = h_part * scale + everything[row_count] + everything[row_count + 1]
+            h_sums = h_sums + everything[row_count] + everything[row_count + 1]
         else:
             rows = row_count * len(even)
-            away = numerator_of(data_all[rows:], w_odd)
+            away = numerator_of(data_odd, w_odd)
             back = over_pix(with_sums(away / h_part - 1.0, h_part), 1)
-            near = numerator_of(data_all[:rows], w_even)
+            near = lax.optimization_barrier(numerator_of(data_even, w_even))
             weight = back[rows].astype(F32) + back[rows + 1].astype(F32)
             near = near + (back[:rows].astype(F32) + 1.0) * weight
             h_two = h_part + weight
@@ -290,22 +332,27 @@
         w_even = jnp.concatenate([w_mine] + [over_pix(w_mine, r) for r in far], axis=0)
         w_odd = over_pix(w_even, 1)
         if rounds == 0:
-            shape = jax.ShapeDtypeStruct((row_count * n_pix, pixels), BF16)
-            data_all = term(tiles_body, shape, blocks(even + odd), 0)
-        w_all = jnp.concatenate([w_even, w_odd], axis=0)
-        w_part = jnp.sum(w_all.astype(F32), axis=0)
+            shape = (row_count * len(even), pixels)
+            data_even = term(tiles_body, shape, BF16, blocks(even), 0)
+            data_odd = term(tiles_body, shape, BF16, blocks(odd), 0)
+
+        def numerator_rows(w, ratio):
+            return lax.dot_general(w, ratio, (((0,), (0,)), ((), ())), preferred_element_type=F32)
+
         last = rounds == ITERS - 1
+        w_part = jnp.sum(w_even.astype(F32), axis=0) + jnp.sum(w_odd.astype(F32), axis=0)
         w_sums = w_part[:half] + over_scan(w_part[half:], 1)
-        product = jnp.dot(w_all, jnp.concatenate(h_pair, axis=0), preferred_element_type=F32)
-        ratio = (data_all.astype(F32) / product).astype(BF16)
-
-        def numerator_rows(w):
-            return lax.dot_general(w, ratio, (((0,), (0,)), ((), ())), preferred_element_type=F32)
-
-        other = over_scan(numerator_rows(w_all[:, half:]), 1)
-        total = numerator_rows(w_all[:, :half]) + other
+        evens = []
+        for part, pair in zip(parts, h_pairs):
+            ratio = ratio_of(data_even[:, part], w_even, pair)
+            evens.append([numerator_rows(w, ratio) for w in (w_even[:, :half], w_even[:, half:])])
+        totals = []
+        for c, (part, pair) in enumerate(zip(parts, h_pairs)):
+            ratio = ratio_of(data_odd[:, part], w_odd, pair)
+            other = over_scan(evens[c][1] + numerator_rows(w_odd[:, half:], ratio), 1)
+            totals.append(evens[c][0] + numerator_rows(w_odd[:, :half], ratio) + other)
         for bit in x_bits[::-1]:
-            count = total.shape[0] // comp_rows
+            count = totals[0].shape[0] // comp_rows
             step = bit >> 1
             if last:
                 keep = [i for i in range(count) if not i & step]
@@ -321,12 +368,17 @@
 
             sums = pick(w_sums, send)
             weight = over_scan(sums, bit)
-            message = (pick(total, send) / sums[:, None] - 1.0).astype(F16)
-            back = over_scan(message, bit).astype(F32) + 1.0
-            total = pick(total, keep) + back * weight[:, None]
+            for c in range(PARTS):
+                message = (pick(totals[c], send) / sums[:, None] - 1.0).astype(F16)
+                back = over_scan(message, bit).astype(F32) + 1.0
+                totals[c] = pick(totals[c], keep) + back * weight[:, None]
             w_sums = pick(w_sums, keep) + weight
-        h_own = h_own[: total.shape[0]] * total / w_sums[:, None]
-    return (to_global(w_local), h_own)
+        for c in range(PARTS):
+            h_own[c] = h_own[c][: totals[c].shape[0]] * totals[c] / w_sums[:, None]
+            if not last:
+                h_mine = h_own[c].astype(BF16)
+                h_pairs[c] = [h_mine, over_scan(h_mine, 1)]
+    return (to_global(w_local), jnp.concatenate(h_own, axis=1))
 
 
 def solution(mesh):

time: 189 us -> 184 us (0.974)
  waiting for transfers between devices: 81 us -> 62.4 us
  starting transfers between devices: 60.3 us -> 74.4 us
  Pallas kernels: 26.1 us -> 18.1 us
  matrix products: 9.58 us -> 14.9 us
    ppermute x33 -> x30, waiting for transfers between devices: 45.3 us -> 32.3 us  [over_pix(): return lax.ppermute(value, 'pix', [(i, i ^ bit) for i in range(n_pix)])]
    ppermute x33 -> x30, starting transfers between devices: 51.7 us -> 62.2 us  [over_pix(): return lax.ppermute(value, 'pix', [(i, i ^ bit) for i in range(n_pix)])]
    pallas_call x6, Pallas kernels: 26.1 us -> 18.1 us  [the longest x2 16.3 us: correct(): pl.pallas_call(functools.partial(stencil_body, start=start, order=order,...]
    ppermute x11 -> x16, waiting for transfers between devices: 35.7 us -> 30.2 us  [over_scan(): return lax.ppermute(value, 'scan', [(i, i ^ bit) for i in range(n_scan)])]
    dot_general x2 -> x4, matrix products: 3.71 us -> 8.71 us  [numerator_of(): lax.dot_general(ratio, h_block, (((1,), (1,)), ((), ())), preferred_eleme...]
    ppermute x11 -> x16, starting transfers between devices: 8.61 us -> 12.3 us  [over_scan(): return lax.ppermute(value, 'scan', [(i, i ^ bit) for i in range(n_scan)])]
    dot_general x4 -> x16, matrix products: 1.89 us -> 3.95 us  [numerator_rows(): lax.dot_general(w, ratio, (((0,), (0,)), ((), ())), preferred_element_typ...]
    dot_general x2 -> x8, matrix products: 3.98 us -> 2.22 us  [ratio_of(): jnp.dot(w_round, jnp.concatenate(pair, axis=0), preferred_element_type=F32)]
  transfers between devices with their start and end apart: 44 -> 46, of which waited for: 20 -> 21; matrix products, arithmetic and copies ran while one was open for 3% -> 7% of each run, Pallas kernels for 12% -> 9%
where the time goes in v1:
time: 184 us
  starting transfers between devices  74.4 us (40%)
  waiting for transfers between devices  62.4 us (34%)
  Pallas kernels  18.1 us (10%)
  matrix products  14.9 us (8%)
  other arithmetic  9.03 us (5%)
  local copies, waits for them, and re-layouts  3.5 us (2%)
    ppermute x30, starting transfers between devices, over_pix(): return lax.ppermute(value, 'pix', [(i, i ^ bit) for i in range(n_pix)])  62.2 us
    ppermute x30, waiting for transfers between devices, over_pix(): return lax.ppermute(value, 'pix', [(i, i ^ bit) for i in range(n_pix)])  32.3 us
    ppermute x16, waiting for transfers between devices, over_scan(): return lax.ppermute(value, 'scan', [(i, i ^ bit) for i in range(n_scan)])  30.2 us
    pallas_call x2, Pallas kernels, correct(): pl.pallas_call(functools.partial(stencil_body, start=start, order=order,...  16.3 us
    ppermute x16, starting transfers between devices, over_scan(): return lax.ppermute(value, 'scan', [(i, i ^ bit) for i in range(n_scan)])  12.3 us
    dot_general x4, matrix products, numerator_of(): lax.dot_general(ratio, h_block, (((1,), (1,)), ((), ())), preferred_eleme...  8.71 us
    dot_general x16, matrix products, numerator_rows(): lax.dot_general(w, ratio, (((0,), (0,)), ((), ())), preferred_element_typ...  3.95 us
  transfers between devices with their start and end apart: 46, of which 21 were waited for; matrix products, arithmetic and copies ran while one was open for 7% of the time, Pallas kernels for 9%

profile of v1, /device:TPU:0, one launch (start us, length us, event | category | flops | bytes accessed | tf_op | source)
XLA Modules:
  0.0 183.7 jit_solution(8787175136715606520)
XLA Ops:
  0.6 3.0 %collective-permute-start.3 = (f32[64,2048]{1,0:T(8,128)}, f32[64,2048]{1,0:T(8,128)S(1)}, u32[]{:S(2)}, u32[]{:S(2)}) collective-permute-start(f32[64,2048]{1,0:T(8,128)} %param.9), channel_id=1, source_target_pairs={{0,16},{8,24},{16,0},{24,8},{1,17},{9,25},{17,1},{25,9},{2,18},{10... | collective-permute-start | bytes 1572872 | tf_op jit(solution)/shard_map/ppermute | solution.py:243
  3.7 1.1 constant_dynamic-update-slice_fusion.1
  4.8 11.0 %collective-permute-done.3 = f32[64,2048]{1,0:T(8,128)S(1)} collective-permute-done((f32[64,2048]{1,0:T(8,128)}, f32[64,2048]{1,0:T(8,128)S(1)}, u32[]{:S(2)}, u32[]{:S(2)}) %collective-permute-start.3) | collective-permute-done | bytes 524320 | tf_op jit(solution)/shard_map/ppermute | solution.py:243
  17.6 9.5 %charge_sharing.2 = (bf16[32,2048]{1,0:T(8,128)(2,1)}, bf16[32,2048]{1,0:T(8,128)(2,1)}, bf16[32,2048]{1,0:T(8,128)(2,1)}, bf16[32,2048]{1,0:T(8,128)(2,1)}, bf1...) custom-call(s32[2]{0:T(128)} %pad_add_fusion.me_ref, ...), custom_call_target="tpu_custom_call" | custom-call | flops 18874368 | bytes 3145728 | tf_op jit(solution)/shard_map/charge_sharing/pallas_call | solution.py:138
  27.1 6.8 %charge_sharing.3 = (bf16[48,2304]{1,0:T(8,128)(2,1)}, bf16[48,2304]{1,0:T(8,128)(2,1)}, bf16[48,2304]{1,0:T(8,128)(2,1)}, bf16[48,2304]{1,0:T(8,128)(2,1)}, bf1...) custom-call(s32[2]{0:T(128)} %pad_add_fusion.me_ref, ...), custom_call_target="tpu_custom_call" | custom-call | flops 9437184 | bytes 1572864 | tf_op jit(solution)/shard_map/charge_sharing/pallas_call | solution.py:138
  33.9 1.8 collective-permute-start
  35.7 1.6 collective-permute-start.1
  37.4 4.8 %collective-permute-start.8 = (bf16[32,2048]{1,0:T(8,128)(2,1)S(1)}, bf16[32,2048]{1,0:T(8,128)(2,1)S(1)}, u32[]{:S(2)}, u32[]{:S(2)}) collective-permute-start(bf16[32,2048]{1,0:T(8,128)(2,1)S(1)} %copy-done.12), channel_id=1, source_target_pairs={{0,7},{1,6},{2,5},{3,4},{4,3},{5,2},{6,1},{7,0},{8,15},{9,14},{10,... | collective-permute-start | bytes 393224 | tf_op jit(solution)/shard_map/ppermute | solution.py:240
  42.2 4.5 %collective-permute-start.9 = (bf16[16,2816]{1,0:T(8,128)(2,1)}, bf16[16,2816]{1,0:T(8,128)(2,1)S(1)}, u32[]{:S(2)}, u32[]{:S(2)}) collective-permute-start(bf16[16,2816]{1,0:T(8,128)(2,1)} %get-tuple-element.41), channel_id=1, source_target_pairs={{0,7},{1,6},{2,5},{3,4},{4,3},{5,2},{6,1},{7,0},{8,15},{9,14},{10,... | collective-permute-start | bytes 270344 | tf_op jit(solution)/shard_map/ppermute | solution.py:240
  48.4 4.0 %collective-permute-start.11 = (bf16[16,2816]{1,0:T(8,128)(2,1)}, bf16[16,2816]{1,0:T(8,128)(2,1)S(1)}, u32[]{:S(2)}, u32[]{:S(2)}) collective-permute-start(bf16[16,2816]{1,0:T(8,128)(2,1)} %get-tuple-element.43), channel_id=1, source_target_pairs={{0,6},{1,7},{2,4},{3,5},{4,2},{5,3},{6,0},{7,1},{8,14},{9,15},{10,... | collective-permute-start | bytes 270344 | tf_op jit(solution)/shard_map/ppermute | solution.py:240
  52.5 3.3 %collective-permute-start.12 = (bf16[32,2048]{1,0:T(8,128)(2,1)S(1)}, bf16[32,2048]{1,0:T(8,128)(2,1)S(1)}, u32[]{:S(2)}, u32[]{:S(2)}) collective-permute-start(bf16[32,2048]{1,0:T(8,128)(2,1)S(1)} %copy-done.10), channel_id=1, source_target_pairs={{0,5},{1,4},{2,7},{3,6},{4,1},{5,0},{6,3},{7,2},{8,13},{9,12},{10,... | collective-permute-start | bytes 393224 | tf_op jit(solution)/shard_map/ppermute | solution.py:240
  57.6 8.5 %collective-permute-start.13 = (bf16[16,2816]{1,0:T(8,128)(2,1)}, bf16[16,2816]{1,0:T(8,128)(2,1)S(1)}, u32[]{:S(2)}, u32[]{:S(2)}) collective-permute-start(bf16[16,2816]{1,0:T(8,128)(2,1)} %get-tuple-element.45), channel_id=1, source_target_pairs={{0,5},{1,4},{2,7},{3,6},{4,1},{5,0},{6,3},{7,2},{8,13},{9,12},{10,... | collective-permute-start | bytes 270344 | tf_op jit(solution)/shard_map/ppermute | solution.py:240
  66.2 5.8 %collective-permute-start.14 = (bf16[32,2048]{1,0:T(8,128)(2,1)S(1)}, bf16[32,2048]{1,0:T(8,128)(2,1)S(1)}, u32[]{:S(2)}, u32[]{:S(2)}) collective-permute-start(bf16[32,2048]{1,0:T(8,128)(2,1)S(1)} %copy-done.9), channel_id=1, source_target_pairs={{0,4},{1,5},{2,6},{3,7},{4,0},{5,1},{6,2},{7,3},{8,12},{9,13},{10,... | collective-permute-start | bytes 393224 | tf_op jit(solution)/shard_map/ppermute | solution.py:240
  71.9 7.0 %collective-permute-done.13.refs_5_.refs_3_ = bf16[16,2816]{1,0:T(8,128)(2,1)S(1)} collective-permute-done((bf16[16,2816]{1,0:T(8,128)(2,1)}, bf16[16,2816]{1,0:T(8,128)(2,1)S(1)}, u32[]{:S(2)}, u32[]{:S(2)}) %collective-permute-start.13) | collective-permute-done | bytes 90144 | tf_op jit(solution)/shard_map/ppermute | solution.py:240
  79.0 6.6 %collective-permute-done.15.refs_7_.refs_3_ = bf16[16,2816]{1,0:T(8,128)(2,1)S(1)} collective-permute-done((bf16[16,2816]{1,0:T(8,128)(2,1)}, bf16[16,2816]{1,0:T(8,128)(2,1)S(1)}, u32[]{:S(2)}, u32[]{:S(2)}) %collective-permute-start.15) | collective-permute-done | bytes 90144 | tf_op jit(solution)/shard_map/ppermute | solution.py:240
  86.6 3.1 %collective-permute-start.19 = (f16[64,256]{1,0:T(8,128)(2,1)S(1)}, f16[64,256]{1,0:T(8,128)(2,1)S(1)}, u32[]{:S(2)}, u32[]{:S(2)}) collective-permute-start(f16[64,256]{1,0:T(8,128)(2,1)S(1)} %get-tuple-element.51), channel_id=1, source_target_pairs={{0,7},{1,6},{2,5},{3,4},{4,3},{5,2},{6,1},{7,0},{8,15},{9,14},{10,... | collective-permute-start | bytes 98312 | tf_op jit(solution)/shard_map/ppermute | solution.py:240
  89.7 1.3 collective-permute-start.18
  91.3 3.3 %collective-permute-start.16 = (f16[64,256]{1,0:T(8,128)(2,1)S(1)}, f16[64,256]{1,0:T(8,128)(2,1)S(1)}, u32[]{:S(2)}, u32[]{:S(2)}) collective-permute-start(f16[64,256]{1,0:T(8,128)(2,1)S(1)} %get-tuple-element.48), channel_id=1, source_target_pairs={{0,4},{1,5},{2,6},{3,7},{4,0},{5,1},{6,2},{7,3},{8,12},{9,13},{10,... | collective-permute-start | bytes 98312 | tf_op jit(solution)/shard_map/ppermute | solution.py:240
  95.3 1.9 %collective-permute-start.6 = (f16[64,256]{1,0:T(8,128)(2,1)S(1)}, f16[64,256]{1,0:T(8,128)(2,1)S(1)}, u32[]{:S(2)}, u32[]{:S(2)}) collective-permute-start(f16[64,256]{1,0:T(8,128)(2,1)S(1)} %get-tuple-element.36), channel_id=1, source_target_pairs={{0,2},{1,3},{2,0},{3,1},{4,6},{5,7},{6,4},{7,5},{8,10},{9,11},{10,... | collective-permute-start | bytes 98312 | tf_op jit(solution)/shard_map/ppermute | solution.py:240
  98.2 1.3 collective-permute-done.7
  99.4 1.6 collective-permute-done.5
  101.9 2.5 %collective-permute-start.22 = (bf16[48,256]{1,0:T(8,128)(2,1)S(1)}, bf16[48,256]{1,0:T(8,128)(2,1)S(1)}, u32[]{:S(2)}, u32[]{:S(2)}) collective-permute-start(bf16[48,256]{1,0:T(8,128)(2,1)S(1)} %get-tuple-element.73), channel_id=1, source_target_pairs={{0,6},{1,7},{2,4},{3,5},{4,2},{5,3},{6,0},{7,1},{8,14},{9,15},{10,... | collective-permute-start | bytes 73736 | tf_op jit(solution)/shard_map/ppermute | solution.py:240
  104.3 1.9 %collective-permute-start.20 = (bf16[48,256]{1,0:T(8,128)(2,1)S(1)}, bf16[48,256]{1,0:T(8,128)(2,1)S(1)}, u32[]{:S(2)}, u32[]{:S(2)}) collective-permute-start(bf16[48,256]{1,0:T(8,128)(2,1)S(1)} %get-tuple-element.73), channel_id=1, source_target_pairs={{0,2},{1,3},{2,0},{3,1},{4,6},{5,7},{6,4},{7,5},{8,10},{9,11},{10,... | collective-permute-start | bytes 73736 | tf_op jit(solution)/shard_map/ppermute | solution.py:240
  106.3 1.2 collective-permute-done.22
  107.5 1.6 collective-permute-done.21
  110.3 3.5 %collective-permute-done.23 = bf16[192,256]{1,0:T(8,128)(2,1)S(1)} collective-permute-done((bf16[192,256]{1,0:T(8,128)(2,1)S(1)}, bf16[192,256]{1,0:T(8,128)(2,1)S(1)}, u32[]{:S(2)}, u32[]{:S(2)}) %collective-permute-start.23) | collective-permute-done | bytes 98336 | tf_op jit(solution)/shard_map/ppermute | solution.py:240
  118.6 1.6 collective-permute-start.26
  120.7 1.5 collective-permute-start.27
  122.1 10.5 %collective-permute-done.27 = f32[128]{0:T(128)S(1)} collective-permute-done((f32[128]{0:T(128)S(1)}, f32[128]{0:T(128)S(1)}, u32[]{:S(2)}, u32[]{:S(2)}) %collective-permute-start.27) | collective-permute-done | bytes 544 | tf_op jit(solution)/shard_map/ppermute | solution.py:243
  135.3 2.2 %fusion.16 = f32[192,256]{1,0:T(8,128)} fusion(bf16[192,256]{1,0:T(8,128)(2,1)S(1)} %collective-permute-done.23, bf16[192,2048]{1,0:T(8,128)(2,1)S(1)} %shard_map.71, bf16[128,1024]{1,0:T(8,128)(2,1)S(1)} %collective-permute-done.31, bf16[128,1024]{1,0:T(8,128)(2,1)} %copy-done.5), kind=kOutput, calls=%fused_computation.36 | convolution fusion | flops 204013568 | bytes 1736704 | tf_op jit(solution)/shard_map/dot_general | solution.py:291
  137.5 2.2 %fusion.28 = f16[192,256]{1,0:T(8,128)(2,1)} fusion(f32[192,256]{1,0:T(8,128)} %fusion.16, bf16[192,256]{1,0:T(8,128)(2,1)S(1)} %collective-permute-done.23, bf16[192,2048]{1,0:T(8,128)(2,1)S(1)} %shard_map.71, f32[256]{0:T(256)S(1)} %maximum_add_fusion, bf16[128,1024]{1,0:T(8,128)(2,1)S(1)} %collective-permute-done.28, bf16[128,1024]{1,0:T(8,128)(2,1)} %copy-done.7), kind=kOutput, calls=%fused_computation.48 | convolution fusion | flops 204210176 | bytes 1836032 | tf_op jit(solution)/shard_map/dot_general | solution.py:291
  139.7 1.6 pad_maximum_fusion.19
  141.8 2.2 %fusion.18 = f32[192,256]{1,0:T(8,128)} fusion(bf16[192,256]{1,0:T(8,128)(2,1)S(1)} %get-tuple-element.72, bf16[192,2048]{1,0:T(8,128)(2,1)S(1)} %shard_map.70, bf16[128,1024]{1,0:T(8,128)(2,1)S(1)} %collective-permute-done.31, bf16[128,1024]{1,0:T(8,128)(2,1)} %copy-done.5), kind=kOutput, calls=%fused_computation.38 | convolution fusion | flops 204013568 | bytes 1736704 | tf_op jit(solution)/shard_map/dot_general | solution.py:291
  144.0 2.1 %fusion.24 = f32[192,256]{1,0:T(8,128)} fusion(f32[192,256]{1,0:T(8,128)} %fusion.18, bf16[192,256]{1,0:T(8,128)(2,1)S(1)} %get-tuple-element.72, bf16[192,2048]{1,0:T(8,128)(2,1)S(1)} %shard_map.70, bf16[128,1024]{1,0:T(8,128)(2,1)S(1)} %collective-permute-done.28, bf16[128,1024]{1,0:T(8,128)(2,1)S(1)} %copy-done.8), kind=kOutput, calls=%fused_computation.44 | convolution fusion | flops 204062720 | bytes 1933312 | tf_op jit(solution)/shard_map/dot_general | solution.py:291
  148.5 1.1 collective-permute-start.33
  149.6 1.2 collective-permute-start.34
  150.8 2.1 %collective-permute-start.35 = (f16[64,256]{1,0:T(8,128)(2,1)S(1)}, f16[64,256]{1,0:T(8,128)(2,1)S(1)}, u32[]{:S(2)}, u32[]{:S(2)}) collective-permute-start(f16[64,256]{1,0:T(8,128)(2,1)S(1)} %get-tuple-element.112), channel_id=1, source_target_pairs={{0,6},{1,7},{2,4},{3,5},{4,2},{5,3},{6,0},{7,1},{8,14},{9,15},{10,... | collective-permute-start | bytes 98312 | tf_op jit(solution)/shard_map/ppermute | solution.py:240
  153.0 2.1 %collective-permute-done.34 = f16[64,256]{1,0:T(8,128)(2,1)S(1)} collective-permute-done((f16[64,256]{1,0:T(8,128)(2,1)S(1)}, f16[64,256]{1,0:T(8,128)(2,1)S(1)}, u32[]{:S(2)}, u32[]{:S(2)}) %collective-permute-start.34) | collective-permute-done | bytes 32800 | tf_op jit(solution)/shard_map/ppermute | solution.py:240
  155.1 1.4 collective-permute-done.35
  157.4 2.2 %collective-permute-start.38 = (bf16[48,256]{1,0:T(8,128)(2,1)S(1)}, bf16[48,256]{1,0:T(8,128)(2,1)S(1)}, u32[]{:S(2)}, u32[]{:S(2)}) collective-permute-start(bf16[48,256]{1,0:T(8,128)(2,1)S(1)} %get-tuple-element.54), channel_id=1, source_target_pairs={{0,6},{1,7},{2,4},{3,5},{4,2},{5,3},{6,0},{7,1},{8,14},{9,15},{10,... | collective-permute-start | bytes 73736 | tf_op jit(solution)/shard_map/ppermute | solution.py:240
  159.6 2.2 %collective-permute-start.36 = (bf16[48,256]{1,0:T(8,128)(2,1)S(1)}, bf16[48,256]{1,0:T(8,128)(2,1)S(1)}, u32[]{:S(2)}, u32[]{:S(2)}) collective-permute-start(bf16[48,256]{1,0:T(8,128)(2,1)S(1)} %get-tuple-element.54), channel_id=1, source_target_pairs={{0,2},{1,3},{2,0},{3,1},{4,6},{5,7},{6,4},{7,5},{8,10},{9,11},{10,... | collective-permute-start | bytes 73736 | tf_op jit(solution)/shard_map/ppermute | solution.py:240
  163.1 1.2 collective-permute-done.37
  164.4 1.1 collective-permute-start.39
  166.0 3.0 %collective-permute-done.39 = bf16[192,256]{1,0:T(8,128)(2,1)S(1)} collective-permute-done((bf16[192,256]{1,0:T(8,128)(2,1)S(1)}, bf16[192,256]{1,0:T(8,128)(2,1)S(1)}, u32[]{:S(2)}, u32[]{:S(2)}) %collective-permute-start.39) | collective-permute-done | bytes 98336 | tf_op jit(solution)/shard_map/ppermute | solution.py:240
  172.0 1.5 collective-permute-start.43
  174.2 1.1 collective-permute-start.42
  176.3 4.3 %collective-permute-done.42 = f16[64,1024]{1,0:T(8,128)(2,1)S(1)} collective-permute-done((f16[64,1024]{1,0:T(8,128)(2,1)S(1)}, f16[64,1024]{1,0:T(8,128)(2,1)S(1)}, u32[]{:S(2)}, u32[]{:S(2)}) %collective-permute-start.42) | collective-permute-done | bytes 131104 | tf_op jit(solution)/shard_map/ppermute | solution.py:243
  180.6 2.1 %collective-permute-done.45 = f16[64,1024]{1,0:T(8,128)(2,1)S(1)} collective-permute-done((f16[64,1024]{1,0:T(8,128)(2,1)S(1)}, f16[64,1024]{1,0:T(8,128)(2,1)S(1)}, u32[]{:S(2)}, u32[]{:S(2)}) %collective-permute-start.45) | collective-permute-done | bytes 131104 | tf_op jit(solution)/shard_map/ppermute | solution.py:243
  (160 shorter events, 29.1 us)
Async XLA Ops:
  0.6 15.2 %collective-permute-start.3 = (f32[64,2048]{1,0:T(8,128)}, f32[64,2048]{1,0:T(8,128)S(1)}, u32[]{:S(2)}, u32[]{:S(2)}) collective-permute-start(f32[64,2048]{1,0:T(8,128)} %param.9), channel_id=1, source_target_pairs={{0,16},{8,24},{16,0},{24,8},{1,17},{9,25},{17,1},{25,9},{2,18},{10... | collective-permute-start | bytes 1572872 | tf_op jit(solution)/shard_map/ppermute | solution.py:243
  16.9 35.5 %collective-permute-start.4 = (bf16[128,2048]{1,0:T(8,128)(2,1)S(1)}, bf16[128,2048]{1,0:T(8,128)(2,1)S(1)}, u32[]{:S(2)}, u32[]{:S(2)}) collective-permute-start(bf16[128,2048]{1,0:T(8,128)(2,1)S(1)} %convert_element_type.311.refs_4_.refs_8_), channel_id=1, source_target_pairs={{0,8},{8,0},{16,24},{24,16},{1,9},{9,1},{17,25},{25,17},{2,10},{10... | collective-permute-start | bytes 1572872 | tf_op jit(solution)/shard_map/ppermute | solution.py:243
  27.1 39.0 %copy-start.9 = (bf16[32,2048]{1,0:T(8,128)(2,1)S(1)}, bf16[32,2048]{1,0:T(8,128)(2,1)}, u32[]{:S(2)}) copy-start(bf16[32,2048]{1,0:T(8,128)(2,1)} %get-tuple-element.46) | copy-start | bytes 393220
  27.1 63.9 %copy-start.4 = (f32[48,256]{1,0:T(8,128)S(1)}, f32[48,256]{1,0:T(8,128)}, u32[]{:S(2)}) copy-start(f32[48,256]{1,0:T(8,128)} %refs_4_.1) | copy-start | bytes 147460
  33.9 8.3 %collective-permute-start = (bf16[48,2304]{1,0:T(8,128)(2,1)}, bf16[48,2304]{1,0:T(8,128)(2,1)S(1)}, u32[]{:S(2)}, u32[]{:S(2)}) collective-permute-start(bf16[48,2304]{1,0:T(8,128)(2,1)} %get-tuple-element.32), channel_id=1, source_target_pairs={{0,1},{1,0},{2,3},{3,2},{4,5},{5,4},{6,7},{7,6},{8,9},{9,8},{10,11... | collective-permute-start | bytes 663560 | tf_op jit(solution)/shard_map/ppermute | solution.py:240
  35.7 11.1 %collective-permute-start.1 = (bf16[48,2304]{1,0:T(8,128)(2,1)}, bf16[48,2304]{1,0:T(8,128)(2,1)S(1)}, u32[]{:S(2)}, u32[]{:S(2)}) collective-permute-start(bf16[48,2304]{1,0:T(8,128)(2,1)} %get-tuple-element.33), channel_id=1, source_target_pairs={{0,2},{1,3},{2,0},{3,1},{4,6},{5,7},{6,4},{7,5},{8,10},{9,11},{10,... | collective-permute-start | bytes 663560 | tf_op jit(solution)/shard_map/ppermute | solution.py:240
  37.3 11.1 %collective-permute-start.2 = (bf16[48,2304]{1,0:T(8,128)(2,1)}, bf16[48,2304]{1,0:T(8,128)(2,1)S(1)}, u32[]{:S(2)}, u32[]{:S(2)}) collective-permute-start(bf16[48,2304]{1,0:T(8,128)(2,1)} %get-tuple-element.34), channel_id=1, source_target_pairs={{0,3},{1,2},{2,1},{3,0},{4,7},{5,6},{6,5},{7,4},{8,11},{9,10},{10,... | collective-permute-start | bytes 663560 | tf_op jit(solution)/shard_map/ppermute | solution.py:240
  37.4 48.2 %collective-permute-start.8 = (bf16[32,2048]{1,0:T(8,128)(2,1)S(1)}, bf16[32,2048]{1,0:T(8,128)(2,1)S(1)}, u32[]{:S(2)}, u32[]{:S(2)}) collective-permute-start(bf16[32,2048]{1,0:T(8,128)(2,1)S(1)} %copy-done.12), channel_id=1, source_target_pairs={{0,7},{1,6},{2,5},{3,4},{4,3},{5,2},{6,1},{7,0},{8,15},{9,14},{10,... | collective-permute-start | bytes 393224 | tf_op jit(solution)/shard_map/ppermute | solution.py:240
  42.2 15.4 %collective-permute-start.9 = (bf16[16,2816]{1,0:T(8,128)(2,1)}, bf16[16,2816]{1,0:T(8,128)(2,1)S(1)}, u32[]{:S(2)}, u32[]{:S(2)}) collective-permute-start(bf16[16,2816]{1,0:T(8,128)(2,1)} %get-tuple-element.41), channel_id=1, source_target_pairs={{0,7},{1,6},{2,5},{3,4},{4,3},{5,2},{6,1},{7,0},{8,15},{9,14},{10,... | collective-permute-start | bytes 270344 | tf_op jit(solution)/shard_map/ppermute | solution.py:240
  46.8 38.8 %collective-permute-start.10 = (bf16[32,2048]{1,0:T(8,128)(2,1)S(1)}, bf16[32,2048]{1,0:T(8,128)(2,1)S(1)}, u32[]{:S(2)}, u32[]{:S(2)}) collective-permute-start(bf16[32,2048]{1,0:T(8,128)(2,1)S(1)} %copy-done.11), channel_id=1, source_target_pairs={{0,6},{1,7},{2,4},{3,5},{4,2},{5,3},{6,0},{7,1},{8,14},{9,15},{10,... | collective-permute-start | bytes 393224 | tf_op jit(solution)/shard_map/ppermute | solution.py:240
  48.4 17.7 %collective-permute-start.11 = (bf16[16,2816]{1,0:T(8,128)(2,1)}, bf16[16,2816]{1,0:T(8,128)(2,1)S(1)}, u32[]{:S(2)}, u32[]{:S(2)}) collective-permute-start(bf16[16,2816]{1,0:T(8,128)(2,1)} %get-tuple-element.43), channel_id=1, source_target_pairs={{0,6},{1,7},{2,4},{3,5},{4,2},{5,3},{6,0},{7,1},{8,14},{9,15},{10,... | collective-permute-start | bytes 270344 | tf_op jit(solution)/shard_map/ppermute | solution.py:240
  52.5 33.2 %collective-permute-start.12 = (bf16[32,2048]{1,0:T(8,128)(2,1)S(1)}, bf16[32,2048]{1,0:T(8,128)(2,1)S(1)}, u32[]{:S(2)}, u32[]{:S(2)}) collective-permute-start(bf16[32,2048]{1,0:T(8,128)(2,1)S(1)} %copy-done.10), channel_id=1, source_target_pairs={{0,5},{1,4},{2,7},{3,6},{4,1},{5,0},{6,3},{7,2},{8,13},{9,12},{10,... | collective-permute-start | bytes 393224 | tf_op jit(solution)/shard_map/ppermute | solution.py:240
  57.6 21.3 %collective-permute-start.13 = (bf16[16,2816]{1,0:T(8,128)(2,1)}, bf16[16,2816]{1,0:T(8,128)(2,1)S(1)}, u32[]{:S(2)}, u32[]{:S(2)}) collective-permute-start(bf16[16,2816]{1,0:T(8,128)(2,1)} %get-tuple-element.45), channel_id=1, source_target_pairs={{0,5},{1,4},{2,7},{3,6},{4,1},{5,0},{6,3},{7,2},{8,13},{9,12},{10,... | collective-permute-start | bytes 270344 | tf_op jit(solution)/shard_map/ppermute | solution.py:240
  66.2 19.5 %collective-permute-start.14 = (bf16[32,2048]{1,0:T(8,128)(2,1)S(1)}, bf16[32,2048]{1,0:T(8,128)(2,1)S(1)}, u32[]{:S(2)}, u32[]{:S(2)}) collective-permute-start(bf16[32,2048]{1,0:T(8,128)(2,1)S(1)} %copy-done.9), channel_id=1, source_target_pairs={{0,4},{1,5},{2,6},{3,7},{4,0},{5,1},{6,2},{7,3},{8,12},{9,13},{10,... | collective-permute-start | bytes 393224 | tf_op jit(solution)/shard_map/ppermute | solution.py:240
  79.0 6.6 %collective-permute-start.15 = (bf16[16,2816]{1,0:T(8,128)(2,1)}, bf16[16,2816]{1,0:T(8,128)(2,1)S(1)}, u32[]{:S(2)}, u32[]{:S(2)}) collective-permute-start(bf16[16,2816]{1,0:T(8,128)(2,1)} %get-tuple-element.47), channel_id=1, source_target_pairs={{0,4},{1,5},{2,6},{3,7},{4,0},{5,1},{6,2},{7,3},{8,12},{9,13},{10,... | collective-permute-start | bytes 270344 | tf_op jit(solution)/shard_map/ppermute | solution.py:240
  86.6 8.6 %collective-permute-start.19 = (f16[64,256]{1,0:T(8,128)(2,1)S(1)}, f16[64,256]{1,0:T(8,128)(2,1)S(1)}, u32[]{:S(2)}, u32[]{:S(2)}) collective-permute-start(f16[64,256]{1,0:T(8,128)(2,1)S(1)} %get-tuple-element.51), channel_id=1, source_target_pairs={{0,7},{1,6},{2,5},{3,4},{4,3},{5,2},{6,1},{7,0},{8,15},{9,14},{10,... | collective-permute-start | bytes 98312 | tf_op jit(solution)/shard_map/ppermute | solution.py:240
  89.7 7.5 %collective-permute-start.18 = (f16[64,256]{1,0:T(8,128)(2,1)S(1)}, f16[64,256]{1,0:T(8,128)(2,1)S(1)}, u32[]{:S(2)}, u32[]{:S(2)}) collective-permute-start(f16[64,256]{1,0:T(8,128)(2,1)S(1)} %get-tuple-element.50), channel_id=1, source_target_pairs={{0,6},{1,7},{2,4},{3,5},{4,2},{5,3},{6,0},{7,1},{8,14},{9,15},{10,... | collective-permute-start | bytes 98312 | tf_op jit(solution)/shard_map/ppermute | solution.py:240
  91.3 6.9 %collective-permute-start.17 = (f16[64,256]{1,0:T(8,128)(2,1)S(1)}, f16[64,256]{1,0:T(8,128)(2,1)S(1)}, u32[]{:S(2)}, u32[]{:S(2)}) collective-permute-start(f16[64,256]{1,0:T(8,128)(2,1)S(1)} %get-tuple-element.49), channel_id=1, source_target_pairs={{0,5},{1,4},{2,7},{3,6},{4,1},{5,0},{6,3},{7,2},{8,13},{9,12},{10,... | collective-permute-start | bytes 98312 | tf_op jit(solution)/shard_map/ppermute | solution.py:240
  91.3 6.8 %collective-permute-start.16 = (f16[64,256]{1,0:T(8,128)(2,1)S(1)}, f16[64,256]{1,0:T(8,128)(2,1)S(1)}, u32[]{:S(2)}, u32[]{:S(2)}) collective-permute-start(f16[64,256]{1,0:T(8,128)(2,1)S(1)} %get-tuple-element.48), channel_id=1, source_target_pairs={{0,4},{1,5},{2,6},{3,7},{4,0},{5,1},{6,2},{7,3},{8,12},{9,13},{10,... | collective-permute-start | bytes 98312 | tf_op jit(solution)/shard_map/ppermute | solution.py:240
  94.6 4.8 %collective-permute-start.7 = (f16[64,256]{1,0:T(8,128)(2,1)S(1)}, f16[64,256]{1,0:T(8,128)(2,1)S(1)}, u32[]{:S(2)}, u32[]{:S(2)}) collective-permute-start(f16[64,256]{1,0:T(8,128)(2,1)S(1)} %get-tuple-element.37), channel_id=1, source_target_pairs={{0,3},{1,2},{2,1},{3,0},{4,7},{5,6},{6,5},{7,4},{8,11},{9,10},{10,... | collective-permute-start | bytes 98312 | tf_op jit(solution)/shard_map/ppermute | solution.py:240
  95.3 4.2 %collective-permute-start.6 = (f16[64,256]{1,0:T(8,128)(2,1)S(1)}, f16[64,256]{1,0:T(8,128)(2,1)S(1)}, u32[]{:S(2)}, u32[]{:S(2)}) collective-permute-start(f16[64,256]{1,0:T(8,128)(2,1)S(1)} %get-tuple-element.36), channel_id=1, source_target_pairs={{0,2},{1,3},{2,0},{3,1},{4,6},{5,7},{6,4},{7,5},{8,10},{9,11},{10,... | collective-permute-start | bytes 98312 | tf_op jit(solution)/shard_map/ppermute | solution.py:240
  97.2 3.9 %collective-permute-start.5 = (f16[64,256]{1,0:T(8,128)(2,1)S(1)}, f16[64,256]{1,0:T(8,128)(2,1)S(1)}, u32[]{:S(2)}, u32[]{:S(2)}) collective-permute-start(f16[64,256]{1,0:T(8,128)(2,1)S(1)} %get-tuple-element.35), channel_id=1, source_target_pairs={{0,1},{1,0},{2,3},{3,2},{4,5},{5,4},{6,7},{7,6},{8,9},{9,8},{10,11... | collective-permute-start | bytes 98312 | tf_op jit(solution)/shard_map/ppermute | solution.py:240
  101.9 5.6 %collective-permute-start.22 = (bf16[48,256]{1,0:T(8,128)(2,1)S(1)}, bf16[48,256]{1,0:T(8,128)(2,1)S(1)}, u32[]{:S(2)}, u32[]{:S(2)}) collective-permute-start(bf16[48,256]{1,0:T(8,128)(2,1)S(1)} %get-tuple-element.73), channel_id=1, source_target_pairs={{0,6},{1,7},{2,4},{3,5},{4,2},{5,3},{6,0},{7,1},{8,14},{9,15},{10,... | collective-permute-start | bytes 73736 | tf_op jit(solution)/shard_map/ppermute | solution.py:240
  104.3 4.7 %collective-permute-start.21 = (bf16[48,256]{1,0:T(8,128)(2,1)S(1)}, bf16[48,256]{1,0:T(8,128)(2,1)S(1)}, u32[]{:S(2)}, u32[]{:S(2)}) collective-permute-start(bf16[48,256]{1,0:T(8,128)(2,1)S(1)} %get-tuple-element.73), channel_id=1, source_target_pairs={{0,4},{1,5},{2,6},{3,7},{4,0},{5,1},{6,2},{7,3},{8,12},{9,13},{10,... | collective-permute-start | bytes 73736 | tf_op jit(solution)/shard_map/ppermute | solution.py:240
  104.3 4.7 %collective-permute-start.20 = (bf16[48,256]{1,0:T(8,128)(2,1)S(1)}, bf16[48,256]{1,0:T(8,128)(2,1)S(1)}, u32[]{:S(2)}, u32[]{:S(2)}) collective-permute-start(bf16[48,256]{1,0:T(8,128)(2,1)S(1)} %get-tuple-element.73), channel_id=1, source_target_pairs={{0,2},{1,3},{2,0},{3,1},{4,6},{5,7},{6,4},{7,5},{8,10},{9,11},{10,... | collective-permute-start | bytes 73736 | tf_op jit(solution)/shard_map/ppermute | solution.py:240
  109.1 4.7 %collective-permute-start.23 = (bf16[192,256]{1,0:T(8,128)(2,1)S(1)}, bf16[192,256]{1,0:T(8,128)(2,1)S(1)}, u32[]{:S(2)}, u32[]{:S(2)}) collective-permute-start(bf16[192,256]{1,0:T(8,128)(2,1)S(1)} %get-tuple-element.72), channel_id=1, source_target_pairs={{0,1},{1,0},{2,3},{3,2},{4,5},{5,4},{6,7},{7,6},{8,9},{9,8},{10,11... | collective-permute-start | bytes 294920 | tf_op jit(solution)/shard_map/ppermute | solution.py:240
  113.9 2.8 %collective-permute-start.25 = (f32[128]{0:T(128)S(1)}, f32[128]{0:T(128)S(1)}, u32[]{:S(2)}, u32[]{:S(2)}) collective-permute-start(f32[128]{0:T(128)S(1)} %slice.271), channel_id=1, source_target_pairs={{0,8},{8,0},{16,24},{24,16},{1,9},{9,1},{17,25},{25,17},{2,10},{10... | collective-permute-start | bytes 1544 | tf_op jit(solution)/shard_map/ppermute | solution.py:243
  114.7 2.1 %collective-permute-start.24 = (f32[128,1024]{1,0:T(8,128)S(1)}, f32[128,1024]{1,0:T(8,128)S(1)}, u32[]{:S(2)}, u32[]{:S(2)}) collective-permute-start(f32[128,1024]{1,0:T(8,128)S(1)} %convolution_add_fusion.6), channel_id=1, source_target_pairs={{0,8},{8,0},{16,24},{24,16},{1,9},{9,1},{17,25},{25,17},{2,10},{10... | collective-permute-start | bytes 1572872 | tf_op jit(solution)/shard_map/ppermute | solution.py:243
  116.1 2.0 %collective-permute-start.29 = (f32[128,1024]{1,0:T(8,128)S(1)}, f32[128,1024]{1,0:T(8,128)S(1)}, u32[]{:S(2)}, u32[]{:S(2)}) collective-permute-start(f32[128,1024]{1,0:T(8,128)S(1)} %convolution_add_fusion.4), channel_id=1, source_target_pairs={{0,8},{8,0},{16,24},{24,16},{1,9},{9,1},{17,25},{25,17},{2,10},{10... | collective-permute-start | bytes 1572872 | tf_op jit(solution)/shard_map/ppermute | solution.py:243
  118.6 14.1 %collective-permute-start.26 = (f16[128,1024]{1,0:T(8,128)(2,1)S(1)}, f16[128,1024]{1,0:T(8,128)(2,1)S(1)}, u32[]{:S(2)}, u32[]{:S(2)}) collective-permute-start(f16[128,1024]{1,0:T(8,128)(2,1)S(1)} %get-tuple-element.126), channel_id=1, source_target_pairs={{0,16},{8,24},{16,0},{24,8},{1,17},{9,25},{17,1},{25,9},{2,18},{10... | collective-permute-start | bytes 786440 | tf_op jit(solution)/shard_map/ppermute | solution.py:243
  120.1 12.6 %collective-permute-start.30 = (f16[128,1024]{1,0:T(8,128)(2,1)S(1)}, f16[128,1024]{1,0:T(8,128)(2,1)S(1)}, u32[]{:S(2)}, u32[]{:S(2)}) collective-permute-start(f16[128,1024]{1,0:T(8,128)(2,1)S(1)} %get-tuple-element.127), channel_id=1, source_target_pairs={{0,16},{8,24},{16,0},{24,8},{1,17},{9,25},{17,1},{25,9},{2,18},{10... | collective-permute-start | bytes 786440 | tf_op jit(solution)/shard_map/ppermute | solution.py:243
  120.7 12.0 %collective-permute-start.27 = (f32[128]{0:T(128)S(1)}, f32[128]{0:T(128)S(1)}, u32[]{:S(2)}, u32[]{:S(2)}) collective-permute-start(f32[128]{0:T(128)S(1)} %pad_maximum_fusion.43), channel_id=1, source_target_pairs={{0,16},{8,24},{16,0},{24,8},{1,17},{9,25},{17,1},{25,9},{2,18},{10... | collective-permute-start | bytes 1544 | tf_op jit(solution)/shard_map/ppermute | solution.py:243
  133.1 1.6 collective-permute-start.31
  133.2 1.9 %collective-permute-start.28 = (bf16[128,1024]{1,0:T(8,128)(2,1)S(1)}, bf16[128,1024]{1,0:T(8,128)(2,1)S(1)}, u32[]{:S(2)}, u32[]{:S(2)}) collective-permute-start(bf16[128,1024]{1,0:T(8,128)(2,1)S(1)} %get-tuple-element.69), channel_id=1, source_target_pairs={{0,8},{8,0},{16,24},{24,16},{1,9},{9,1},{17,25},{25,17},{2,10},{10... | collective-permute-start | bytes 786440 | tf_op jit(solution)/shard_map/ppermute | solution.py:243
  141.3 5.3 %collective-permute-start.32 = (f16[208,256]{1,0:T(8,128)(2,1)}, f16[208,256]{1,0:T(8,128)(2,1)}, u32[]{:S(2)}, u32[]{:S(2)}) collective-permute-start(f16[208,256]{1,0:T(8,128)(2,1)} %pad_maximum_fusion.19), channel_id=1, source_target_pairs={{0,1},{1,0},{2,3},{3,2},{4,5},{5,4},{6,7},{7,6},{8,9},{9,8},{10,11... | collective-permute-start | bytes 319496 | tf_op jit(solution)/shard_map/ppermute | solution.py:240
  148.5 4.5 %collective-permute-start.33 = (f16[64,256]{1,0:T(8,128)(2,1)S(1)}, f16[64,256]{1,0:T(8,128)(2,1)S(1)}, u32[]{:S(2)}, u32[]{:S(2)}) collective-permute-start(f16[64,256]{1,0:T(8,128)(2,1)S(1)} %get-tuple-element.113), channel_id=1, source_target_pairs={{0,2},{1,3},{2,0},{3,1},{4,6},{5,7},{6,4},{7,5},{8,10},{9,11},{10,... | collective-permute-start | bytes 98312 | tf_op jit(solution)/shard_map/ppermute | solution.py:240
  149.6 5.5 %collective-permute-start.34 = (f16[64,256]{1,0:T(8,128)(2,1)S(1)}, f16[64,256]{1,0:T(8,128)(2,1)S(1)}, u32[]{:S(2)}, u32[]{:S(2)}) collective-permute-start(f16[64,256]{1,0:T(8,128)(2,1)S(1)} %get-tuple-element.114), channel_id=1, source_target_pairs={{0,4},{1,5},{2,6},{3,7},{4,0},{5,1},{6,2},{7,3},{8,12},{9,13},{10,... | collective-permute-start | bytes 98312 | tf_op jit(solution)/shard_map/ppermute | solution.py:240
  150.8 5.7 %collective-permute-start.35 = (f16[64,256]{1,0:T(8,128)(2,1)S(1)}, f16[64,256]{1,0:T(8,128)(2,1)S(1)}, u32[]{:S(2)}, u32[]{:S(2)}) collective-permute-start(f16[64,256]{1,0:T(8,128)(2,1)S(1)} %get-tuple-element.112), channel_id=1, source_target_pairs={{0,6},{1,7},{2,4},{3,5},{4,2},{5,3},{6,0},{7,1},{8,14},{9,15},{10,... | collective-permute-start | bytes 98312 | tf_op jit(solution)/shard_map/ppermute | solution.py:240
  157.4 5.7 %collective-permute-start.38 = (bf16[48,256]{1,0:T(8,128)(2,1)S(1)}, bf16[48,256]{1,0:T(8,128)(2,1)S(1)}, u32[]{:S(2)}, u32[]{:S(2)}) collective-permute-start(bf16[48,256]{1,0:T(8,128)(2,1)S(1)} %get-tuple-element.54), channel_id=1, source_target_pairs={{0,6},{1,7},{2,4},{3,5},{4,2},{5,3},{6,0},{7,1},{8,14},{9,15},{10,... | collective-permute-start | bytes 73736 | tf_op jit(solution)/shard_map/ppermute | solution.py:240
  159.6 4.7 %collective-permute-start.37 = (bf16[48,256]{1,0:T(8,128)(2,1)S(1)}, bf16[48,256]{1,0:T(8,128)(2,1)S(1)}, u32[]{:S(2)}, u32[]{:S(2)}) collective-permute-start(bf16[48,256]{1,0:T(8,128)(2,1)S(1)} %get-tuple-element.54), channel_id=1, source_target_pairs={{0,4},{1,5},{2,6},{3,7},{4,0},{5,1},{6,2},{7,3},{8,12},{9,13},{10,... | collective-permute-start | bytes 73736 | tf_op jit(solution)/shard_map/ppermute | solution.py:240
  159.6 4.7 %collective-permute-start.36 = (bf16[48,256]{1,0:T(8,128)(2,1)S(1)}, bf16[48,256]{1,0:T(8,128)(2,1)S(1)}, u32[]{:S(2)}, u32[]{:S(2)}) collective-permute-start(bf16[48,256]{1,0:T(8,128)(2,1)S(1)} %get-tuple-element.54), channel_id=1, source_target_pairs={{0,2},{1,3},{2,0},{3,1},{4,6},{5,7},{6,4},{7,5},{8,10},{9,11},{10,... | collective-permute-start | bytes 73736 | tf_op jit(solution)/shard_map/ppermute | solution.py:240
  164.4 4.7 %collective-permute-start.39 = (bf16[192,256]{1,0:T(8,128)(2,1)S(1)}, bf16[192,256]{1,0:T(8,128)(2,1)S(1)}, u32[]{:S(2)}, u32[]{:S(2)}) collective-permute-start(bf16[192,256]{1,0:T(8,128)(2,1)S(1)} %get-tuple-element.53), channel_id=1, source_target_pairs={{0,1},{1,0},{2,3},{3,2},{4,5},{5,4},{6,7},{7,6},{8,9},{9,8},{10,11... | collective-permute-start | bytes 294920 | tf_op jit(solution)/shard_map/ppermute | solution.py:240
  169.9 3.7 %collective-permute-start.40 = (f32[128,1024]{1,0:T(8,128)S(1)}, f32[128,1024]{1,0:T(8,128)S(1)}, u32[]{:S(2)}, u32[]{:S(2)}) collective-permute-start(f32[128,1024]{1,0:T(8,128)S(1)} %convolution_add_fusion.2), channel_id=1, source_target_pairs={{0,8},{8,0},{16,24},{24,16},{1,9},{9,1},{17,25},{25,17},{2,10},{10... | collective-permute-start | bytes 1572872 | tf_op jit(solution)/shard_map/ppermute | solution.py:243
  170.0 1.9 %collective-permute-start.41 = (f32[128]{0:T(128)S(1)}, f32[128]{0:T(128)S(1)}, u32[]{:S(2)}, u32[]{:S(2)}) collective-permute-start(f32[128]{0:T(128)S(1)} %slice.309), channel_id=1, source_target_pairs={{0,8},{8,0},{16,24},{24,16},{1,9},{9,1},{17,25},{25,17},{2,10},{10... | collective-permute-start | bytes 1544 | tf_op jit(solution)/shard_map/ppermute | solution.py:243
  171.4 2.4 %collective-permute-start.44 = (f32[128,1024]{1,0:T(8,128)S(1)}, f32[128,1024]{1,0:T(8,128)S(1)}, u32[]{:S(2)}, u32[]{:S(2)}) collective-permute-start(f32[128,1024]{1,0:T(8,128)S(1)} %convolution_add_fusion), channel_id=1, source_target_pairs={{0,8},{8,0},{16,24},{24,16},{1,9},{9,1},{17,25},{25,17},{2,10},{10... | collective-permute-start | bytes 1572872 | tf_op jit(solution)/shard_map/ppermute | solution.py:243
  172.0 4.3 %collective-permute-start.43 = (f32[64]{0:T(128)S(1)}, f32[64]{0:T(128)S(1)}, u32[]{:S(2)}, u32[]{:S(2)}) collective-permute-start(f32[64]{0:T(128)S(1)} %slice.310), channel_id=1, source_target_pairs={{0,16},{8,24},{16,0},{24,8},{1,17},{9,25},{17,1},{25,9},{2,18},{10... | collective-permute-start | bytes 776 | tf_op jit(solution)/shard_map/ppermute | solution.py:243
  174.2 6.4 %collective-permute-start.42 = (f16[64,1024]{1,0:T(8,128)(2,1)S(1)}, f16[64,1024]{1,0:T(8,128)(2,1)S(1)}, u32[]{:S(2)}, u32[]{:S(2)}) collective-permute-start(f16[64,1024]{1,0:T(8,128)(2,1)S(1)} %get-tuple-element.124), channel_id=1, source_target_pairs={{0,16},{8,24},{16,0},{24,8},{1,17},{9,25},{17,1},{25,9},{2,18},{10... | collective-permute-start | bytes 393224 | tf_op jit(solution)/shard_map/ppermute | solution.py:243
  175.3 7.4 %collective-permute-start.45 = (f16[64,1024]{1,0:T(8,128)(2,1)S(1)}, f16[64,1024]{1,0:T(8,128)(2,1)S(1)}, u32[]{:S(2)}, u32[]{:S(2)}) collective-permute-start(f16[64,1024]{1,0:T(8,128)(2,1)S(1)} %get-tuple-element.125), channel_id=1, source_target_pairs={{0,16},{8,24},{16,0},{24,8},{1,17},{9,25},{17,1},{25,9},{2,18},{10... | collective-permute-start | bytes 393224 | tf_op jit(solution)/shard_map/ppermute | solution.py:243
  (11 other events, 134.6 us)

commit v2 on v1

--- a/solution.py
+++ b/solution.py
@@ -163,27 +163,40 @@
 PARTS = 2
 
 
-def ratio_tile(data_refs, w, h_refs, at, tile):
-    h_tile = jnp.concatenate([ref[:, at : at + tile] for ref in h_refs], axis=0)
-    product = jnp.dot(w, h_tile, preferred_element_type=F32)
-    values = jnp.concatenate([ref[:, at : at + tile] for ref in data_refs], axis=0).astype(F32)
-    return (values / product).astype(BF16), h_tile
-
-
-def w_term_body(*refs):
-    *data_refs, h_one, h_two, out_ref = refs
-    pixels = h_one.shape[1]
+def w_term_body(*refs, count, carried, scale):
+    out_ref = refs[-1]
+    data_refs, rest = refs[:count], list(refs[count:-1])
     rank = out_ref.shape[1]
-    w = jnp.concatenate([ref[:, at : at + rank] for ref in data_refs for at in range(pixels, ref.shape[1], rank)], axis=0)
-    tile = min(TILE, pixels)
-    ones = jnp.ones((16, tile), BF16)
-    total = None
-    for at in range(0, pixels, tile):
-        ratio, h_tile = ratio_tile(data_refs, w, (h_one, h_two), at, tile)
-        ratio = jnp.concatenate([ratio, ones], axis=0)
-        term = lax.dot_general(ratio, h_tile, (((1,), (1,)), ((), ())), preferred_element_type=F32)
-        total = term if total is None else total + term
-    out_ref[...] = total
+    rows = sum(ref.shape[0] for ref in data_refs)
+    by = None if carried else rest.pop(0)[...]
+    w_ref = None if carried else rest.pop(0)
+    pixels = sum(ref.shape[1] for ref in rest[::2])
+    if carried:
+        w = jnp.concatenate([ref[:, at : at + rank] for ref in data_refs for at in range(pixels, ref.shape[1], rank)], axis=0)
+    else:
+        w = w_ref[...]
+    total, start = None, 0
+    for pair in zip(rest[::2], rest[1::2]):
+        width = pair[0].shape[1]
+        tile = min(TILE, width)
+        ones = jnp.ones((16, tile), BF16)
+        for at in range(0, width, tile):
+            h_tile = jnp.concatenate([ref[:, at : at + tile] for ref in pair], axis=0)
+            product = jnp.dot(w, h_tile, preferred_element_type=F32)
+            values = jnp.concatenate([ref[:, start + at : start + at + tile] for ref in data_refs], axis=0).astype(F32)
+            ratio = jnp.concatenate([(values / product).astype(BF16), ones], axis=0)
+            term = lax.dot_general(ratio, h_tile, (((1,), (1,)), ((), ())), preferred_element_type=F32)
+            total = term if total is None else total + term
+        start += width
+    sums = total[rows : rows + 1]
+    if carried:
+        numerators, sums = total[:rows] * scale, sums * scale
+    else:
+        numerators, sums = (total[:rows] - sums) / by, sums / by
+    high = sums.astype(BF16).astype(F32)
+    line = lax.broadcasted_iota(jnp.int32, (16, rank), 0)
+    out_ref[:rows] = numerators
+    out_ref[rows:] = jnp.where(line == 0, high, jnp.where(line == 1, sums - high, 0.0))
 
 
 def tiles_body(*refs):
@@ -209,18 +222,9 @@
     )(*[pltpu.with_memory_space_constraint(a, pltpu.VMEM) for a in args])
 
 
-def halves(value):
-    high = value.astype(F16)
-    return high, (value - high.astype(F32)).astype(F16)
-
-
-def with_sums(block, sums):
-    high, low = halves(sums)
-    return jnp.concatenate([block.astype(F16), high[None], low[None], jnp.zeros((14, len(sums)), F16)], axis=0)
-
-
 def groups_of(n_pix):
-    return [list(range(n_pix // 2)), list(range(n_pix - 1, n_pix // 2 - 1, -1))]
+    far = list(range(n_pix - 1, n_pix // 2 - 1, -1))
+    return [list(range(n_pix // 2)), far[: len(far) // 2], far[len(far) // 2 :]]
 
 
 def local(raw_frames, gain_map, coupling, factor_w, factor_h, n_scan, n_pix):
@@ -276,57 +280,49 @@
         return [part for r in which for part in tile[r]]
 
     for rounds in range(ITERS):
-        if rounds:
-            h_part = sum(jnp.concatenate([jnp.sum(h.astype(F32), axis=1) for h in pair]) for pair in h_pairs)
-
         def ratio_of(values, w_round, pair):
             product = jnp.dot(w_round, jnp.concatenate(pair, axis=0), preferred_element_type=F32)
             return (values.astype(F32) / product).astype(BF16)
 
-        def numerator_of(values, w_round):
-            terms = []
-            for part, pair in zip(parts, h_pairs):
-                ratio = ratio_of(values[:, part], w_round, pair)
-                h_block = jnp.concatenate(pair, axis=0)
-                terms.append(lax.dot_general(ratio, h_block, (((1,), (1,)), ((), ())), preferred_element_type=F32))
-            return sum(terms)
+        def w_term(data, h_list, w=None):
+            rows = sum(d.shape[0] for d in data)
+            body = functools.partial(w_term_body, count=len(data), carried=w is None, scale=scale)
+            args = [*data, *([] if w is None else [first_sums, w]), *h_list]
+            return term(body, (rows + 16, rank), F32, args, 4 * rows * rank * pixels)
+
+        def block_of(values, i):
+            rows = values.shape[0] - 16
+            return jnp.concatenate([values[row_count * i : row_count * (i + 1)], values[rows:]], axis=0)
+
+        def combined(values, others):
+            return functools.reduce(lambda a, b: a + b, [o.astype(F32) for o in others], values)
 
         if rounds == 0:
             backs, h_here = [], [h_mine, h_other]
             for group in groups_of(n_pix):
-                rows = row_count * len(group)
-                shape = (rows + 16, rank)
-                partial = term(w_term_body, shape, F32, blocks(group) + h_here, 4 * rows * rank * pixels) * scale
-                h_sums = partial[rows]
+                partial = w_term(blocks(group), h_here)
                 messages = {}
                 for j, r in enumerate(group):
-                    block = partial[row_count * j : row_count * (j + 1)]
                     if r == 0:
-                        numerator = block
+                        numerator = block_of(partial, j)
                     else:
-                        messages[r] = with_sums(block, h_sums)
+                        messages[r] = block_of(partial, j).astype(F16)
                 h_here, messages = lax.optimization_barrier((h_here, messages))
                 for r, message in messages.items():
                     backs.append(over_pix(message, r))
-            everything = functools.reduce(lambda a, b: a + b, [b.astype(F32) for b in backs])
-            numerator = numerator + everything[:row_count]
-            h_sums = h_sums + everything[row_count] + everything[row_count + 1]
+            numerator = combined(numerator, backs)
+            h_sums = numerator[row_count : row_count + 1] + numerator[row_count + 1 : row_count + 2]
+            first_sums = h_sums
+            w_local = w_local * numerator[:row_count] / h_sums
         else:
-            rows = row_count * len(even)
-            away = numerator_of(data_odd, w_odd)
-            back = over_pix(with_sums(away / h_part - 1.0, h_part), 1)
-            near = lax.optimization_barrier(numerator_of(data_even, w_even))
-            weight = back[rows].astype(F32) + back[rows + 1].astype(F32)
-            near = near + (back[:rows].astype(F32) + 1.0) * weight
-            h_two = h_part + weight
-            numerator, h_sums = near[:row_count], h_two
-            for i, r in enumerate(far):
-                mean = near[row_count * (i + 1) : row_count * (i + 2)] / h_two - 1.0
-                back = over_pix(with_sums(mean, h_two), r)
-                weight = back[row_count].astype(F32) + back[row_count + 1].astype(F32)
-                numerator = numerator + (back[:row_count].astype(F32) + 1.0) * weight
-                h_sums = h_sums + weight
-        w_local = w_local * numerator / h_sums
+            h_list = [h for pair in h_pairs for h in pair]
+            back = over_pix(w_term([data_odd], h_list, w_odd).astype(F16), 1)
+            near = w_term([data_even], h_list, w_even)
+            near = combined(near, [back])
+            backs = [over_pix(block_of(near, i + 1).astype(F16), r) for i, r in enumerate(far)]
+            numerator = combined(block_of(near, 0), backs)
+            h_sums = numerator[row_count : row_count + 1] + numerator[row_count + 1 : row_count + 2]
+            w_local = w_local * (numerator[:row_count] + h_sums) / h_sums
 
         w_mine = w_local.astype(BF16)
         w_even = jnp.concatenate([w_mine] + [over_pix(w_mine, r) for r in far], axis=0)
@@ -348,9 +344,12 @@
             evens.append([numerator_rows(w, ratio) for w in (w_even[:, :half], w_even[:, half:])])
         totals = []
         for c, (part, pair) in enumerate(zip(parts, h_pairs)):
-            ratio = ratio_of(data_odd[:, part], w_odd, pair)
-            other = over_scan(evens[c][1] + numerator_rows(w_odd[:, half:], ratio), 1)
-            totals.append(evens[c][0] + numerator_rows(w_odd[:, :half], ratio) + other)
+            w_here = w_odd
+            if c:
+                w_here, _ = lax.optimization_barrier((w_odd, other))
+            ratio = ratio_of(data_odd[:, part], w_here, pair)
+            other = evens[c][1] + numerator_rows(w_here[:, half:], ratio)
+            totals.append(evens[c][0] + numerator_rows(w_here[:, :half], ratio) + over_scan(other, 1))
         for bit in x_bits[::-1]:
             count = totals[0].shape[0] // comp_rows
             step = bit >> 1
@@ -368,16 +367,23 @@
 
             sums = pick(w_sums, send)
             weight = over_scan(sums, bit)
+            backs = []
             for c in range(PARTS):
-                message = (pick(totals[c], send) / sums[:, None] - 1.0).astype(F16)
-                back = over_scan(message, bit).astype(F32) + 1.0
-                totals[c] = pick(totals[c], keep) + back * weight[:, None]
+                value = totals[c]
+                if c:
+                    value, _ = lax.optimization_barrier((value, message))
+                message = (pick(value, send) / sums[:, None] - 1.0).astype(F16)
+                backs.append(over_scan(message, bit))
+            for c in range(PARTS):
+                if c and bit == x_bits[0]:
+                    backs[c], h_own[c - 1] = lax.optimization_barrier((backs[c], h_own[c - 1]))
+                totals[c] = pick(totals[c], keep) + (backs[c].astype(F32) + 1.0) * weight[:, None]
+                if bit == x_bits[0]:
+                    h_own[c] = h_own[c][: totals[c].shape[0]] * totals[c] / (pick(w_sums, keep) + weight)[:, None]
+                    if not last:
+                        h_mine = h_own[c].astype(BF16)
+                        h_pairs[c] = [h_mine, over_scan(h_mine, 1)]
             w_sums = pick(w_sums, keep) + weight
-        for c in range(PARTS):
-            h_own[c] = h_own[c][: totals[c].shape[0]] * totals[c] / w_sums[:, None]
-            if not last:
-                h_mine = h_own[c].astype(BF16)
-                h_pairs[c] = [h_mine, over_scan(h_mine, 1)]
     return (to_global(w_local), jnp.concatenate(h_own, axis=1))
 
 

time: 184 us -> 174 us (0.946)
  matrix products: 14.9 us -> 6.16 us
  other arithmetic: 9.03 us -> 4.17 us
  Pallas kernels: 18.1 us -> 20.8 us
  starting transfers between devices: 74.4 us -> 76.9 us
    dot_general x4 -> x0, matrix products: 8.71 us -> none  [numerator_of(): lax.dot_general(ratio, h_block, (((1,), (1,)), ((), ())), preferred_eleme...]
    ppermute x30, waiting for transfers between devices: 32.3 us -> 29.4 us  [over_pix(): return lax.ppermute(value, 'pix', [(i, i ^ bit) for i in range(n_pix)])]
    ppermute x30, starting transfers between devices: 62.2 us -> 65 us  [over_pix(): return lax.ppermute(value, 'pix', [(i, i ^ bit) for i in range(n_pix)])]
    pallas_call x4 -> x7, Pallas kernels: 1.83 us -> 4.56 us  [term(): pl.pallas_call(body, out_shape=pltpu.VMEM(shape, dtype), in_specs=[VMEM]...]
    ppermute x16, waiting for transfers between devices: 30.2 us -> 32.3 us  [over_scan(): return lax.ppermute(value, 'scan', [(i, i ^ bit) for i in range(n_scan)])]
  transfers between devices with their start and end apart: 46 -> 46, of which waited for: 21 -> 25; matrix products, arithmetic and copies ran while one was open for 7% -> 5% of each run, Pallas kernels for 9% -> 11%
where the time goes in v2:
time: 174 us
  starting transfers between devices  76.9 us (44%)
  waiting for transfers between devices  61.8 us (36%)
  Pallas kernels  20.8 us (12%)
  matrix products  6.16 us (4%)
  other arithmetic  4.17 us (2%)
  local copies, waits for them, and re-layouts  2.51 us (1%)
    ppermute x30, starting transfers between devices, over_pix(): return lax.ppermute(value, 'pix', [(i, i ^ bit) for i in range(n_pix)])  65 us
    ppermute x16, waiting for transfers between devices, over_scan(): return lax.ppermute(value, 'scan', [(i, i ^ bit) for i in range(n_scan)])  32.3 us
    ppermute x30, waiting for transfers between devices, over_pix(): return lax.ppermute(value, 'pix', [(i, i ^ bit) for i in range(n_pix)])  29.4 us
    pallas_call x2, Pallas kernels, correct(): pl.pallas_call(functools.partial(stencil_body, start=start, order=order,...  16.2 us
    ppermute x16, starting transfers between devices, over_scan(): return lax.ppermute(value, 'scan', [(i, i ^ bit) for i in range(n_scan)])  12 us
    pallas_call x7, Pallas kernels, term(): pl.pallas_call(body, out_shape=pltpu.VMEM(shape, dtype), in_specs=[VMEM]...  4.56 us
    dot_general x16, matrix products, numerator_rows(): lax.dot_general(w, ratio, (((0,), (0,)), ((), ())), preferred_element_typ...  3.92 us
  transfers between devices with their start and end apart: 46, of which 25 were waited for; matrix products, arithmetic and copies ran while one was open for 5% of the time, Pallas kernels for 11%

profile of v2, /device:TPU:0, one launch (start us, length us, event | category | flops | bytes accessed | tf_op | source)
XLA Modules:
  0.0 173.7 jit_solution(5045755987571142251)
XLA Ops:
  0.6 3.0 %collective-permute-start.3 = (f32[64,2048]{1,0:T(8,128)}, f32[64,2048]{1,0:T(8,128)S(1)}, u32[]{:S(2)}, u32[]{:S(2)}) collective-permute-start(f32[64,2048]{1,0:T(8,128)} %param.9), channel_id=1, source_target_pairs={{0,16},{8,24},{16,0},{24,8},{1,17},{9,25},{17,1},{25,9},{2,18},{10... | collective-permute-start | bytes 1572872 | tf_op jit(solution)/shard_map/ppermute | solution.py:247
  3.7 1.1 constant_dynamic-update-slice_fusion.1
  4.8 11.0 %collective-permute-done.3 = f32[64,2048]{1,0:T(8,128)S(1)} collective-permute-done((f32[64,2048]{1,0:T(8,128)}, f32[64,2048]{1,0:T(8,128)S(1)}, u32[]{:S(2)}, u32[]{:S(2)}) %collective-permute-start.3) | collective-permute-done | bytes 524320 | tf_op jit(solution)/shard_map/ppermute | solution.py:247
  16.7 9.5 %charge_sharing.2 = (bf16[32,2048]{1,0:T(8,128)(2,1)}, bf16[32,2048]{1,0:T(8,128)(2,1)}, bf16[32,2048]{1,0:T(8,128)(2,1)}, bf16[32,2048]{1,0:T(8,128)(2,1)}, bf1...) custom-call(s32[2]{0:T(128)} %pad_add_fusion.me_ref, ...), custom_call_target="tpu_custom_call" | custom-call | flops 18874368 | bytes 3145728 | tf_op jit(solution)/shard_map/charge_sharing/pallas_call | solution.py:138
  26.1 6.8 %charge_sharing.3 = (bf16[48,2304]{1,0:T(8,128)(2,1)}, bf16[48,2304]{1,0:T(8,128)(2,1)}, bf16[48,2304]{1,0:T(8,128)(2,1)}, bf16[48,2304]{1,0:T(8,128)(2,1)}, bf1...) custom-call(s32[2]{0:T(128)} %pad_add_fusion.me_ref, ...), custom_call_target="tpu_custom_call" | custom-call | flops 9437184 | bytes 1572864 | tf_op jit(solution)/shard_map/charge_sharing/pallas_call | solution.py:138
  32.9 1.8 %collective-permute-start = (bf16[48,2304]{1,0:T(8,128)(2,1)}, bf16[48,2304]{1,0:T(8,128)(2,1)S(1)}, u32[]{:S(2)}, u32[]{:S(2)}) collective-permute-start(bf16[48,2304]{1,0:T(8,128)(2,1)} %get-tuple-element.42), channel_id=1, source_target_pairs={{0,1},{1,0},{2,3},{3,2},{4,5},{5,4},{6,7},{7,6},{8,9},{9,8},{10,11... | collective-permute-start | bytes 663560 | tf_op jit(solution)/shard_map/ppermute | solution.py:244
  34.7 1.6 collective-permute-start.1
  36.4 4.8 %collective-permute-start.8 = (bf16[32,2048]{1,0:T(8,128)(2,1)S(1)}, bf16[32,2048]{1,0:T(8,128)(2,1)S(1)}, u32[]{:S(2)}, u32[]{:S(2)}) collective-permute-start(bf16[32,2048]{1,0:T(8,128)(2,1)S(1)} %copy-done.6), channel_id=1, source_target_pairs={{0,7},{1,6},{2,5},{3,4},{4,3},{5,2},{6,1},{7,0},{8,15},{9,14},{10,... | collective-permute-start | bytes 393224 | tf_op jit(solution)/shard_map/ppermute | solution.py:244
  41.2 4.5 %collective-permute-start.9 = (bf16[16,2816]{1,0:T(8,128)(2,1)}, bf16[16,2816]{1,0:T(8,128)(2,1)S(1)}, u32[]{:S(2)}, u32[]{:S(2)}) collective-permute-start(bf16[16,2816]{1,0:T(8,128)(2,1)} %get-tuple-element.51), channel_id=1, source_target_pairs={{0,7},{1,6},{2,5},{3,4},{4,3},{5,2},{6,1},{7,0},{8,15},{9,14},{10,... | collective-permute-start | bytes 270344 | tf_op jit(solution)/shard_map/ppermute | solution.py:244
  47.4 4.0 %collective-permute-start.11 = (bf16[16,2816]{1,0:T(8,128)(2,1)}, bf16[16,2816]{1,0:T(8,128)(2,1)S(1)}, u32[]{:S(2)}, u32[]{:S(2)}) collective-permute-start(bf16[16,2816]{1,0:T(8,128)(2,1)} %get-tuple-element.53), channel_id=1, source_target_pairs={{0,6},{1,7},{2,4},{3,5},{4,2},{5,3},{6,0},{7,1},{8,14},{9,15},{10,... | collective-permute-start | bytes 270344 | tf_op jit(solution)/shard_map/ppermute | solution.py:244
  51.5 3.3 %collective-permute-start.14 = (bf16[32,2048]{1,0:T(8,128)(2,1)S(1)}, bf16[32,2048]{1,0:T(8,128)(2,1)S(1)}, u32[]{:S(2)}, u32[]{:S(2)}) collective-permute-start(bf16[32,2048]{1,0:T(8,128)(2,1)S(1)} %copy-done.4), channel_id=1, source_target_pairs={{0,5},{1,4},{2,7},{3,6},{4,1},{5,0},{6,3},{7,2},{8,13},{9,12},{10,... | collective-permute-start | bytes 393224 | tf_op jit(solution)/shard_map/ppermute | solution.py:244
  56.6 8.5 %collective-permute-start.15 = (bf16[16,2816]{1,0:T(8,128)(2,1)}, bf16[16,2816]{1,0:T(8,128)(2,1)S(1)}, u32[]{:S(2)}, u32[]{:S(2)}) collective-permute-start(bf16[16,2816]{1,0:T(8,128)(2,1)} %get-tuple-element.59), channel_id=1, source_target_pairs={{0,5},{1,4},{2,7},{3,6},{4,1},{5,0},{6,3},{7,2},{8,13},{9,12},{10,... | collective-permute-start | bytes 270344 | tf_op jit(solution)/shard_map/ppermute | solution.py:244
  65.2 5.8 %collective-permute-start.16 = (bf16[32,2048]{1,0:T(8,128)(2,1)S(1)}, bf16[32,2048]{1,0:T(8,128)(2,1)S(1)}, u32[]{:S(2)}, u32[]{:S(2)}) collective-permute-start(bf16[32,2048]{1,0:T(8,128)(2,1)S(1)} %copy-done.3), channel_id=1, source_target_pairs={{0,4},{1,5},{2,6},{3,7},{4,0},{5,1},{6,2},{7,3},{8,12},{9,13},{10,... | collective-permute-start | bytes 393224 | tf_op jit(solution)/shard_map/ppermute | solution.py:244
  72.0 7.8 %collective-permute-done.15.refs_1_.refs_3_ = bf16[16,2816]{1,0:T(8,128)(2,1)S(1)} collective-permute-done((bf16[16,2816]{1,0:T(8,128)(2,1)}, bf16[16,2816]{1,0:T(8,128)(2,1)S(1)}, u32[]{:S(2)}, u32[]{:S(2)}) %collective-permute-start.15) | collective-permute-done | bytes 90144 | tf_op jit(solution)/shard_map/ppermute | solution.py:244
  79.9 4.7 %collective-permute-done.17.refs_3_ = bf16[16,2816]{1,0:T(8,128)(2,1)S(1)} collective-permute-done((bf16[16,2816]{1,0:T(8,128)(2,1)}, bf16[16,2816]{1,0:T(8,128)(2,1)S(1)}, u32[]{:S(2)}, u32[]{:S(2)}) %collective-permute-start.17) | collective-permute-done | bytes 90144 | tf_op jit(solution)/shard_map/ppermute | solution.py:244
  85.7 2.9 %collective-permute-start.18 = (f16[64,256]{1,0:T(8,128)(2,1)S(1)}, f16[64,256]{1,0:T(8,128)(2,1)S(1)}, u32[]{:S(2)}, u32[]{:S(2)}) collective-permute-start(f16[64,256]{1,0:T(8,128)(2,1)S(1)} %concatenate.112), channel_id=1, source_target_pairs={{0,4},{1,5},{2,6},{3,7},{4,0},{5,1},{6,2},{7,3},{8,12},{9,13},{10,... | collective-permute-start | bytes 98312 | tf_op jit(solution)/shard_map/ppermute | solution.py:244
  88.8 2.4 %collective-permute-start.13 = (f16[64,256]{1,0:T(8,128)(2,1)S(1)}, f16[64,256]{1,0:T(8,128)(2,1)S(1)}, u32[]{:S(2)}, u32[]{:S(2)}) collective-permute-start(f16[64,256]{1,0:T(8,128)(2,1)S(1)} %pad_maximum_fusion.20), channel_id=1, source_target_pairs={{0,7},{1,6},{2,5},{3,4},{4,3},{5,2},{6,1},{7,0},{8,15},{9,14},{10,... | collective-permute-start | bytes 98312 | tf_op jit(solution)/shard_map/ppermute | solution.py:244
  91.2 2.5 %collective-permute-start.12 = (f16[64,256]{1,0:T(8,128)(2,1)S(1)}, f16[64,256]{1,0:T(8,128)(2,1)S(1)}, u32[]{:S(2)}, u32[]{:S(2)}) collective-permute-start(f16[64,256]{1,0:T(8,128)(2,1)S(1)} %concatenate.111), channel_id=1, source_target_pairs={{0,6},{1,7},{2,4},{3,5},{4,2},{5,3},{6,0},{7,1},{8,14},{9,15},{10,... | collective-permute-start | bytes 98312 | tf_op jit(solution)/shard_map/ppermute | solution.py:244
  93.7 2.0 %collective-permute-start.6 = (f16[64,256]{1,0:T(8,128)(2,1)S(1)}, f16[64,256]{1,0:T(8,128)(2,1)S(1)}, u32[]{:S(2)}, u32[]{:S(2)}) collective-permute-start(f16[64,256]{1,0:T(8,128)(2,1)S(1)} %get-tuple-element.46), channel_id=1, source_target_pairs={{0,2},{1,3},{2,0},{3,1},{4,6},{5,7},{6,4},{7,5},{8,10},{9,11},{10,... | collective-permute-start | bytes 98312 | tf_op jit(solution)/shard_map/ppermute | solution.py:244
  95.6 1.5 collective-permute-start.5
  97.2 1.2 collective-permute-done.7
  99.7 1.4 collective-permute-start.22
  101.3 2.9 %collective-permute-start.20 = (bf16[48,256]{1,0:T(8,128)(2,1)S(1)}, bf16[48,256]{1,0:T(8,128)(2,1)S(1)}, u32[]{:S(2)}, u32[]{:S(2)}) collective-permute-start(bf16[48,256]{1,0:T(8,128)(2,1)S(1)} %get-tuple-element.84), channel_id=1, source_target_pairs={{0,2},{1,3},{2,0},{3,1},{4,6},{5,7},{6,4},{7,5},{8,10},{9,11},{10,... | collective-permute-start | bytes 73736 | tf_op jit(solution)/shard_map/ppermute | solution.py:244
  104.2 1.2 collective-permute-done.22
  106.2 1.6 collective-permute-start.23
  108.4 2.5 %collective-permute-done.23.refs_2_ = bf16[192,256]{1,0:T(8,128)(2,1)S(1)} collective-permute-done((bf16[192,256]{1,0:T(8,128)(2,1)S(1)}, bf16[192,256]{1,0:T(8,128)(2,1)S(1)}, u32[]{:S(2)}, u32[]{:S(2)}) %collective-permute-start.23) | collective-permute-done | bytes 98336 | tf_op jit(solution)/shard_map/ppermute | solution.py:244
  113.7 1.5 collective-permute-start.27
  115.4 1.8 %collective-permute-done.27 = f32[128]{0:T(128)S(1)} collective-permute-done((f32[128]{0:T(128)S(1)}, f32[128]{0:T(128)S(1)}, u32[]{:S(2)}, u32[]{:S(2)}) %collective-permute-start.27) | collective-permute-done | bytes 544 | tf_op jit(solution)/shard_map/ppermute | solution.py:247
  117.7 1.6 collective-permute-start.26
  120.3 6.6 %collective-permute-done.26 = f16[128,1024]{1,0:T(8,128)(2,1)S(1)} collective-permute-done((f16[128,1024]{1,0:T(8,128)(2,1)S(1)}, f16[128,1024]{1,0:T(8,128)(2,1)S(1)}, u32[]{:S(2)}, u32[]{:S(2)}) %collective-permute-start.26) | collective-permute-done | bytes 262176 | tf_op jit(solution)/shard_map/ppermute | solution.py:247
  127.3 3.7 %collective-permute-done.30 = f16[128,1024]{1,0:T(8,128)(2,1)S(1)} collective-permute-done((f16[128,1024]{1,0:T(8,128)(2,1)S(1)}, f16[128,1024]{1,0:T(8,128)(2,1)S(1)}, u32[]{:S(2)}, u32[]{:S(2)}) %collective-permute-start.30) | collective-permute-done | bytes 262176 | tf_op jit(solution)/shard_map/ppermute | solution.py:247
  131.3 1.5 collective-permute-done.31.refs_6_
  133.6 1.6 collective-permute-start.32
  136.1 2.6 %collective-permute-done.32 = f16[208,256]{1,0:T(8,128)(2,1)S(1)} collective-permute-done((f16[208,256]{1,0:T(8,128)(2,1)S(1)}, f16[208,256]{1,0:T(8,128)(2,1)S(1)}, u32[]{:S(2)}, u32[]{:S(2)}) %collective-permute-start.32) | collective-permute-done | bytes 106528 | tf_op jit(solution)/shard_map/ppermute | solution.py:244
  138.8 2.2 %collective-permute-start.35 = (f16[64,256]{1,0:T(8,128)(2,1)S(1)}, f16[64,256]{1,0:T(8,128)(2,1)S(1)}, u32[]{:S(2)}, u32[]{:S(2)}) collective-permute-start(f16[64,256]{1,0:T(8,128)(2,1)S(1)} %concatenate.113), channel_id=1, source_target_pairs={{0,6},{1,7},{2,4},{3,5},{4,2},{5,3},{6,0},{7,1},{8,14},{9,15},{10,... | collective-permute-start | bytes 98312 | tf_op jit(solution)/shard_map/ppermute | solution.py:244
  141.0 1.2 collective-permute-start.34
  142.2 1.1 collective-permute-start.33
  143.4 1.3 collective-permute-done.35
  144.6 1.3 collective-permute-done.34
  146.3 1.6 collective-permute-start.38
  148.9 1.9 %collective-permute-start.36 = (bf16[48,256]{1,0:T(8,128)(2,1)S(1)}, bf16[48,256]{1,0:T(8,128)(2,1)S(1)}, u32[]{:S(2)}, u32[]{:S(2)}) collective-permute-start(bf16[48,256]{1,0:T(8,128)(2,1)S(1)} %get-tuple-element.74), channel_id=1, source_target_pairs={{0,2},{1,3},{2,0},{3,1},{4,6},{5,7},{6,4},{7,5},{8,10},{9,11},{10,... | collective-permute-start | bytes 73736 | tf_op jit(solution)/shard_map/ppermute | solution.py:244
  153.0 1.6 collective-permute-start.39
  155.2 2.5 %collective-permute-done.39 = bf16[192,256]{1,0:T(8,128)(2,1)S(1)} collective-permute-done((bf16[192,256]{1,0:T(8,128)(2,1)S(1)}, bf16[192,256]{1,0:T(8,128)(2,1)S(1)}, u32[]{:S(2)}, u32[]{:S(2)}) %collective-permute-start.39) | collective-permute-done | bytes 98336 | tf_op jit(solution)/shard_map/ppermute | solution.py:244
  161.3 1.5 collective-permute-start.45
  163.0 1.8 %collective-permute-done.45 = f32[64]{0:T(128)S(1)} collective-permute-done((f32[64]{0:T(128)S(1)}, f32[64]{0:T(128)S(1)}, u32[]{:S(2)}, u32[]{:S(2)}) %collective-permute-start.45) | collective-permute-done | bytes 288 | tf_op jit(solution)/shard_map/ppermute | solution.py:247
  165.2 1.6 collective-permute-start.44
  167.8 3.6 %collective-permute-done.44 = f16[64,1024]{1,0:T(8,128)(2,1)S(1)} collective-permute-done((f16[64,1024]{1,0:T(8,128)(2,1)S(1)}, f16[64,1024]{1,0:T(8,128)(2,1)S(1)}, u32[]{:S(2)}, u32[]{:S(2)}) %collective-permute-start.44) | collective-permute-done | bytes 131104 | tf_op jit(solution)/shard_map/ppermute | solution.py:247
  171.5 1.3 collective-permute-done.43
  (155 shorter events, 26.7 us)
Async XLA Ops:
  0.6 15.2 %collective-permute-start.3 = (f32[64,2048]{1,0:T(8,128)}, f32[64,2048]{1,0:T(8,128)S(1)}, u32[]{:S(2)}, u32[]{:S(2)}) collective-permute-start(f32[64,2048]{1,0:T(8,128)} %param.9), channel_id=1, source_target_pairs={{0,16},{8,24},{16,0},{24,8},{1,17},{9,25},{17,1},{25,9},{2,18},{10... | collective-permute-start | bytes 1572872 | tf_op jit(solution)/shard_map/ppermute | solution.py:247
  15.9 35.5 %collective-permute-start.4 = (bf16[128,2048]{1,0:T(8,128)(2,1)S(1)}, bf16[128,2048]{1,0:T(8,128)(2,1)S(1)}, u32[]{:S(2)}, u32[]{:S(2)}) collective-permute-start(bf16[128,2048]{1,0:T(8,128)(2,1)S(1)} %convert_element_type.137.refs_4_), channel_id=1, source_target_pairs={{0,8},{8,0},{16,24},{24,16},{1,9},{9,1},{17,25},{25,17},{2,10},{10... | collective-permute-start | bytes 1572872 | tf_op jit(solution)/shard_map/ppermute | solution.py:247
  26.1 39.0 %copy-start.3 = (bf16[32,2048]{1,0:T(8,128)(2,1)S(1)}, bf16[32,2048]{1,0:T(8,128)(2,1)}, u32[]{:S(2)}) copy-start(bf16[32,2048]{1,0:T(8,128)(2,1)} %get-tuple-element.60) | copy-start | bytes 393220
  32.9 8.3 %collective-permute-start = (bf16[48,2304]{1,0:T(8,128)(2,1)}, bf16[48,2304]{1,0:T(8,128)(2,1)S(1)}, u32[]{:S(2)}, u32[]{:S(2)}) collective-permute-start(bf16[48,2304]{1,0:T(8,128)(2,1)} %get-tuple-element.42), channel_id=1, source_target_pairs={{0,1},{1,0},{2,3},{3,2},{4,5},{5,4},{6,7},{7,6},{8,9},{9,8},{10,11... | collective-permute-start | bytes 663560 | tf_op jit(solution)/shard_map/ppermute | solution.py:244
  34.7 11.1 %collective-permute-start.1 = (bf16[48,2304]{1,0:T(8,128)(2,1)}, bf16[48,2304]{1,0:T(8,128)(2,1)S(1)}, u32[]{:S(2)}, u32[]{:S(2)}) collective-permute-start(bf16[48,2304]{1,0:T(8,128)(2,1)} %get-tuple-element.43), channel_id=1, source_target_pairs={{0,2},{1,3},{2,0},{3,1},{4,6},{5,7},{6,4},{7,5},{8,10},{9,11},{10,... | collective-permute-start | bytes 663560 | tf_op jit(solution)/shard_map/ppermute | solution.py:244
  36.3 11.1 %collective-permute-start.2 = (bf16[48,2304]{1,0:T(8,128)(2,1)}, bf16[48,2304]{1,0:T(8,128)(2,1)S(1)}, u32[]{:S(2)}, u32[]{:S(2)}) collective-permute-start(bf16[48,2304]{1,0:T(8,128)(2,1)} %get-tuple-element.44), channel_id=1, source_target_pairs={{0,3},{1,2},{2,1},{3,0},{4,7},{5,6},{6,5},{7,4},{8,11},{9,10},{10,... | collective-permute-start | bytes 663560 | tf_op jit(solution)/shard_map/ppermute | solution.py:244
  36.4 34.5 %collective-permute-start.8 = (bf16[32,2048]{1,0:T(8,128)(2,1)S(1)}, bf16[32,2048]{1,0:T(8,128)(2,1)S(1)}, u32[]{:S(2)}, u32[]{:S(2)}) collective-permute-start(bf16[32,2048]{1,0:T(8,128)(2,1)S(1)} %copy-done.6), channel_id=1, source_target_pairs={{0,7},{1,6},{2,5},{3,4},{4,3},{5,2},{6,1},{7,0},{8,15},{9,14},{10,... | collective-permute-start | bytes 393224 | tf_op jit(solution)/shard_map/ppermute | solution.py:244
  41.2 15.4 %collective-permute-start.9 = (bf16[16,2816]{1,0:T(8,128)(2,1)}, bf16[16,2816]{1,0:T(8,128)(2,1)S(1)}, u32[]{:S(2)}, u32[]{:S(2)}) collective-permute-start(bf16[16,2816]{1,0:T(8,128)(2,1)} %get-tuple-element.51), channel_id=1, source_target_pairs={{0,7},{1,6},{2,5},{3,4},{4,3},{5,2},{6,1},{7,0},{8,15},{9,14},{10,... | collective-permute-start | bytes 270344 | tf_op jit(solution)/shard_map/ppermute | solution.py:244
  45.8 25.2 %collective-permute-start.10 = (bf16[32,2048]{1,0:T(8,128)(2,1)S(1)}, bf16[32,2048]{1,0:T(8,128)(2,1)S(1)}, u32[]{:S(2)}, u32[]{:S(2)}) collective-permute-start(bf16[32,2048]{1,0:T(8,128)(2,1)S(1)} %copy-done.5), channel_id=1, source_target_pairs={{0,6},{1,7},{2,4},{3,5},{4,2},{5,3},{6,0},{7,1},{8,14},{9,15},{10,... | collective-permute-start | bytes 393224 | tf_op jit(solution)/shard_map/ppermute | solution.py:244
  47.4 17.7 %collective-permute-start.11 = (bf16[16,2816]{1,0:T(8,128)(2,1)}, bf16[16,2816]{1,0:T(8,128)(2,1)S(1)}, u32[]{:S(2)}, u32[]{:S(2)}) collective-permute-start(bf16[16,2816]{1,0:T(8,128)(2,1)} %get-tuple-element.53), channel_id=1, source_target_pairs={{0,6},{1,7},{2,4},{3,5},{4,2},{5,3},{6,0},{7,1},{8,14},{9,15},{10,... | collective-permute-start | bytes 270344 | tf_op jit(solution)/shard_map/ppermute | solution.py:244
  51.5 33.1 %collective-permute-start.14 = (bf16[32,2048]{1,0:T(8,128)(2,1)S(1)}, bf16[32,2048]{1,0:T(8,128)(2,1)S(1)}, u32[]{:S(2)}, u32[]{:S(2)}) collective-permute-start(bf16[32,2048]{1,0:T(8,128)(2,1)S(1)} %copy-done.4), channel_id=1, source_target_pairs={{0,5},{1,4},{2,7},{3,6},{4,1},{5,0},{6,3},{7,2},{8,13},{9,12},{10,... | collective-permute-start | bytes 393224 | tf_op jit(solution)/shard_map/ppermute | solution.py:244
  55.7 33.0 %copy-start.1 = (bf16[48,2304]{1,0:T(8,128)(2,1)S(1)}, bf16[48,2304]{1,0:T(8,128)(2,1)}, u32[]{:S(2)}) copy-start(bf16[48,2304]{1,0:T(8,128)(2,1)} %get-tuple-element.41.refs_0_) | copy-start | bytes 663556
  56.6 23.3 %collective-permute-start.15 = (bf16[16,2816]{1,0:T(8,128)(2,1)}, bf16[16,2816]{1,0:T(8,128)(2,1)S(1)}, u32[]{:S(2)}, u32[]{:S(2)}) collective-permute-start(bf16[16,2816]{1,0:T(8,128)(2,1)} %get-tuple-element.59), channel_id=1, source_target_pairs={{0,5},{1,4},{2,7},{3,6},{4,1},{5,0},{6,3},{7,2},{8,13},{9,12},{10,... | collective-permute-start | bytes 270344 | tf_op jit(solution)/shard_map/ppermute | solution.py:244
  65.2 19.5 %collective-permute-start.16 = (bf16[32,2048]{1,0:T(8,128)(2,1)S(1)}, bf16[32,2048]{1,0:T(8,128)(2,1)S(1)}, u32[]{:S(2)}, u32[]{:S(2)}) collective-permute-start(bf16[32,2048]{1,0:T(8,128)(2,1)S(1)} %copy-done.3), channel_id=1, source_target_pairs={{0,4},{1,5},{2,6},{3,7},{4,0},{5,1},{6,2},{7,3},{8,12},{9,13},{10,... | collective-permute-start | bytes 393224 | tf_op jit(solution)/shard_map/ppermute | solution.py:244
  70.9 13.7 %collective-permute-start.17 = (bf16[16,2816]{1,0:T(8,128)(2,1)}, bf16[16,2816]{1,0:T(8,128)(2,1)S(1)}, u32[]{:S(2)}, u32[]{:S(2)}) collective-permute-start(bf16[16,2816]{1,0:T(8,128)(2,1)} %get-tuple-element.61), channel_id=1, source_target_pairs={{0,4},{1,5},{2,6},{3,7},{4,0},{5,1},{6,2},{7,3},{8,12},{9,13},{10,... | collective-permute-start | bytes 270344 | tf_op jit(solution)/shard_map/ppermute | solution.py:244
  85.7 8.0 %collective-permute-start.19 = (f16[64,256]{1,0:T(8,128)(2,1)S(1)}, f16[64,256]{1,0:T(8,128)(2,1)S(1)}, u32[]{:S(2)}, u32[]{:S(2)}) collective-permute-start(f16[64,256]{1,0:T(8,128)(2,1)S(1)} %pad_maximum_fusion.21), channel_id=1, source_target_pairs={{0,5},{1,4},{2,7},{3,6},{4,1},{5,0},{6,3},{7,2},{8,13},{9,12},{10,... | collective-permute-start | bytes 98312 | tf_op jit(solution)/shard_map/ppermute | solution.py:244
  85.7 9.9 %collective-permute-start.18 = (f16[64,256]{1,0:T(8,128)(2,1)S(1)}, f16[64,256]{1,0:T(8,128)(2,1)S(1)}, u32[]{:S(2)}, u32[]{:S(2)}) collective-permute-start(f16[64,256]{1,0:T(8,128)(2,1)S(1)} %concatenate.112), channel_id=1, source_target_pairs={{0,4},{1,5},{2,6},{3,7},{4,0},{5,1},{6,2},{7,3},{8,12},{9,13},{10,... | collective-permute-start | bytes 98312 | tf_op jit(solution)/shard_map/ppermute | solution.py:244
  88.8 8.4 %collective-permute-start.13 = (f16[64,256]{1,0:T(8,128)(2,1)S(1)}, f16[64,256]{1,0:T(8,128)(2,1)S(1)}, u32[]{:S(2)}, u32[]{:S(2)}) collective-permute-start(f16[64,256]{1,0:T(8,128)(2,1)S(1)} %pad_maximum_fusion.20), channel_id=1, source_target_pairs={{0,7},{1,6},{2,5},{3,4},{4,3},{5,2},{6,1},{7,0},{8,15},{9,14},{10,... | collective-permute-start | bytes 98312 | tf_op jit(solution)/shard_map/ppermute | solution.py:244
  91.2 6.0 %collective-permute-start.12 = (f16[64,256]{1,0:T(8,128)(2,1)S(1)}, f16[64,256]{1,0:T(8,128)(2,1)S(1)}, u32[]{:S(2)}, u32[]{:S(2)}) collective-permute-start(f16[64,256]{1,0:T(8,128)(2,1)S(1)} %concatenate.111), channel_id=1, source_target_pairs={{0,6},{1,7},{2,4},{3,5},{4,2},{5,3},{6,0},{7,1},{8,14},{9,15},{10,... | collective-permute-start | bytes 98312 | tf_op jit(solution)/shard_map/ppermute | solution.py:244
  93.7 4.8 %collective-permute-start.7 = (f16[64,256]{1,0:T(8,128)(2,1)S(1)}, f16[64,256]{1,0:T(8,128)(2,1)S(1)}, u32[]{:S(2)}, u32[]{:S(2)}) collective-permute-start(f16[64,256]{1,0:T(8,128)(2,1)S(1)} %concatenate.110), channel_id=1, source_target_pairs={{0,3},{1,2},{2,1},{3,0},{4,7},{5,6},{6,5},{7,4},{8,11},{9,10},{10,... | collective-permute-start | bytes 98312 | tf_op jit(solution)/shard_map/ppermute | solution.py:244
  93.7 4.8 %collective-permute-start.6 = (f16[64,256]{1,0:T(8,128)(2,1)S(1)}, f16[64,256]{1,0:T(8,128)(2,1)S(1)}, u32[]{:S(2)}, u32[]{:S(2)}) collective-permute-start(f16[64,256]{1,0:T(8,128)(2,1)S(1)} %get-tuple-element.46), channel_id=1, source_target_pairs={{0,2},{1,3},{2,0},{3,1},{4,6},{5,7},{6,4},{7,5},{8,10},{9,11},{10,... | collective-permute-start | bytes 98312 | tf_op jit(solution)/shard_map/ppermute | solution.py:244
  95.6 3.9 %collective-permute-start.5 = (f16[64,256]{1,0:T(8,128)(2,1)S(1)}, f16[64,256]{1,0:T(8,128)(2,1)S(1)}, u32[]{:S(2)}, u32[]{:S(2)}) collective-permute-start(f16[64,256]{1,0:T(8,128)(2,1)S(1)} %get-tuple-element.45), channel_id=1, source_target_pairs={{0,1},{1,0},{2,3},{3,2},{4,5},{5,4},{6,7},{7,6},{8,9},{9,8},{10,11... | collective-permute-start | bytes 98312 | tf_op jit(solution)/shard_map/ppermute | solution.py:244
  99.7 5.7 %collective-permute-start.22 = (bf16[48,256]{1,0:T(8,128)(2,1)S(1)}, bf16[48,256]{1,0:T(8,128)(2,1)S(1)}, u32[]{:S(2)}, u32[]{:S(2)}) collective-permute-start(bf16[48,256]{1,0:T(8,128)(2,1)S(1)} %get-tuple-element.84), channel_id=1, source_target_pairs={{0,6},{1,7},{2,4},{3,5},{4,2},{5,3},{6,0},{7,1},{8,14},{9,15},{10,... | collective-permute-start | bytes 73736 | tf_op jit(solution)/shard_map/ppermute | solution.py:244
  101.1 4.8 %collective-permute-start.21 = (bf16[48,256]{1,0:T(8,128)(2,1)S(1)}, bf16[48,256]{1,0:T(8,128)(2,1)S(1)}, u32[]{:S(2)}, u32[]{:S(2)}) collective-permute-start(bf16[48,256]{1,0:T(8,128)(2,1)S(1)} %get-tuple-element.84), channel_id=1, source_target_pairs={{0,4},{1,5},{2,6},{3,7},{4,0},{5,1},{6,2},{7,3},{8,12},{9,13},{10,... | collective-permute-start | bytes 73736 | tf_op jit(solution)/shard_map/ppermute | solution.py:244
  101.3 4.9 %collective-permute-start.20 = (bf16[48,256]{1,0:T(8,128)(2,1)S(1)}, bf16[48,256]{1,0:T(8,128)(2,1)S(1)}, u32[]{:S(2)}, u32[]{:S(2)}) collective-permute-start(bf16[48,256]{1,0:T(8,128)(2,1)S(1)} %get-tuple-element.84), channel_id=1, source_target_pairs={{0,2},{1,3},{2,0},{3,1},{4,6},{5,7},{6,4},{7,5},{8,10},{9,11},{10,... | collective-permute-start | bytes 73736 | tf_op jit(solution)/shard_map/ppermute | solution.py:244
  106.2 4.7 %collective-permute-start.23 = (bf16[192,256]{1,0:T(8,128)(2,1)S(1)}, bf16[192,256]{1,0:T(8,128)(2,1)S(1)}, u32[]{:S(2)}, u32[]{:S(2)}) collective-permute-start(bf16[192,256]{1,0:T(8,128)(2,1)S(1)} %get-tuple-element.83.refs_2_), channel_id=1, source_target_pairs={{0,1},{1,0},{2,3},{3,2},{4,5},{5,4},{6,7},{7,6},{8,9},{9,8},{10,11... | collective-permute-start | bytes 294920 | tf_op jit(solution)/shard_map/ppermute | solution.py:244
  111.0 2.6 %collective-permute-start.25 = (f32[128]{0:T(128)S(1)}, f32[128]{0:T(128)S(1)}, u32[]{:S(2)}, u32[]{:S(2)}) collective-permute-start(f32[128]{0:T(128)S(1)} %slice.262), channel_id=1, source_target_pairs={{0,8},{8,0},{16,24},{24,16},{1,9},{9,1},{17,25},{25,17},{2,10},{10... | collective-permute-start | bytes 1544 | tf_op jit(solution)/shard_map/ppermute | solution.py:247
  111.8 5.4 %collective-permute-start.24 = (f32[128,1024]{1,0:T(8,128)S(1)}, f32[128,1024]{1,0:T(8,128)S(1)}, u32[]{:S(2)}, u32[]{:S(2)}) collective-permute-start(f32[128,1024]{1,0:T(8,128)S(1)} %convolution_add_fusion.6), channel_id=1, source_target_pairs={{0,8},{8,0},{16,24},{24,16},{1,9},{9,1},{17,25},{25,17},{2,10},{10... | collective-permute-start | bytes 1572872 | tf_op jit(solution)/shard_map/ppermute | solution.py:247
  113.4 5.8 %collective-permute-start.29 = (f32[128,1024]{1,0:T(8,128)S(1)}, f32[128,1024]{1,0:T(8,128)S(1)}, u32[]{:S(2)}, u32[]{:S(2)}) collective-permute-start(f32[128,1024]{1,0:T(8,128)S(1)} %convolution_add_fusion.4), channel_id=1, source_target_pairs={{0,8},{8,0},{16,24},{24,16},{1,9},{9,1},{17,25},{25,17},{2,10},{10... | collective-permute-start | bytes 1572872 | tf_op jit(solution)/shard_map/ppermute | solution.py:247
  113.7 3.6 %collective-permute-start.27 = (f32[128]{0:T(128)S(1)}, f32[128]{0:T(128)S(1)}, u32[]{:S(2)}, u32[]{:S(2)}) collective-permute-start(f32[128]{0:T(128)S(1)} %pad_maximum_fusion.22), channel_id=1, source_target_pairs={{0,16},{8,24},{16,0},{24,8},{1,17},{9,25},{17,1},{25,9},{2,18},{10... | collective-permute-start | bytes 1544 | tf_op jit(solution)/shard_map/ppermute | solution.py:247
  117.7 9.2 %collective-permute-start.26 = (f16[128,1024]{1,0:T(8,128)(2,1)S(1)}, f16[128,1024]{1,0:T(8,128)(2,1)S(1)}, u32[]{:S(2)}, u32[]{:S(2)}) collective-permute-start(f16[128,1024]{1,0:T(8,128)(2,1)S(1)} %fusion.15), channel_id=1, source_target_pairs={{0,16},{8,24},{16,0},{24,8},{1,17},{9,25},{17,1},{25,9},{2,18},{10... | collective-permute-start | bytes 786440 | tf_op jit(solution)/shard_map/ppermute | solution.py:247
  119.7 11.2 %collective-permute-start.30 = (f16[128,1024]{1,0:T(8,128)(2,1)S(1)}, f16[128,1024]{1,0:T(8,128)(2,1)S(1)}, u32[]{:S(2)}, u32[]{:S(2)}) collective-permute-start(f16[128,1024]{1,0:T(8,128)(2,1)S(1)} %fusion.17), channel_id=1, source_target_pairs={{0,16},{8,24},{16,0},{24,8},{1,17},{9,25},{17,1},{25,9},{2,18},{10... | collective-permute-start | bytes 786440 | tf_op jit(solution)/shard_map/ppermute | solution.py:247
  127.2 4.1 %collective-permute-start.28 = (bf16[128,1024]{1,0:T(8,128)(2,1)S(1)}, bf16[128,1024]{1,0:T(8,128)(2,1)S(1)}, u32[]{:S(2)}, u32[]{:S(2)}) collective-permute-start(bf16[128,1024]{1,0:T(8,128)(2,1)S(1)} %get-tuple-element.80.refs_3_), channel_id=1, source_target_pairs={{0,8},{8,0},{16,24},{24,16},{1,9},{9,1},{17,25},{25,17},{2,10},{10... | collective-permute-start | bytes 786440 | tf_op jit(solution)/shard_map/ppermute | solution.py:247
  131.2 1.6 collective-permute-start.31
  133.6 5.1 %collective-permute-start.32 = (f16[208,256]{1,0:T(8,128)(2,1)S(1)}, f16[208,256]{1,0:T(8,128)(2,1)S(1)}, u32[]{:S(2)}, u32[]{:S(2)}) collective-permute-start(f16[208,256]{1,0:T(8,128)(2,1)S(1)} %convert_element_type.162), channel_id=1, source_target_pairs={{0,1},{1,0},{2,3},{3,2},{4,5},{5,4},{6,7},{7,6},{8,9},{9,8},{10,11... | collective-permute-start | bytes 319496 | tf_op jit(solution)/shard_map/ppermute | solution.py:244
  138.8 5.8 %collective-permute-start.35 = (f16[64,256]{1,0:T(8,128)(2,1)S(1)}, f16[64,256]{1,0:T(8,128)(2,1)S(1)}, u32[]{:S(2)}, u32[]{:S(2)}) collective-permute-start(f16[64,256]{1,0:T(8,128)(2,1)S(1)} %concatenate.113), channel_id=1, source_target_pairs={{0,6},{1,7},{2,4},{3,5},{4,2},{5,3},{6,0},{7,1},{8,14},{9,15},{10,... | collective-permute-start | bytes 98312 | tf_op jit(solution)/shard_map/ppermute | solution.py:244
  141.0 4.9 %collective-permute-start.34 = (f16[64,256]{1,0:T(8,128)(2,1)S(1)}, f16[64,256]{1,0:T(8,128)(2,1)S(1)}, u32[]{:S(2)}, u32[]{:S(2)}) collective-permute-start(f16[64,256]{1,0:T(8,128)(2,1)S(1)} %get-tuple-element.111), channel_id=1, source_target_pairs={{0,4},{1,5},{2,6},{3,7},{4,0},{5,1},{6,2},{7,3},{8,12},{9,13},{10,... | collective-permute-start | bytes 98312 | tf_op jit(solution)/shard_map/ppermute | solution.py:244
  142.2 4.0 %collective-permute-start.33 = (f16[64,256]{1,0:T(8,128)(2,1)S(1)}, f16[64,256]{1,0:T(8,128)(2,1)S(1)}, u32[]{:S(2)}, u32[]{:S(2)}) collective-permute-start(f16[64,256]{1,0:T(8,128)(2,1)S(1)} %get-tuple-element.110), channel_id=1, source_target_pairs={{0,2},{1,3},{2,0},{3,1},{4,6},{5,7},{6,4},{7,5},{8,10},{9,11},{10,... | collective-permute-start | bytes 98312 | tf_op jit(solution)/shard_map/ppermute | solution.py:244
  146.3 5.7 %collective-permute-start.38 = (bf16[48,256]{1,0:T(8,128)(2,1)S(1)}, bf16[48,256]{1,0:T(8,128)(2,1)S(1)}, u32[]{:S(2)}, u32[]{:S(2)}) collective-permute-start(bf16[48,256]{1,0:T(8,128)(2,1)S(1)} %get-tuple-element.74), channel_id=1, source_target_pairs={{0,6},{1,7},{2,4},{3,5},{4,2},{5,3},{6,0},{7,1},{8,14},{9,15},{10,... | collective-permute-start | bytes 73736 | tf_op jit(solution)/shard_map/ppermute | solution.py:244
  148.0 5.0 %collective-permute-start.37 = (bf16[48,256]{1,0:T(8,128)(2,1)S(1)}, bf16[48,256]{1,0:T(8,128)(2,1)S(1)}, u32[]{:S(2)}, u32[]{:S(2)}) collective-permute-start(bf16[48,256]{1,0:T(8,128)(2,1)S(1)} %get-tuple-element.74), channel_id=1, source_target_pairs={{0,4},{1,5},{2,6},{3,7},{4,0},{5,1},{6,2},{7,3},{8,12},{9,13},{10,... | collective-permute-start | bytes 73736 | tf_op jit(solution)/shard_map/ppermute | solution.py:244
  148.9 4.1 %collective-permute-start.36 = (bf16[48,256]{1,0:T(8,128)(2,1)S(1)}, bf16[48,256]{1,0:T(8,128)(2,1)S(1)}, u32[]{:S(2)}, u32[]{:S(2)}) collective-permute-start(bf16[48,256]{1,0:T(8,128)(2,1)S(1)} %get-tuple-element.74), channel_id=1, source_target_pairs={{0,2},{1,3},{2,0},{3,1},{4,6},{5,7},{6,4},{7,5},{8,10},{9,11},{10,... | collective-permute-start | bytes 73736 | tf_op jit(solution)/shard_map/ppermute | solution.py:244
  153.0 4.7 %collective-permute-start.39 = (bf16[192,256]{1,0:T(8,128)(2,1)S(1)}, bf16[192,256]{1,0:T(8,128)(2,1)S(1)}, u32[]{:S(2)}, u32[]{:S(2)}) collective-permute-start(bf16[192,256]{1,0:T(8,128)(2,1)S(1)} %get-tuple-element.73), channel_id=1, source_target_pairs={{0,1},{1,0},{2,3},{3,2},{4,5},{5,4},{6,7},{7,6},{8,9},{9,8},{10,11... | collective-permute-start | bytes 294920 | tf_op jit(solution)/shard_map/ppermute | solution.py:244
  159.2 5.6 %collective-permute-start.41 = (f32[128,1024]{1,0:T(8,128)S(1)}, f32[128,1024]{1,0:T(8,128)S(1)}, u32[]{:S(2)}, u32[]{:S(2)}) collective-permute-start(f32[128,1024]{1,0:T(8,128)S(1)} %convolution_add_fusion.2), channel_id=1, source_target_pairs={{0,8},{8,0},{16,24},{24,16},{1,9},{9,1},{17,25},{25,17},{2,10},{10... | collective-permute-start | bytes 1572872 | tf_op jit(solution)/shard_map/ppermute | solution.py:247
  159.4 1.8 %collective-permute-start.42 = (f32[128]{0:T(128)S(1)}, f32[128]{0:T(128)S(1)}, u32[]{:S(2)}, u32[]{:S(2)}) collective-permute-start(f32[128]{0:T(128)S(1)} %slice.293), channel_id=1, source_target_pairs={{0,8},{8,0},{16,24},{24,16},{1,9},{9,1},{17,25},{25,17},{2,10},{10... | collective-permute-start | bytes 1544 | tf_op jit(solution)/shard_map/ppermute | solution.py:247
  160.2 6.6 %collective-permute-start.40 = (f32[128,1024]{1,0:T(8,128)S(1)}, f32[128,1024]{1,0:T(8,128)S(1)}, u32[]{:S(2)}, u32[]{:S(2)}) collective-permute-start(f32[128,1024]{1,0:T(8,128)S(1)} %convolution_add_fusion.1), channel_id=1, source_target_pairs={{0,8},{8,0},{16,24},{24,16},{1,9},{9,1},{17,25},{25,17},{2,10},{10... | collective-permute-start | bytes 1572872 | tf_op jit(solution)/shard_map/ppermute | solution.py:247
  161.3 3.6 %collective-permute-start.45 = (f32[64]{0:T(128)S(1)}, f32[64]{0:T(128)S(1)}, u32[]{:S(2)}, u32[]{:S(2)}) collective-permute-start(f32[64]{0:T(128)S(1)} %slice.294), channel_id=1, source_target_pairs={{0,16},{8,24},{16,0},{24,8},{1,17},{9,25},{17,1},{25,9},{2,18},{10... | collective-permute-start | bytes 776 | tf_op jit(solution)/shard_map/ppermute | solution.py:247
  165.2 6.1 %collective-permute-start.44 = (f16[64,1024]{1,0:T(8,128)(2,1)S(1)}, f16[64,1024]{1,0:T(8,128)(2,1)S(1)}, u32[]{:S(2)}, u32[]{:S(2)}) collective-permute-start(f16[64,1024]{1,0:T(8,128)(2,1)S(1)} %fusion.23), channel_id=1, source_target_pairs={{0,16},{8,24},{16,0},{24,8},{1,17},{9,25},{17,1},{25,9},{2,18},{10... | collective-permute-start | bytes 393224 | tf_op jit(solution)/shard_map/ppermute | solution.py:247
  167.2 5.6 %collective-permute-start.43 = (f16[64,1024]{1,0:T(8,128)(2,1)S(1)}, f16[64,1024]{1,0:T(8,128)(2,1)S(1)}, u32[]{:S(2)}, u32[]{:S(2)}) collective-permute-start(f16[64,1024]{1,0:T(8,128)(2,1)S(1)} %add_convert_fusion), channel_id=1, source_target_pairs={{0,16},{8,24},{16,0},{24,8},{1,17},{9,25},{17,1},{25,9},{2,18},{10... | collective-permute-start | bytes 393224 | tf_op jit(solution)/shard_map/ppermute | solution.py:247
  (5 other events, 89.1 us)

commit v3 on v2

--- a/solution.py
+++ b/solution.py
@@ -25,12 +25,18 @@
     return jnp.concatenate([blocks[j] for j in order], axis=1)
 
 
-def stencil_body(me_ref, raw_ref, gain_ref, couple_ref, *refs, start, order, near):
+def stencil_body(raw_ref, gain_ref, couple_ref, *refs, start, order, far):
     refs, (gain_s, near_s, stage) = refs[:-3], refs[-3:]
     rows, cols = gain_ref.shape
     parts, frames, pixels = stage.shape
     groups = frames // 8
-    band = rows // parts
+    band = rows // (2 * parts)
+    me = lax.axis_index("pix")
+    own_half = me // parts
+    half = 1 - own_half if far else own_half
+    first_row = half * (rows // 2)
+    above = half.astype(F32)
+    below = 1.0 - above
 
     @pl.when(pl.program_id(0) == 0)
     def _():
@@ -46,19 +52,16 @@
     def every(ref, row):
         return ref[pl.ds(row, 8, stride=0), :]
 
-    def advance(state, row, end=False):
+    def advance(state, row, there=None):
         levels, scaled, weight = state
-        if end:
-            w_new = zero
-            enter = [zero] * groups
-            s_new = [zero] * groups
-        else:
-            w_new = every(near_s, row)
-            gain = every(gain_ref, row)
-            gain_scaled = every(gain_s, row)
-            raws = [raw_ref[pl.ds(g * 8 * rows + row, 8, stride=rows), :] for g in range(groups)]
-            enter = [raw * gain for raw in raws]
-            s_new = [raw * gain_scaled for raw in raws]
+        w_new = every(near_s, row)
+        gain = every(gain_ref, row)
+        gain_scaled = every(gain_s, row)
+        if there is not None:
+            w_new, gain, gain_scaled = w_new * there, gain * there, gain_scaled * there
+        raws = [raw_ref[pl.ds(g * 8 * rows + row, 8, stride=rows), :] for g in range(groups)]
+        enter = [raw * gain for raw in raws]
+        s_new = [raw * gain_scaled for raw in raws]
         out, new_levels = [], []
         for g in range(groups):
             new = enter[g]
@@ -80,7 +83,11 @@
 
     def one_band(part, state, error, first=False, last=False):
         for i in range(band):
-            state, out = advance(state, part * band + SWEEPS + i, end=last and i + SWEEPS >= band)
+            if last and i + SWEEPS >= band:
+                row = jnp.minimum(first_row + rows // 2 + (i + SWEEPS - band), rows - 1)
+                state, out = advance(state, row, below)
+            else:
+                state, out = advance(state, first_row + part * band + SWEEPS + i)
             value = jnp.concatenate(out, axis=0)
             value = value + (value * shift if first and i == 0 else error)
             rounded = value.astype(BF16)
@@ -93,70 +100,57 @@
         [[zero] * SWEEPS for _ in range(groups)],
         [zero] * SWEEPS,
     )
-    for row in range(SWEEPS):
-        state, _ = advance(state, row)
+    for i in range(SWEEPS):
+        state, _ = advance(state, jnp.maximum(first_row - SWEEPS + i, 0), above)
+    for i in range(SWEEPS):
+        state, _ = advance(state, first_row + i)
     carry = one_band(0, state, None, first=True)
     carry = lax.fori_loop(1, parts - 1, lambda part, c: one_band(part, *c), carry)
     one_band(parts - 1, *carry, last=True)
-
-    def mine(r):
-        return stage[jnp.bitwise_xor(me_ref[0], r)]
-
-    if near is None:
-        for r, out_ref in enumerate(refs):
-            out_ref[...] = mine(r)
-        return
-    early, w_ref, out_refs = refs[:near], refs[near], refs[near + 1 :]
-    w_mine = reordered(w_ref[...], me_ref[1], order).astype(BF16)
-    rank = w_mine.shape[1]
-    for r, out_ref in enumerate(out_refs):
-        if r < near:
-            before = early[r].shape[0]
-            out_ref[:before, :pixels] = early[r][...]
-            out_ref[before:, :pixels] = mine(r)
-            out_ref[:, pixels:] = w_mine
-        else:
-            out_ref[:, :pixels] = mine(r)
-            for i in range(w_mine.shape[0] // frames):
-                out_ref[:, pixels + rank * i : pixels + rank * (i + 1)] = w_mine[frames * i : frames * (i + 1)]
-
-
-def correct(raw_frames, gain_map, coupling, at, parts, start, count, early=None, factor_w=None, order=None):
+    w = None
+    if order is not None:
+        w, refs = reordered(refs[0][...], lax.axis_index("scan"), order).astype(BF16), refs[1:]
+    for r, out_ref in enumerate(refs):
+        out_ref[:, :pixels] = stage[jnp.bitwise_xor(me, r) % parts]
+        for i in range(0 if w is None else w.shape[0] // frames):
+            at, rank = pixels + w.shape[1] * i, w.shape[1]
+            out_ref[:, at : at + rank] = w[frames * i : frames * (i + 1)]
+
+
+def correct(raw_frames, gain_map, coupling, parts, far, start, count, factor_w=None, order=None):
     frames, rows, cols = raw_frames.shape
     group = 16
     pixels = rows * cols // parts
     first = start // group
-    if early is None:
-        extra, near = [], None
-        shapes = [(count, pixels)] * parts
-        out_specs = [pl.BlockSpec((group, pixels), lambda i, m: (i, 0))] * parts
-    else:
+    extra, specs, width = [], [], pixels
+    if factor_w is not None:
         rank = factor_w.shape[1]
-        extra, near = [*early, factor_w], len(early)
-        shapes = [(frames, pixels + rank)] * near + [(group, pixels + rank * (frames // group))] * (parts - near)
-        out_specs = [pl.BlockSpec(shape, lambda i, m: (0, 0)) for shape in shapes]
+        extra = [factor_w]
+        if count == frames:
+            specs, width = [pl.BlockSpec((group, rank), lambda i: (i, 0))], pixels + rank
+        else:
+            specs, width = [pl.BlockSpec((frames, rank), lambda i: (0, 0))], pixels + rank * (frames // group)
     return pl.pallas_call(
-        functools.partial(stencil_body, start=start, order=order, near=near),
-        out_shape=[jax.ShapeDtypeStruct(shape, BF16) for shape in shapes],
-        grid_spec=pltpu.PrefetchScalarGridSpec(
-            num_scalar_prefetch=1,
+        functools.partial(stencil_body, start=start, order=order, far=far),
+        out_shape=[jax.ShapeDtypeStruct((count, width), BF16)] * (parts // 2),
+        grid_spec=pl.GridSpec(
             grid=(count // group,),
             in_specs=[
-                pl.BlockSpec((group * rows, cols), lambda i, m: (i + first, 0)),
-                pl.BlockSpec((rows, cols), lambda i, m: (0, 0)),
-                pl.BlockSpec((rows, cols), lambda i, m: (0, 0)),
+                pl.BlockSpec((group * rows, cols), lambda i: (i + first, 0)),
+                pl.BlockSpec((rows, cols), lambda i: (0, 0)),
+                pl.BlockSpec((rows, cols), lambda i: (0, 0)),
             ]
-            + [pl.BlockSpec(x.shape, lambda i, m: (0, 0)) for x in extra],
-            out_specs=out_specs,
-            scratch_shapes=[pltpu.VMEM((rows, cols), F32)] * 2 + [pltpu.VMEM((parts, group, pixels), BF16)],
+            + specs,
+            out_specs=[pl.BlockSpec((group, width), lambda i: (i, 0))] * (parts // 2),
+            scratch_shapes=[pltpu.VMEM((rows, cols), F32)] * 2 + [pltpu.VMEM((parts // 2, group, pixels), BF16)],
         ),
         cost_estimate=pl.CostEstimate(
-            flops=count * rows * cols * SWEEPS * 9,
-            bytes_accessed=count * rows * cols * 6,
+            flops=count * rows * cols * SWEEPS * 5,
+            bytes_accessed=count * rows * cols * 5,
             transcendentals=0,
         ),
         name="charge_sharing",
-    )(at, raw_frames.reshape(frames * rows, cols), gain_map, coupling, *extra)
+    )(raw_frames.reshape(frames * rows, cols), gain_map, coupling, *extra)
 
 
 TILE = 256
@@ -230,7 +224,6 @@
 def local(raw_frames, gain_map, coupling, factor_w, factor_h, n_scan, n_pix):
     scan_bits = n_scan.bit_length() - 1
     scan = lax.axis_index("scan")
-    me = lax.axis_index("pix")
     row_count, rank = factor_w.shape
     comp_rows, pixels = factor_h.shape
     half = rank // 2
@@ -258,14 +251,16 @@
     close = n_pix // 2
     frames = raw_frames.shape[0]
     tile = {r: [] for r in range(n_pix)}
-    at = jnp.stack([me, scan]).astype(jnp.int32)
-    early = correct(raw_frames, gain_map, coupling, at, n_pix, 0, frames - 16)
-    late = correct(raw_frames, gain_map, coupling, at, n_pix, frames - 16, 16, early[:close], factor_w, comp_order)
-    for c, messages in enumerate([early, late]):
-        for r in range(1, n_pix):
-            if c or r >= close:
-                tile[r].append(over_pix(messages[r], r))
-    tile[0].append(late[0])
+    stencil = functools.partial(correct, raw_frames, gain_map, coupling, n_pix)
+    early = stencil(True, 0, frames - 16)
+    here = stencil(False, 0, frames, factor_w, comp_order)
+    late = stencil(True, frames - 16, 16, factor_w, comp_order)
+    tile[0].append(here[0])
+    for first, messages in [(close, early), (0, here), (close, late)]:
+        for i, message in enumerate(messages):
+            r = first + i
+            if r:
+                tile[r].append(over_pix(message, r))
 
     for bit in x_bits:
         factor_h = jnp.concatenate([factor_h, over_scan(factor_h, bit)], 0)

time: 174 us -> 166 us (0.954)
  starting transfers between devices: 76.9 us -> 67.2 us
  waiting for transfers between devices: 61.8 us -> 64.2 us
    ppermute x30, starting transfers between devices: 65 us -> 55.2 us  [over_pix(): return lax.ppermute(value, 'pix', [(i, i ^ bit) for i in range(n_pix)])]
    ppermute x30, waiting for transfers between devices: 29.4 us -> 31.9 us  [over_pix(): return lax.ppermute(value, 'pix', [(i, i ^ bit) for i in range(n_pix)])]
    pallas_call x2 -> x3, Pallas kernels: 16.2 us -> 16.9 us  [correct(): pl.pallas_call(functools.partial(stencil_body, start=start, order=order,...]
  transfers between devices with their start and end apart: 46 -> 46, of which waited for: 25 -> 25; matrix products, arithmetic and copies ran while one was open for 5% -> 5% of each run, Pallas kernels for 11% -> 12%
where the time goes in v3:
time: 166 us; the launch traced here: 165 us
  starting transfers between devices  67.2 us (40%)
  waiting for transfers between devices  64.2 us (39%)
  Pallas kernels  21.5 us (13%)
  matrix products  6.15 us (4%)
  other arithmetic  3.47 us (2%)
    ppermute x30, starting transfers between devices, over_pix(): return lax.ppermute(value, 'pix', [(i, i ^ bit) for i in range(n_pix)])  55.2 us
    ppermute x16, waiting for transfers between devices, over_scan(): return lax.ppermute(value, 'scan', [(i, i ^ bit) for i in range(n_scan)])  32.4 us
    ppermute x30, waiting for transfers between devices, over_pix(): return lax.ppermute(value, 'pix', [(i, i ^ bit) for i in range(n_pix)])  31.9 us
    pallas_call x3, Pallas kernels, correct(): pl.pallas_call(functools.partial(stencil_body, start=start, order=order,...  16.9 us
    ppermute x16, starting transfers between devices, over_scan(): return lax.ppermute(value, 'scan', [(i, i ^ bit) for i in range(n_scan)])  12 us
    pallas_call x7, Pallas kernels, term(): pl.pallas_call(body, out_shape=pltpu.VMEM(shape, dtype), in_specs=[VMEM]...  4.57 us
    dot_general x16, matrix products, numerator_rows(): lax.dot_general(w, ratio, (((0,), (0,)), ((), ())), preferred_element_typ...  3.92 us
  transfers between devices with their start and end apart: 46, of which 25 were waited for; matrix products, arithmetic and copies ran while one was open for 5% of the time, Pallas kernels for 12%

profile of v3, /device:TPU:0, one launch (start us, length us, event | category | flops | bytes accessed | tf_op | source)
XLA Modules:
  0.0 165.4 jit_solution(17987881191913210686)
XLA Ops:
  0.6 3.0 %collective-permute-start.3 = (f32[64,2048]{1,0:T(8,128)}, f32[64,2048]{1,0:T(8,128)S(1)}, u32[]{:S(2)}, u32[]{:S(2)}) collective-permute-start(f32[64,2048]{1,0:T(8,128)} %param.9), channel_id=1, source_target_pairs={{0,16},{8,24},{16,0},{24,8},{1,17},{9,25},{17,1},{25,9},{2,18},{10... | collective-permute-start | bytes 1572872 | tf_op jit(solution)/shard_map/ppermute | solution.py:240
  3.7 1.1 constant_dynamic-update-slice_fusion.1
  4.8 11.0 %collective-permute-done.3 = f32[64,2048]{1,0:T(8,128)S(1)} collective-permute-done((f32[64,2048]{1,0:T(8,128)}, f32[64,2048]{1,0:T(8,128)S(1)}, u32[]{:S(2)}, u32[]{:S(2)}) %collective-permute-start.3) | collective-permute-done | bytes 524320 | tf_op jit(solution)/shard_map/ppermute | solution.py:240
  16.0 7.4 %charge_sharing.3 = (bf16[48,2304]{1,0:T(8,128)(2,1)}, bf16[48,2304]{1,0:T(8,128)(2,1)}, bf16[48,2304]{1,0:T(8,128)(2,1)}, bf16[48,2304]{1,0:T(8,128)(2,1)}) custom-call(f32[6144,128]{1,0:T(8,128)} %bitcast.28, f32[128,128]{1,0:T(8,128)} %gain_ref.5, f32[128,128]{1,0:T(8,128)} %couple_ref.5, f32[48,256]{1,0:T(8,128)} %refs_0_.3), custom_call_target="tpu_custom_call" | custom-call | flops 15728640 | bytes 3932160 | tf_op jit(solution)/shard_map/charge_sharing/pallas_call | solution.py:133
  23.4 1.8 %collective-permute-start = (bf16[48,2304]{1,0:T(8,128)(2,1)}, bf16[48,2304]{1,0:T(8,128)(2,1)S(1)}, u32[]{:S(2)}, u32[]{:S(2)}) collective-permute-start(bf16[48,2304]{1,0:T(8,128)(2,1)} %get-tuple-element.34), channel_id=1, source_target_pairs={{0,1},{1,0},{2,3},{3,2},{4,5},{5,4},{6,7},{7,6},{8,9},{9,8},{10,11... | collective-permute-start | bytes 663560 | tf_op jit(solution)/shard_map/ppermute | solution.py:237
  25.2 1.6 collective-permute-start.1
  26.9 5.5 %charge_sharing.4 = (bf16[32,2048]{1,0:T(8,128)(2,1)}, bf16[32,2048]{1,0:T(8,128)(2,1)}, bf16[32,2048]{1,0:T(8,128)(2,1)}, bf16[32,2048]{1,0:T(8,128)(2,1)}) custom-call(f32[6144,128]{1,0:T(8,128)} %bitcast.29, f32[128,128]{1,0:T(8,128)} %gain_ref.5, f32[128,128]{1,0:T(8,128)} %couple_ref.5), custom_call_target="tpu_custom_call" | custom-call | flops 10485760 | bytes 2621440 | tf_op jit(solution)/shard_map/charge_sharing/pallas_call | solution.py:133
  32.5 4.9 %collective-permute-start.8 = (bf16[32,2048]{1,0:T(8,128)(2,1)}, bf16[32,2048]{1,0:T(8,128)(2,1)S(1)}, u32[]{:S(2)}, u32[]{:S(2)}) collective-permute-start(bf16[32,2048]{1,0:T(8,128)(2,1)} %get-tuple-element.42), channel_id=1, source_target_pairs={{0,7},{1,6},{2,5},{3,4},{4,3},{5,2},{6,1},{7,0},{8,15},{9,14},{10,... | collective-permute-start | bytes 393224 | tf_op jit(solution)/shard_map/ppermute | solution.py:237
  37.3 4.0 %charge_sharing.5 = (bf16[16,2816]{1,0:T(8,128)(2,1)}, bf16[16,2816]{1,0:T(8,128)(2,1)}, bf16[16,2816]{1,0:T(8,128)(2,1)}, bf16[16,2816]{1,0:T(8,128)(2,1)}) custom-call(f32[6144,128]{1,0:T(8,128)} %bitcast.30, f32[128,128]{1,0:T(8,128)} %gain_ref.5, f32[128,128]{1,0:T(8,128)} %couple_ref.5, f32[48,256]{1,0:T(8,128)} %refs_0_.3), custom_call_target="tpu_custom_call" | custom-call | flops 5242880 | bytes 1310720 | tf_op jit(solution)/shard_map/charge_sharing/pallas_call | solution.py:133
  41.4 3.7 %collective-permute-start.10 = (bf16[32,2048]{1,0:T(8,128)(2,1)S(1)}, bf16[32,2048]{1,0:T(8,128)(2,1)S(1)}, u32[]{:S(2)}, u32[]{:S(2)}) collective-permute-start(bf16[32,2048]{1,0:T(8,128)(2,1)S(1)} %copy-done.4), channel_id=1, source_target_pairs={{0,6},{1,7},{2,4},{3,5},{4,2},{5,3},{6,0},{7,1},{8,14},{9,15},{10,... | collective-permute-start | bytes 393224 | tf_op jit(solution)/shard_map/ppermute | solution.py:237
  46.2 3.5 %collective-permute-done.9.refs_1_.refs_5_ = bf16[16,2816]{1,0:T(8,128)(2,1)S(1)} collective-permute-done((bf16[16,2816]{1,0:T(8,128)(2,1)}, bf16[16,2816]{1,0:T(8,128)(2,1)S(1)}, u32[]{:S(2)}, u32[]{:S(2)}) %collective-permute-start.9) | collective-permute-done | bytes 90144 | tf_op jit(solution)/shard_map/ppermute | solution.py:237
  49.7 9.5 %collective-permute-start.15 = (bf16[16,2816]{1,0:T(8,128)(2,1)}, bf16[16,2816]{1,0:T(8,128)(2,1)S(1)}, u32[]{:S(2)}, u32[]{:S(2)}) collective-permute-start(bf16[16,2816]{1,0:T(8,128)(2,1)} %get-tuple-element.51), channel_id=1, source_target_pairs={{0,5},{1,4},{2,7},{3,6},{4,1},{5,0},{6,3},{7,2},{8,13},{9,12},{10,... | collective-permute-start | bytes 270344 | tf_op jit(solution)/shard_map/ppermute | solution.py:237
  59.3 3.8 %collective-permute-start.16 = (bf16[32,2048]{1,0:T(8,128)(2,1)S(1)}, bf16[32,2048]{1,0:T(8,128)(2,1)S(1)}, u32[]{:S(2)}, u32[]{:S(2)}) collective-permute-start(bf16[32,2048]{1,0:T(8,128)(2,1)S(1)} %copy-done.2), channel_id=1, source_target_pairs={{0,4},{1,5},{2,6},{3,7},{4,0},{5,1},{6,2},{7,3},{8,12},{9,13},{10,... | collective-permute-start | bytes 393224 | tf_op jit(solution)/shard_map/ppermute | solution.py:237
  64.2 8.3 %collective-permute-done.15.refs_1_.refs_3_ = bf16[16,2816]{1,0:T(8,128)(2,1)S(1)} collective-permute-done((bf16[16,2816]{1,0:T(8,128)(2,1)}, bf16[16,2816]{1,0:T(8,128)(2,1)S(1)}, u32[]{:S(2)}, u32[]{:S(2)}) %collective-permute-start.15) | collective-permute-done | bytes 90144 | tf_op jit(solution)/shard_map/ppermute | solution.py:237
  72.5 2.9 %collective-permute-done.17.refs_3_ = bf16[16,2816]{1,0:T(8,128)(2,1)S(1)} collective-permute-done((bf16[16,2816]{1,0:T(8,128)(2,1)}, bf16[16,2816]{1,0:T(8,128)(2,1)S(1)}, u32[]{:S(2)}, u32[]{:S(2)}) %collective-permute-start.17) | collective-permute-done | bytes 90144 | tf_op jit(solution)/shard_map/ppermute | solution.py:237
  76.6 3.1 %collective-permute-start.18 = (f16[64,256]{1,0:T(8,128)(2,1)S(1)}, f16[64,256]{1,0:T(8,128)(2,1)S(1)}, u32[]{:S(2)}, u32[]{:S(2)}) collective-permute-start(f16[64,256]{1,0:T(8,128)(2,1)S(1)} %concatenate.112), channel_id=1, source_target_pairs={{0,4},{1,5},{2,6},{3,7},{4,0},{5,1},{6,2},{7,3},{8,12},{9,13},{10,... | collective-permute-start | bytes 98312 | tf_op jit(solution)/shard_map/ppermute | solution.py:237
  79.9 3.3 %collective-permute-start.13 = (f16[64,256]{1,0:T(8,128)(2,1)S(1)}, f16[64,256]{1,0:T(8,128)(2,1)S(1)}, u32[]{:S(2)}, u32[]{:S(2)}) collective-permute-start(f16[64,256]{1,0:T(8,128)(2,1)S(1)} %pad_maximum_fusion.20), channel_id=1, source_target_pairs={{0,7},{1,6},{2,5},{3,4},{4,3},{5,2},{6,1},{7,0},{8,15},{9,14},{10,... | collective-permute-start | bytes 98312 | tf_op jit(solution)/shard_map/ppermute | solution.py:237
  83.2 1.3 collective-permute-start.12
  84.5 2.2 %collective-permute-start.6 = (f16[64,256]{1,0:T(8,128)(2,1)S(1)}, f16[64,256]{1,0:T(8,128)(2,1)S(1)}, u32[]{:S(2)}, u32[]{:S(2)}) collective-permute-start(f16[64,256]{1,0:T(8,128)(2,1)S(1)} %get-tuple-element.38), channel_id=1, source_target_pairs={{0,2},{1,3},{2,0},{3,1},{4,6},{5,7},{6,4},{7,5},{8,10},{9,11},{10,... | collective-permute-start | bytes 98312 | tf_op jit(solution)/shard_map/ppermute | solution.py:237
  86.7 1.3 collective-permute-start.5
  89.3 1.3 collective-permute-done.5
  90.8 2.4 %collective-permute-start.22 = (bf16[48,256]{1,0:T(8,128)(2,1)S(1)}, bf16[48,256]{1,0:T(8,128)(2,1)S(1)}, u32[]{:S(2)}, u32[]{:S(2)}) collective-permute-start(bf16[48,256]{1,0:T(8,128)(2,1)S(1)} %get-tuple-element.76), channel_id=1, source_target_pairs={{0,6},{1,7},{2,4},{3,5},{4,2},{5,3},{6,0},{7,1},{8,14},{9,15},{10,... | collective-permute-start | bytes 73736 | tf_op jit(solution)/shard_map/ppermute | solution.py:237
  93.2 2.1 %collective-permute-start.20 = (bf16[48,256]{1,0:T(8,128)(2,1)S(1)}, bf16[48,256]{1,0:T(8,128)(2,1)S(1)}, u32[]{:S(2)}, u32[]{:S(2)}) collective-permute-start(bf16[48,256]{1,0:T(8,128)(2,1)S(1)} %get-tuple-element.76), channel_id=1, source_target_pairs={{0,2},{1,3},{2,0},{3,1},{4,6},{5,7},{6,4},{7,5},{8,10},{9,11},{10,... | collective-permute-start | bytes 73736 | tf_op jit(solution)/shard_map/ppermute | solution.py:237
  95.3 1.2 collective-permute-done.22
  96.5 1.4 collective-permute-done.21
  98.0 1.6 collective-permute-start.23
  100.1 2.5 %collective-permute-done.23.refs_2_ = bf16[192,256]{1,0:T(8,128)(2,1)S(1)} collective-permute-done((bf16[192,256]{1,0:T(8,128)(2,1)S(1)}, bf16[192,256]{1,0:T(8,128)(2,1)S(1)}, u32[]{:S(2)}, u32[]{:S(2)}) %collective-permute-start.23) | collective-permute-done | bytes 98336 | tf_op jit(solution)/shard_map/ppermute | solution.py:237
  105.4 1.5 collective-permute-start.27
  107.2 1.8 %collective-permute-done.27 = f32[128]{0:T(128)S(1)} collective-permute-done((f32[128]{0:T(128)S(1)}, f32[128]{0:T(128)S(1)}, u32[]{:S(2)}, u32[]{:S(2)}) %collective-permute-start.27) | collective-permute-done | bytes 544 | tf_op jit(solution)/shard_map/ppermute | solution.py:240
  109.5 1.6 collective-permute-start.26
  112.1 6.6 %collective-permute-done.26 = f16[128,1024]{1,0:T(8,128)(2,1)S(1)} collective-permute-done((f16[128,1024]{1,0:T(8,128)(2,1)S(1)}, f16[128,1024]{1,0:T(8,128)(2,1)S(1)}, u32[]{:S(2)}, u32[]{:S(2)}) %collective-permute-start.26) | collective-permute-done | bytes 262176 | tf_op jit(solution)/shard_map/ppermute | solution.py:240
  119.0 3.7 %collective-permute-done.30 = f16[128,1024]{1,0:T(8,128)(2,1)S(1)} collective-permute-done((f16[128,1024]{1,0:T(8,128)(2,1)S(1)}, f16[128,1024]{1,0:T(8,128)(2,1)S(1)}, u32[]{:S(2)}, u32[]{:S(2)}) %collective-permute-start.30) | collective-permute-done | bytes 262176 | tf_op jit(solution)/shard_map/ppermute | solution.py:240
  123.0 1.5 collective-permute-done.31.refs_6_
  125.4 1.6 collective-permute-start.32
  127.8 2.6 %collective-permute-done.32 = f16[208,256]{1,0:T(8,128)(2,1)S(1)} collective-permute-done((f16[208,256]{1,0:T(8,128)(2,1)S(1)}, f16[208,256]{1,0:T(8,128)(2,1)S(1)}, u32[]{:S(2)}, u32[]{:S(2)}) %collective-permute-start.32) | collective-permute-done | bytes 106528 | tf_op jit(solution)/shard_map/ppermute | solution.py:237
  130.5 1.8 %collective-permute-start.35 = (f16[64,256]{1,0:T(8,128)(2,1)S(1)}, f16[64,256]{1,0:T(8,128)(2,1)S(1)}, u32[]{:S(2)}, u32[]{:S(2)}) collective-permute-start(f16[64,256]{1,0:T(8,128)(2,1)S(1)} %concatenate.113), channel_id=1, source_target_pairs={{0,6},{1,7},{2,4},{3,5},{4,2},{5,3},{6,0},{7,1},{8,14},{9,15},{10,... | collective-permute-start | bytes 98312 | tf_op jit(solution)/shard_map/ppermute | solution.py:237
  133.3 1.8 %collective-permute-start.33 = (f16[64,256]{1,0:T(8,128)(2,1)S(1)}, f16[64,256]{1,0:T(8,128)(2,1)S(1)}, u32[]{:S(2)}, u32[]{:S(2)}) collective-permute-start(f16[64,256]{1,0:T(8,128)(2,1)S(1)} %get-tuple-element.102), channel_id=1, source_target_pairs={{0,2},{1,3},{2,0},{3,1},{4,6},{5,7},{6,4},{7,5},{8,10},{9,11},{10,... | collective-permute-start | bytes 98312 | tf_op jit(solution)/shard_map/ppermute | solution.py:237
  135.1 1.5 collective-permute-done.35
  137.6 2.2 %collective-permute-start.38 = (bf16[48,256]{1,0:T(8,128)(2,1)S(1)}, bf16[48,256]{1,0:T(8,128)(2,1)S(1)}, u32[]{:S(2)}, u32[]{:S(2)}) collective-permute-start(bf16[48,256]{1,0:T(8,128)(2,1)S(1)} %get-tuple-element.66), channel_id=1, source_target_pairs={{0,6},{1,7},{2,4},{3,5},{4,2},{5,3},{6,0},{7,1},{8,14},{9,15},{10,... | collective-permute-start | bytes 73736 | tf_op jit(solution)/shard_map/ppermute | solution.py:237
  140.6 1.5 collective-permute-start.36
  143.3 1.3 collective-permute-done.37
  144.7 1.6 collective-permute-start.39
  146.9 2.5 %collective-permute-done.39 = bf16[192,256]{1,0:T(8,128)(2,1)S(1)} collective-permute-done((bf16[192,256]{1,0:T(8,128)(2,1)S(1)}, bf16[192,256]{1,0:T(8,128)(2,1)S(1)}, u32[]{:S(2)}, u32[]{:S(2)}) %collective-permute-start.39) | collective-permute-done | bytes 98336 | tf_op jit(solution)/shard_map/ppermute | solution.py:237
  153.0 1.5 collective-permute-start.45
  154.8 1.8 %collective-permute-done.45 = f32[64]{0:T(128)S(1)} collective-permute-done((f32[64]{0:T(128)S(1)}, f32[64]{0:T(128)S(1)}, u32[]{:S(2)}, u32[]{:S(2)}) %collective-permute-start.45) | collective-permute-done | bytes 288 | tf_op jit(solution)/shard_map/ppermute | solution.py:240
  157.0 1.6 collective-permute-start.44
  159.5 3.6 %collective-permute-done.44 = f16[64,1024]{1,0:T(8,128)(2,1)S(1)} collective-permute-done((f16[64,1024]{1,0:T(8,128)(2,1)S(1)}, f16[64,1024]{1,0:T(8,128)(2,1)S(1)}, u32[]{:S(2)}, u32[]{:S(2)}) %collective-permute-start.44) | collective-permute-done | bytes 131104 | tf_op jit(solution)/shard_map/ppermute | solution.py:240
  163.2 1.3 collective-permute-done.43
  (151 shorter events, 23.4 us)
Async XLA Ops:
  0.6 15.2 %collective-permute-start.3 = (f32[64,2048]{1,0:T(8,128)}, f32[64,2048]{1,0:T(8,128)S(1)}, u32[]{:S(2)}, u32[]{:S(2)}) collective-permute-start(f32[64,2048]{1,0:T(8,128)} %param.9), channel_id=1, source_target_pairs={{0,16},{8,24},{16,0},{24,8},{1,17},{9,25},{17,1},{25,9},{2,18},{10... | collective-permute-start | bytes 1572872 | tf_op jit(solution)/shard_map/ppermute | solution.py:240
  15.9 29.3 %collective-permute-start.4 = (bf16[128,2048]{1,0:T(8,128)(2,1)S(1)}, bf16[128,2048]{1,0:T(8,128)(2,1)S(1)}, u32[]{:S(2)}, u32[]{:S(2)}) collective-permute-start(bf16[128,2048]{1,0:T(8,128)(2,1)S(1)} %convert_element_type.137.refs_4_), channel_id=1, source_target_pairs={{0,8},{8,0},{16,24},{24,16},{1,9},{9,1},{17,25},{25,17},{2,10},{10... | collective-permute-start | bytes 1572872 | tf_op jit(solution)/shard_map/ppermute | solution.py:240
  23.4 17.9 %collective-permute-start = (bf16[48,2304]{1,0:T(8,128)(2,1)}, bf16[48,2304]{1,0:T(8,128)(2,1)S(1)}, u32[]{:S(2)}, u32[]{:S(2)}) collective-permute-start(bf16[48,2304]{1,0:T(8,128)(2,1)} %get-tuple-element.34), channel_id=1, source_target_pairs={{0,1},{1,0},{2,3},{3,2},{4,5},{5,4},{6,7},{7,6},{8,9},{9,8},{10,11... | collective-permute-start | bytes 663560 | tf_op jit(solution)/shard_map/ppermute | solution.py:237
  25.2 16.2 %collective-permute-start.1 = (bf16[48,2304]{1,0:T(8,128)(2,1)}, bf16[48,2304]{1,0:T(8,128)(2,1)S(1)}, u32[]{:S(2)}, u32[]{:S(2)}) collective-permute-start(bf16[48,2304]{1,0:T(8,128)(2,1)} %get-tuple-element.35), channel_id=1, source_target_pairs={{0,2},{1,3},{2,0},{3,1},{4,6},{5,7},{6,4},{7,5},{8,10},{9,11},{10,... | collective-permute-start | bytes 663560 | tf_op jit(solution)/shard_map/ppermute | solution.py:237
  26.8 18.3 %collective-permute-start.2 = (bf16[48,2304]{1,0:T(8,128)(2,1)}, bf16[48,2304]{1,0:T(8,128)(2,1)S(1)}, u32[]{:S(2)}, u32[]{:S(2)}) collective-permute-start(bf16[48,2304]{1,0:T(8,128)(2,1)} %get-tuple-element.36), channel_id=1, source_target_pairs={{0,3},{1,2},{2,1},{3,0},{4,7},{5,6},{6,5},{7,4},{8,11},{9,10},{10,... | collective-permute-start | bytes 663560 | tf_op jit(solution)/shard_map/ppermute | solution.py:237
  32.5 26.8 %copy-start.2 = (bf16[32,2048]{1,0:T(8,128)(2,1)S(1)}, bf16[32,2048]{1,0:T(8,128)(2,1)}, u32[]{:S(2)}) copy-start(bf16[32,2048]{1,0:T(8,128)(2,1)} %get-tuple-element.52) | copy-start | bytes 393220
  32.5 30.6 %collective-permute-start.8 = (bf16[32,2048]{1,0:T(8,128)(2,1)}, bf16[32,2048]{1,0:T(8,128)(2,1)S(1)}, u32[]{:S(2)}, u32[]{:S(2)}) collective-permute-start(bf16[32,2048]{1,0:T(8,128)(2,1)} %get-tuple-element.42), channel_id=1, source_target_pairs={{0,7},{1,6},{2,5},{3,4},{4,3},{5,2},{6,1},{7,0},{8,15},{9,14},{10,... | collective-permute-start | bytes 393224 | tf_op jit(solution)/shard_map/ppermute | solution.py:237
  41.3 8.4 %collective-permute-start.9 = (bf16[16,2816]{1,0:T(8,128)(2,1)}, bf16[16,2816]{1,0:T(8,128)(2,1)S(1)}, u32[]{:S(2)}, u32[]{:S(2)}) collective-permute-start(bf16[16,2816]{1,0:T(8,128)(2,1)} %get-tuple-element.43), channel_id=1, source_target_pairs={{0,7},{1,6},{2,5},{3,4},{4,3},{5,2},{6,1},{7,0},{8,15},{9,14},{10,... | collective-permute-start | bytes 270344 | tf_op jit(solution)/shard_map/ppermute | solution.py:237
  41.4 21.8 %collective-permute-start.10 = (bf16[32,2048]{1,0:T(8,128)(2,1)S(1)}, bf16[32,2048]{1,0:T(8,128)(2,1)S(1)}, u32[]{:S(2)}, u32[]{:S(2)}) collective-permute-start(bf16[32,2048]{1,0:T(8,128)(2,1)S(1)} %copy-done.4), channel_id=1, source_target_pairs={{0,6},{1,7},{2,4},{3,5},{4,2},{5,3},{6,0},{7,1},{8,14},{9,15},{10,... | collective-permute-start | bytes 393224 | tf_op jit(solution)/shard_map/ppermute | solution.py:237
  45.1 14.2 %collective-permute-start.11 = (bf16[16,2816]{1,0:T(8,128)(2,1)}, bf16[16,2816]{1,0:T(8,128)(2,1)S(1)}, u32[]{:S(2)}, u32[]{:S(2)}) collective-permute-start(bf16[16,2816]{1,0:T(8,128)(2,1)} %get-tuple-element.45), channel_id=1, source_target_pairs={{0,6},{1,7},{2,4},{3,5},{4,2},{5,3},{6,0},{7,1},{8,14},{9,15},{10,... | collective-permute-start | bytes 270344 | tf_op jit(solution)/shard_map/ppermute | solution.py:237
  45.3 30.2 %collective-permute-start.14 = (bf16[32,2048]{1,0:T(8,128)(2,1)S(1)}, bf16[32,2048]{1,0:T(8,128)(2,1)S(1)}, u32[]{:S(2)}, u32[]{:S(2)}) collective-permute-start(bf16[32,2048]{1,0:T(8,128)(2,1)S(1)} %copy-done.3), channel_id=1, source_target_pairs={{0,5},{1,4},{2,7},{3,6},{4,1},{5,0},{6,3},{7,2},{8,13},{9,12},{10,... | collective-permute-start | bytes 393224 | tf_op jit(solution)/shard_map/ppermute | solution.py:237
  45.3 34.4 %copy-start.1 = (f32[48,256]{1,0:T(8,128)S(1)}, f32[48,256]{1,0:T(8,128)}, u32[]{:S(2)}) copy-start(f32[48,256]{1,0:T(8,128)} %refs_0_.3) | copy-start | bytes 147460
  49.7 22.8 %collective-permute-start.15 = (bf16[16,2816]{1,0:T(8,128)(2,1)}, bf16[16,2816]{1,0:T(8,128)(2,1)S(1)}, u32[]{:S(2)}, u32[]{:S(2)}) collective-permute-start(bf16[16,2816]{1,0:T(8,128)(2,1)} %get-tuple-element.51), channel_id=1, source_target_pairs={{0,5},{1,4},{2,7},{3,6},{4,1},{5,0},{6,3},{7,2},{8,13},{9,12},{10,... | collective-permute-start | bytes 270344 | tf_op jit(solution)/shard_map/ppermute | solution.py:237
  59.3 16.2 %collective-permute-start.16 = (bf16[32,2048]{1,0:T(8,128)(2,1)S(1)}, bf16[32,2048]{1,0:T(8,128)(2,1)S(1)}, u32[]{:S(2)}, u32[]{:S(2)}) collective-permute-start(bf16[32,2048]{1,0:T(8,128)(2,1)S(1)} %copy-done.2), channel_id=1, source_target_pairs={{0,4},{1,5},{2,6},{3,7},{4,0},{5,1},{6,2},{7,3},{8,12},{9,13},{10,... | collective-permute-start | bytes 393224 | tf_op jit(solution)/shard_map/ppermute | solution.py:237
  63.1 12.4 %collective-permute-start.17 = (bf16[16,2816]{1,0:T(8,128)(2,1)}, bf16[16,2816]{1,0:T(8,128)(2,1)S(1)}, u32[]{:S(2)}, u32[]{:S(2)}) collective-permute-start(bf16[16,2816]{1,0:T(8,128)(2,1)} %get-tuple-element.53), channel_id=1, source_target_pairs={{0,4},{1,5},{2,6},{3,7},{4,0},{5,1},{6,2},{7,3},{8,12},{9,13},{10,... | collective-permute-start | bytes 270344 | tf_op jit(solution)/shard_map/ppermute | solution.py:237
  76.5 8.0 %collective-permute-start.19 = (f16[64,256]{1,0:T(8,128)(2,1)S(1)}, f16[64,256]{1,0:T(8,128)(2,1)S(1)}, u32[]{:S(2)}, u32[]{:S(2)}) collective-permute-start(f16[64,256]{1,0:T(8,128)(2,1)S(1)} %pad_maximum_fusion.21), channel_id=1, source_target_pairs={{0,5},{1,4},{2,7},{3,6},{4,1},{5,0},{6,3},{7,2},{8,13},{9,12},{10,... | collective-permute-start | bytes 98312 | tf_op jit(solution)/shard_map/ppermute | solution.py:237
  76.6 10.1 %collective-permute-start.18 = (f16[64,256]{1,0:T(8,128)(2,1)S(1)}, f16[64,256]{1,0:T(8,128)(2,1)S(1)}, u32[]{:S(2)}, u32[]{:S(2)}) collective-permute-start(f16[64,256]{1,0:T(8,128)(2,1)S(1)} %concatenate.112), channel_id=1, source_target_pairs={{0,4},{1,5},{2,6},{3,7},{4,0},{5,1},{6,2},{7,3},{8,12},{9,13},{10,... | collective-permute-start | bytes 98312 | tf_op jit(solution)/shard_map/ppermute | solution.py:237
  79.9 8.2 %collective-permute-start.13 = (f16[64,256]{1,0:T(8,128)(2,1)S(1)}, f16[64,256]{1,0:T(8,128)(2,1)S(1)}, u32[]{:S(2)}, u32[]{:S(2)}) collective-permute-start(f16[64,256]{1,0:T(8,128)(2,1)S(1)} %pad_maximum_fusion.20), channel_id=1, source_target_pairs={{0,7},{1,6},{2,5},{3,4},{4,3},{5,2},{6,1},{7,0},{8,15},{9,14},{10,... | collective-permute-start | bytes 98312 | tf_op jit(solution)/shard_map/ppermute | solution.py:237
  83.2 5.8 %collective-permute-start.12 = (f16[64,256]{1,0:T(8,128)(2,1)S(1)}, f16[64,256]{1,0:T(8,128)(2,1)S(1)}, u32[]{:S(2)}, u32[]{:S(2)}) collective-permute-start(f16[64,256]{1,0:T(8,128)(2,1)S(1)} %concatenate.111), channel_id=1, source_target_pairs={{0,6},{1,7},{2,4},{3,5},{4,2},{5,3},{6,0},{7,1},{8,14},{9,15},{10,... | collective-permute-start | bytes 98312 | tf_op jit(solution)/shard_map/ppermute | solution.py:237
  84.5 4.8 %collective-permute-start.7 = (f16[64,256]{1,0:T(8,128)(2,1)S(1)}, f16[64,256]{1,0:T(8,128)(2,1)S(1)}, u32[]{:S(2)}, u32[]{:S(2)}) collective-permute-start(f16[64,256]{1,0:T(8,128)(2,1)S(1)} %concatenate.110), channel_id=1, source_target_pairs={{0,3},{1,2},{2,1},{3,0},{4,7},{5,6},{6,5},{7,4},{8,11},{9,10},{10,... | collective-permute-start | bytes 98312 | tf_op jit(solution)/shard_map/ppermute | solution.py:237
  84.5 4.8 %collective-permute-start.6 = (f16[64,256]{1,0:T(8,128)(2,1)S(1)}, f16[64,256]{1,0:T(8,128)(2,1)S(1)}, u32[]{:S(2)}, u32[]{:S(2)}) collective-permute-start(f16[64,256]{1,0:T(8,128)(2,1)S(1)} %get-tuple-element.38), channel_id=1, source_target_pairs={{0,2},{1,3},{2,0},{3,1},{4,6},{5,7},{6,4},{7,5},{8,10},{9,11},{10,... | collective-permute-start | bytes 98312 | tf_op jit(solution)/shard_map/ppermute | solution.py:237
  86.7 3.9 %collective-permute-start.5 = (f16[64,256]{1,0:T(8,128)(2,1)S(1)}, f16[64,256]{1,0:T(8,128)(2,1)S(1)}, u32[]{:S(2)}, u32[]{:S(2)}) collective-permute-start(f16[64,256]{1,0:T(8,128)(2,1)S(1)} %get-tuple-element.37), channel_id=1, source_target_pairs={{0,1},{1,0},{2,3},{3,2},{4,5},{5,4},{6,7},{7,6},{8,9},{9,8},{10,11... | collective-permute-start | bytes 98312 | tf_op jit(solution)/shard_map/ppermute | solution.py:237
  90.8 5.7 %collective-permute-start.22 = (bf16[48,256]{1,0:T(8,128)(2,1)S(1)}, bf16[48,256]{1,0:T(8,128)(2,1)S(1)}, u32[]{:S(2)}, u32[]{:S(2)}) collective-permute-start(bf16[48,256]{1,0:T(8,128)(2,1)S(1)} %get-tuple-element.76), channel_id=1, source_target_pairs={{0,6},{1,7},{2,4},{3,5},{4,2},{5,3},{6,0},{7,1},{8,14},{9,15},{10,... | collective-permute-start | bytes 73736 | tf_op jit(solution)/shard_map/ppermute | solution.py:237
  93.2 4.7 %collective-permute-start.21 = (bf16[48,256]{1,0:T(8,128)(2,1)S(1)}, bf16[48,256]{1,0:T(8,128)(2,1)S(1)}, u32[]{:S(2)}, u32[]{:S(2)}) collective-permute-start(bf16[48,256]{1,0:T(8,128)(2,1)S(1)} %get-tuple-element.76), channel_id=1, source_target_pairs={{0,4},{1,5},{2,6},{3,7},{4,0},{5,1},{6,2},{7,3},{8,12},{9,13},{10,... | collective-permute-start | bytes 73736 | tf_op jit(solution)/shard_map/ppermute | solution.py:237
  93.2 4.7 %collective-permute-start.20 = (bf16[48,256]{1,0:T(8,128)(2,1)S(1)}, bf16[48,256]{1,0:T(8,128)(2,1)S(1)}, u32[]{:S(2)}, u32[]{:S(2)}) collective-permute-start(bf16[48,256]{1,0:T(8,128)(2,1)S(1)} %get-tuple-element.76), channel_id=1, source_target_pairs={{0,2},{1,3},{2,0},{3,1},{4,6},{5,7},{6,4},{7,5},{8,10},{9,11},{10,... | collective-permute-start | bytes 73736 | tf_op jit(solution)/shard_map/ppermute | solution.py:237
  98.0 4.7 %collective-permute-start.23 = (bf16[192,256]{1,0:T(8,128)(2,1)S(1)}, bf16[192,256]{1,0:T(8,128)(2,1)S(1)}, u32[]{:S(2)}, u32[]{:S(2)}) collective-permute-start(bf16[192,256]{1,0:T(8,128)(2,1)S(1)} %get-tuple-element.75.refs_2_), channel_id=1, source_target_pairs={{0,1},{1,0},{2,3},{3,2},{4,5},{5,4},{6,7},{7,6},{8,9},{9,8},{10,11... | collective-permute-start | bytes 294920 | tf_op jit(solution)/shard_map/ppermute | solution.py:237
  102.7 2.6 %collective-permute-start.25 = (f32[128]{0:T(128)S(1)}, f32[128]{0:T(128)S(1)}, u32[]{:S(2)}, u32[]{:S(2)}) collective-permute-start(f32[128]{0:T(128)S(1)} %slice.262), channel_id=1, source_target_pairs={{0,8},{8,0},{16,24},{24,16},{1,9},{9,1},{17,25},{25,17},{2,10},{10... | collective-permute-start | bytes 1544 | tf_op jit(solution)/shard_map/ppermute | solution.py:240
  103.6 5.4 %collective-permute-start.24 = (f32[128,1024]{1,0:T(8,128)S(1)}, f32[128,1024]{1,0:T(8,128)S(1)}, u32[]{:S(2)}, u32[]{:S(2)}) collective-permute-start(f32[128,1024]{1,0:T(8,128)S(1)} %convolution_add_fusion.6), channel_id=1, source_target_pairs={{0,8},{8,0},{16,24},{24,16},{1,9},{9,1},{17,25},{25,17},{2,10},{10... | collective-permute-start | bytes 1572872 | tf_op jit(solution)/shard_map/ppermute | solution.py:240
  105.2 5.8 %collective-permute-start.29 = (f32[128,1024]{1,0:T(8,128)S(1)}, f32[128,1024]{1,0:T(8,128)S(1)}, u32[]{:S(2)}, u32[]{:S(2)}) collective-permute-start(f32[128,1024]{1,0:T(8,128)S(1)} %convolution_add_fusion.4), channel_id=1, source_target_pairs={{0,8},{8,0},{16,24},{24,16},{1,9},{9,1},{17,25},{25,17},{2,10},{10... | collective-permute-start | bytes 1572872 | tf_op jit(solution)/shard_map/ppermute | solution.py:240
  105.4 3.6 %collective-permute-start.27 = (f32[128]{0:T(128)S(1)}, f32[128]{0:T(128)S(1)}, u32[]{:S(2)}, u32[]{:S(2)}) collective-permute-start(f32[128]{0:T(128)S(1)} %pad_maximum_fusion.22), channel_id=1, source_target_pairs={{0,16},{8,24},{16,0},{24,8},{1,17},{9,25},{17,1},{25,9},{2,18},{10... | collective-permute-start | bytes 1544 | tf_op jit(solution)/shard_map/ppermute | solution.py:240
  109.5 9.2 %collective-permute-start.26 = (f16[128,1024]{1,0:T(8,128)(2,1)S(1)}, f16[128,1024]{1,0:T(8,128)(2,1)S(1)}, u32[]{:S(2)}, u32[]{:S(2)}) collective-permute-start(f16[128,1024]{1,0:T(8,128)(2,1)S(1)} %fusion.15), channel_id=1, source_target_pairs={{0,16},{8,24},{16,0},{24,8},{1,17},{9,25},{17,1},{25,9},{2,18},{10... | collective-permute-start | bytes 786440 | tf_op jit(solution)/shard_map/ppermute | solution.py:240
  111.5 11.2 %collective-permute-start.30 = (f16[128,1024]{1,0:T(8,128)(2,1)S(1)}, f16[128,1024]{1,0:T(8,128)(2,1)S(1)}, u32[]{:S(2)}, u32[]{:S(2)}) collective-permute-start(f16[128,1024]{1,0:T(8,128)(2,1)S(1)} %fusion.17), channel_id=1, source_target_pairs={{0,16},{8,24},{16,0},{24,8},{1,17},{9,25},{17,1},{25,9},{2,18},{10... | collective-permute-start | bytes 786440 | tf_op jit(solution)/shard_map/ppermute | solution.py:240
  118.9 4.1 %collective-permute-start.28 = (bf16[128,1024]{1,0:T(8,128)(2,1)S(1)}, bf16[128,1024]{1,0:T(8,128)(2,1)S(1)}, u32[]{:S(2)}, u32[]{:S(2)}) collective-permute-start(bf16[128,1024]{1,0:T(8,128)(2,1)S(1)} %get-tuple-element.72.refs_3_), channel_id=1, source_target_pairs={{0,8},{8,0},{16,24},{24,16},{1,9},{9,1},{17,25},{25,17},{2,10},{10... | collective-permute-start | bytes 786440 | tf_op jit(solution)/shard_map/ppermute | solution.py:240
  122.9 1.6 collective-permute-start.31
  125.4 5.1 %collective-permute-start.32 = (f16[208,256]{1,0:T(8,128)(2,1)S(1)}, f16[208,256]{1,0:T(8,128)(2,1)S(1)}, u32[]{:S(2)}, u32[]{:S(2)}) collective-permute-start(f16[208,256]{1,0:T(8,128)(2,1)S(1)} %convert_element_type.162), channel_id=1, source_target_pairs={{0,1},{1,0},{2,3},{3,2},{4,5},{5,4},{6,7},{7,6},{8,9},{9,8},{10,11... | collective-permute-start | bytes 319496 | tf_op jit(solution)/shard_map/ppermute | solution.py:237
  130.5 6.0 %collective-permute-start.35 = (f16[64,256]{1,0:T(8,128)(2,1)S(1)}, f16[64,256]{1,0:T(8,128)(2,1)S(1)}, u32[]{:S(2)}, u32[]{:S(2)}) collective-permute-start(f16[64,256]{1,0:T(8,128)(2,1)S(1)} %concatenate.113), channel_id=1, source_target_pairs={{0,6},{1,7},{2,4},{3,5},{4,2},{5,3},{6,0},{7,1},{8,14},{9,15},{10,... | collective-permute-start | bytes 98312 | tf_op jit(solution)/shard_map/ppermute | solution.py:237
  132.3 4.9 %collective-permute-start.34 = (f16[64,256]{1,0:T(8,128)(2,1)S(1)}, f16[64,256]{1,0:T(8,128)(2,1)S(1)}, u32[]{:S(2)}, u32[]{:S(2)}) collective-permute-start(f16[64,256]{1,0:T(8,128)(2,1)S(1)} %get-tuple-element.103), channel_id=1, source_target_pairs={{0,4},{1,5},{2,6},{3,7},{4,0},{5,1},{6,2},{7,3},{8,12},{9,13},{10,... | collective-permute-start | bytes 98312 | tf_op jit(solution)/shard_map/ppermute | solution.py:237
  133.3 4.2 %collective-permute-start.33 = (f16[64,256]{1,0:T(8,128)(2,1)S(1)}, f16[64,256]{1,0:T(8,128)(2,1)S(1)}, u32[]{:S(2)}, u32[]{:S(2)}) collective-permute-start(f16[64,256]{1,0:T(8,128)(2,1)S(1)} %get-tuple-element.102), channel_id=1, source_target_pairs={{0,2},{1,3},{2,0},{3,1},{4,6},{5,7},{6,4},{7,5},{8,10},{9,11},{10,... | collective-permute-start | bytes 98312 | tf_op jit(solution)/shard_map/ppermute | solution.py:237
  137.6 5.7 %collective-permute-start.38 = (bf16[48,256]{1,0:T(8,128)(2,1)S(1)}, bf16[48,256]{1,0:T(8,128)(2,1)S(1)}, u32[]{:S(2)}, u32[]{:S(2)}) collective-permute-start(bf16[48,256]{1,0:T(8,128)(2,1)S(1)} %get-tuple-element.66), channel_id=1, source_target_pairs={{0,6},{1,7},{2,4},{3,5},{4,2},{5,3},{6,0},{7,1},{8,14},{9,15},{10,... | collective-permute-start | bytes 73736 | tf_op jit(solution)/shard_map/ppermute | solution.py:237
  139.9 4.8 %collective-permute-start.37 = (bf16[48,256]{1,0:T(8,128)(2,1)S(1)}, bf16[48,256]{1,0:T(8,128)(2,1)S(1)}, u32[]{:S(2)}, u32[]{:S(2)}) collective-permute-start(bf16[48,256]{1,0:T(8,128)(2,1)S(1)} %get-tuple-element.66), channel_id=1, source_target_pairs={{0,4},{1,5},{2,6},{3,7},{4,0},{5,1},{6,2},{7,3},{8,12},{9,13},{10,... | collective-permute-start | bytes 73736 | tf_op jit(solution)/shard_map/ppermute | solution.py:237
  140.6 4.1 %collective-permute-start.36 = (bf16[48,256]{1,0:T(8,128)(2,1)S(1)}, bf16[48,256]{1,0:T(8,128)(2,1)S(1)}, u32[]{:S(2)}, u32[]{:S(2)}) collective-permute-start(bf16[48,256]{1,0:T(8,128)(2,1)S(1)} %get-tuple-element.66), channel_id=1, source_target_pairs={{0,2},{1,3},{2,0},{3,1},{4,6},{5,7},{6,4},{7,5},{8,10},{9,11},{10,... | collective-permute-start | bytes 73736 | tf_op jit(solution)/shard_map/ppermute | solution.py:237
  144.7 4.7 %collective-permute-start.39 = (bf16[192,256]{1,0:T(8,128)(2,1)S(1)}, bf16[192,256]{1,0:T(8,128)(2,1)S(1)}, u32[]{:S(2)}, u32[]{:S(2)}) collective-permute-start(bf16[192,256]{1,0:T(8,128)(2,1)S(1)} %get-tuple-element.65), channel_id=1, source_target_pairs={{0,1},{1,0},{2,3},{3,2},{4,5},{5,4},{6,7},{7,6},{8,9},{9,8},{10,11... | collective-permute-start | bytes 294920 | tf_op jit(solution)/shard_map/ppermute | solution.py:237
  151.0 5.6 %collective-permute-start.41 = (f32[128,1024]{1,0:T(8,128)S(1)}, f32[128,1024]{1,0:T(8,128)S(1)}, u32[]{:S(2)}, u32[]{:S(2)}) collective-permute-start(f32[128,1024]{1,0:T(8,128)S(1)} %convolution_add_fusion.2), channel_id=1, source_target_pairs={{0,8},{8,0},{16,24},{24,16},{1,9},{9,1},{17,25},{25,17},{2,10},{10... | collective-permute-start | bytes 1572872 | tf_op jit(solution)/shard_map/ppermute | solution.py:240
  151.1 1.8 %collective-permute-start.42 = (f32[128]{0:T(128)S(1)}, f32[128]{0:T(128)S(1)}, u32[]{:S(2)}, u32[]{:S(2)}) collective-permute-start(f32[128]{0:T(128)S(1)} %slice.293), channel_id=1, source_target_pairs={{0,8},{8,0},{16,24},{24,16},{1,9},{9,1},{17,25},{25,17},{2,10},{10... | collective-permute-start | bytes 1544 | tf_op jit(solution)/shard_map/ppermute | solution.py:240
  151.9 6.6 %collective-permute-start.40 = (f32[128,1024]{1,0:T(8,128)S(1)}, f32[128,1024]{1,0:T(8,128)S(1)}, u32[]{:S(2)}, u32[]{:S(2)}) collective-permute-start(f32[128,1024]{1,0:T(8,128)S(1)} %convolution_add_fusion.1), channel_id=1, source_target_pairs={{0,8},{8,0},{16,24},{24,16},{1,9},{9,1},{17,25},{25,17},{2,10},{10... | collective-permute-start | bytes 1572872 | tf_op jit(solution)/shard_map/ppermute | solution.py:240
  153.0 3.6 %collective-permute-start.45 = (f32[64]{0:T(128)S(1)}, f32[64]{0:T(128)S(1)}, u32[]{:S(2)}, u32[]{:S(2)}) collective-permute-start(f32[64]{0:T(128)S(1)} %slice.294), channel_id=1, source_target_pairs={{0,16},{8,24},{16,0},{24,8},{1,17},{9,25},{17,1},{25,9},{2,18},{10... | collective-permute-start | bytes 776 | tf_op jit(solution)/shard_map/ppermute | solution.py:240
  157.0 6.1 %collective-permute-start.44 = (f16[64,1024]{1,0:T(8,128)(2,1)S(1)}, f16[64,1024]{1,0:T(8,128)(2,1)S(1)}, u32[]{:S(2)}, u32[]{:S(2)}) collective-permute-start(f16[64,1024]{1,0:T(8,128)(2,1)S(1)} %fusion.23), channel_id=1, source_target_pairs={{0,16},{8,24},{16,0},{24,8},{1,17},{9,25},{17,1},{25,9},{2,18},{10... | collective-permute-start | bytes 393224 | tf_op jit(solution)/shard_map/ppermute | solution.py:240
  158.9 5.6 %collective-permute-start.43 = (f16[64,1024]{1,0:T(8,128)(2,1)S(1)}, f16[64,1024]{1,0:T(8,128)(2,1)S(1)}, u32[]{:S(2)}, u32[]{:S(2)}) collective-permute-start(f16[64,1024]{1,0:T(8,128)(2,1)S(1)} %add_convert_fusion), channel_id=1, source_target_pairs={{0,16},{8,24},{16,0},{24,8},{1,17},{9,25},{17,1},{25,9},{2,18},{10... | collective-permute-start | bytes 393224 | tf_op jit(solution)/shard_map/ppermute | solution.py:240
  (3 other events, 40.2 us)

commit v4 on v3

--- a/solution.py
+++ b/solution.py
@@ -153,7 +153,7 @@
     )(raw_frames.reshape(frames * rows, cols), gain_map, coupling, *extra)
 
 
-TILE = 256
+TILE = 512
 PARTS = 2
 
 
@@ -218,7 +218,7 @@
 
 def groups_of(n_pix):
     far = list(range(n_pix - 1, n_pix // 2 - 1, -1))
-    return [list(range(n_pix // 2)), far[: len(far) // 2], far[len(far) // 2 :]]
+    return [list(range(n_pix // 2)), far]
 
 
 def local(raw_frames, gain_map, coupling, factor_w, factor_h, n_scan, n_pix):
@@ -379,7 +379,8 @@
                         h_mine = h_own[c].astype(BF16)
                         h_pairs[c] = [h_mine, over_scan(h_mine, 1)]
             w_sums = pick(w_sums, keep) + weight
-    return (to_global(w_local), jnp.concatenate(h_own, axis=1))
+    w_factor = to_global(w_local)
+    return (w_factor, jnp.concatenate(h_own, axis=1))
 
 
 def solution(mesh):

time: 166 us -> 168 us (1.012)
  waiting for transfers between devices: 64.2 us -> 71.6 us
  starting transfers between devices: 67.2 us -> 63 us
    ppermute x30, waiting for transfers between devices: 31.9 us -> 39.3 us  [over_pix(): return lax.ppermute(value, 'pix', [(i, i ^ bit) for i in range(n_pix)])]
    ppermute x30, starting transfers between devices: 55.2 us -> 51.1 us  [over_pix(): return lax.ppermute(value, 'pix', [(i, i ^ bit) for i in range(n_pix)])]
    pallas_call x7 -> x6, Pallas kernels: 4.57 us -> 3.48 us  [term(): pl.pallas_call(body, out_shape=pltpu.VMEM(shape, dtype), in_specs=[VMEM]...]
  transfers between devices with their start and end apart: 46 -> 46, of which waited for: 25 -> 24; matrix products, arithmetic and copies ran while one was open for 5% -> 5% of each run, Pallas kernels for 12% -> 11%
where the time goes in v4:
time: 168 us
  waiting for transfers between devices  71.6 us (43%)
  starting transfers between devices  63 us (38%)
  Pallas kernels  20.4 us (12%)
  matrix products  6.15 us (4%)
  other arithmetic  3.46 us (2%)
    ppermute x30, starting transfers between devices, over_pix(): return lax.ppermute(value, 'pix', [(i, i ^ bit) for i in range(n_pix)])  51.1 us
    ppermute x30, waiting for transfers between devices, over_pix(): return lax.ppermute(value, 'pix', [(i, i ^ bit) for i in range(n_pix)])  39.3 us
    ppermute x16, waiting for transfers between devices, over_scan(): return lax.ppermute(value, 'scan', [(i, i ^ bit) for i in range(n_scan)])  32.4 us
    pallas_call x3, Pallas kernels, correct(): pl.pallas_call(functools.partial(stencil_body, start=start, order=order,...  16.9 us
    ppermute x16, starting transfers between devices, over_scan(): return lax.ppermute(value, 'scan', [(i, i ^ bit) for i in range(n_scan)])  12 us
    dot_general x16, matrix products, numerator_rows(): lax.dot_general(w, ratio, (((0,), (0,)), ((), ())), preferred_element_typ...  3.92 us
    pallas_call x6, Pallas kernels, term(): pl.pallas_call(body, out_shape=pltpu.VMEM(shape, dtype), in_specs=[VMEM]...  3.48 us
  transfers between devices with their start and end apart: 46, of which 24 were waited for; matrix products, arithmetic and copies ran while one was open for 5% of the time, Pallas kernels for 11%

profile of v4, /device:TPU:0, one launch (start us, length us, event | category | flops | bytes accessed | tf_op | source)
XLA Modules:
  0.0 167.5 jit_solution(10658249406181718423)
XLA Ops:
  0.6 3.0 %collective-permute-start.3 = (f32[64,2048]{1,0:T(8,128)}, f32[64,2048]{1,0:T(8,128)S(1)}, u32[]{:S(2)}, u32[]{:S(2)}) collective-permute-start(f32[64,2048]{1,0:T(8,128)} %param.9), channel_id=1, source_target_pairs={{0,16},{8,24},{16,0},{24,8},{1,17},{9,25},{17,1},{25,9},{2,18},{10... | collective-permute-start | bytes 1572872 | tf_op jit(solution)/shard_map/ppermute | solution.py:240
  3.7 1.1 constant_dynamic-update-slice_fusion.1
  4.8 11.0 %collective-permute-done.3 = f32[64,2048]{1,0:T(8,128)S(1)} collective-permute-done((f32[64,2048]{1,0:T(8,128)}, f32[64,2048]{1,0:T(8,128)S(1)}, u32[]{:S(2)}, u32[]{:S(2)}) %collective-permute-start.3) | collective-permute-done | bytes 524320 | tf_op jit(solution)/shard_map/ppermute | solution.py:240
  16.0 7.4 %charge_sharing.3 = (bf16[48,2304]{1,0:T(8,128)(2,1)}, bf16[48,2304]{1,0:T(8,128)(2,1)}, bf16[48,2304]{1,0:T(8,128)(2,1)}, bf16[48,2304]{1,0:T(8,128)(2,1)}) custom-call(f32[6144,128]{1,0:T(8,128)} %bitcast.28, f32[128,128]{1,0:T(8,128)} %gain_ref.5, f32[128,128]{1,0:T(8,128)} %couple_ref.5, f32[48,256]{1,0:T(8,128)} %refs_0_.3), custom_call_target="tpu_custom_call" | custom-call | flops 15728640 | bytes 3932160 | tf_op jit(solution)/shard_map/charge_sharing/pallas_call | solution.py:133
  23.4 1.8 %collective-permute-start = (bf16[48,2304]{1,0:T(8,128)(2,1)}, bf16[48,2304]{1,0:T(8,128)(2,1)S(1)}, u32[]{:S(2)}, u32[]{:S(2)}) collective-permute-start(bf16[48,2304]{1,0:T(8,128)(2,1)} %get-tuple-element.32), channel_id=1, source_target_pairs={{0,1},{1,0},{2,3},{3,2},{4,5},{5,4},{6,7},{7,6},{8,9},{9,8},{10,11... | collective-permute-start | bytes 663560 | tf_op jit(solution)/shard_map/ppermute | solution.py:237
  25.2 1.6 collective-permute-start.1
  26.9 5.5 %charge_sharing.4 = (bf16[32,2048]{1,0:T(8,128)(2,1)}, bf16[32,2048]{1,0:T(8,128)(2,1)}, bf16[32,2048]{1,0:T(8,128)(2,1)}, bf16[32,2048]{1,0:T(8,128)(2,1)}) custom-call(f32[6144,128]{1,0:T(8,128)} %bitcast.29, f32[128,128]{1,0:T(8,128)} %gain_ref.5, f32[128,128]{1,0:T(8,128)} %couple_ref.5), custom_call_target="tpu_custom_call" | custom-call | flops 10485760 | bytes 2621440 | tf_op jit(solution)/shard_map/charge_sharing/pallas_call | solution.py:133
  32.5 4.9 %collective-permute-start.8 = (bf16[32,2048]{1,0:T(8,128)(2,1)}, bf16[32,2048]{1,0:T(8,128)(2,1)S(1)}, u32[]{:S(2)}, u32[]{:S(2)}) collective-permute-start(bf16[32,2048]{1,0:T(8,128)(2,1)} %get-tuple-element.40), channel_id=1, source_target_pairs={{0,7},{1,6},{2,5},{3,4},{4,3},{5,2},{6,1},{7,0},{8,15},{9,14},{10,... | collective-permute-start | bytes 393224 | tf_op jit(solution)/shard_map/ppermute | solution.py:237
  37.3 4.0 %charge_sharing.5 = (bf16[16,2816]{1,0:T(8,128)(2,1)}, bf16[16,2816]{1,0:T(8,128)(2,1)}, bf16[16,2816]{1,0:T(8,128)(2,1)}, bf16[16,2816]{1,0:T(8,128)(2,1)}) custom-call(f32[6144,128]{1,0:T(8,128)} %bitcast.30, f32[128,128]{1,0:T(8,128)} %gain_ref.5, f32[128,128]{1,0:T(8,128)} %couple_ref.5, f32[48,256]{1,0:T(8,128)} %refs_0_.3), custom_call_target="tpu_custom_call" | custom-call | flops 5242880 | bytes 1310720 | tf_op jit(solution)/shard_map/charge_sharing/pallas_call | solution.py:133
  41.5 3.7 %collective-permute-start.10 = (bf16[32,2048]{1,0:T(8,128)(2,1)S(1)}, bf16[32,2048]{1,0:T(8,128)(2,1)S(1)}, u32[]{:S(2)}, u32[]{:S(2)}) collective-permute-start(bf16[32,2048]{1,0:T(8,128)(2,1)S(1)} %copy-done.4), channel_id=1, source_target_pairs={{0,6},{1,7},{2,4},{3,5},{4,2},{5,3},{6,0},{7,1},{8,14},{9,15},{10,... | collective-permute-start | bytes 393224 | tf_op jit(solution)/shard_map/ppermute | solution.py:237
  46.2 3.5 %collective-permute-done.9.refs_1_.refs_5_ = bf16[16,2816]{1,0:T(8,128)(2,1)S(1)} collective-permute-done((bf16[16,2816]{1,0:T(8,128)(2,1)}, bf16[16,2816]{1,0:T(8,128)(2,1)S(1)}, u32[]{:S(2)}, u32[]{:S(2)}) %collective-permute-start.9) | collective-permute-done | bytes 90144 | tf_op jit(solution)/shard_map/ppermute | solution.py:237
  49.8 9.5 %collective-permute-start.13 = (bf16[16,2816]{1,0:T(8,128)(2,1)}, bf16[16,2816]{1,0:T(8,128)(2,1)S(1)}, u32[]{:S(2)}, u32[]{:S(2)}) collective-permute-start(bf16[16,2816]{1,0:T(8,128)(2,1)} %get-tuple-element.45), channel_id=1, source_target_pairs={{0,5},{1,4},{2,7},{3,6},{4,1},{5,0},{6,3},{7,2},{8,13},{9,12},{10,... | collective-permute-start | bytes 270344 | tf_op jit(solution)/shard_map/ppermute | solution.py:237
  59.3 3.8 %collective-permute-start.14 = (bf16[32,2048]{1,0:T(8,128)(2,1)S(1)}, bf16[32,2048]{1,0:T(8,128)(2,1)S(1)}, u32[]{:S(2)}, u32[]{:S(2)}) collective-permute-start(bf16[32,2048]{1,0:T(8,128)(2,1)S(1)} %copy-done.2), channel_id=1, source_target_pairs={{0,4},{1,5},{2,6},{3,7},{4,0},{5,1},{6,2},{7,3},{8,12},{9,13},{10,... | collective-permute-start | bytes 393224 | tf_op jit(solution)/shard_map/ppermute | solution.py:237
  63.1 7.3 %collective-permute-done.13.refs_5_.refs_3_ = bf16[16,2816]{1,0:T(8,128)(2,1)S(1)} collective-permute-done((bf16[16,2816]{1,0:T(8,128)(2,1)}, bf16[16,2816]{1,0:T(8,128)(2,1)S(1)}, u32[]{:S(2)}, u32[]{:S(2)}) %collective-permute-start.13) | collective-permute-done | bytes 90144 | tf_op jit(solution)/shard_map/ppermute | solution.py:237
  70.5 5.6 %collective-permute-done.15.refs_7_.refs_3_ = bf16[16,2816]{1,0:T(8,128)(2,1)S(1)} collective-permute-done((bf16[16,2816]{1,0:T(8,128)(2,1)}, bf16[16,2816]{1,0:T(8,128)(2,1)S(1)}, u32[]{:S(2)}, u32[]{:S(2)}) %collective-permute-start.15) | collective-permute-done | bytes 90144 | tf_op jit(solution)/shard_map/ppermute | solution.py:237
  76.1 0.8 shard_map.69
  77.1 4.1 %collective-permute-start.19 = (f16[64,256]{1,0:T(8,128)(2,1)S(1)}, f16[64,256]{1,0:T(8,128)(2,1)S(1)}, u32[]{:S(2)}, u32[]{:S(2)}) collective-permute-start(f16[64,256]{1,0:T(8,128)(2,1)S(1)} %get-tuple-element.51), channel_id=1, source_target_pairs={{0,7},{1,6},{2,5},{3,4},{4,3},{5,2},{6,1},{7,0},{8,15},{9,14},{10,... | collective-permute-start | bytes 98312 | tf_op jit(solution)/shard_map/ppermute | solution.py:237
  81.2 0.9 collective-permute-start.18
  82.4 2.7 %collective-permute-start.16 = (f16[64,256]{1,0:T(8,128)(2,1)S(1)}, f16[64,256]{1,0:T(8,128)(2,1)S(1)}, u32[]{:S(2)}, u32[]{:S(2)}) collective-permute-start(f16[64,256]{1,0:T(8,128)(2,1)S(1)} %concatenate.112), channel_id=1, source_target_pairs={{0,4},{1,5},{2,6},{3,7},{4,0},{5,1},{6,2},{7,3},{8,12},{9,13},{10,... | collective-permute-start | bytes 98312 | tf_op jit(solution)/shard_map/ppermute | solution.py:237
  85.1 1.7 collective-permute-start.7
  86.8 1.5 collective-permute-start.6
  88.7 1.2 collective-permute-done.7
  90.7 1.5 collective-permute-done.5
  92.3 3.0 %collective-permute-start.22 = (bf16[48,256]{1,0:T(8,128)(2,1)S(1)}, bf16[48,256]{1,0:T(8,128)(2,1)S(1)}, u32[]{:S(2)}, u32[]{:S(2)}) collective-permute-start(bf16[48,256]{1,0:T(8,128)(2,1)S(1)} %get-tuple-element.72), channel_id=1, source_target_pairs={{0,6},{1,7},{2,4},{3,5},{4,2},{5,3},{6,0},{7,1},{8,14},{9,15},{10,... | collective-permute-start | bytes 73736 | tf_op jit(solution)/shard_map/ppermute | solution.py:237
  95.3 1.5 collective-permute-start.20
  96.8 1.2 collective-permute-done.22
  98.0 2.0 %collective-permute-done.21 = bf16[48,256]{1,0:T(8,128)(2,1)S(1)} collective-permute-done((bf16[48,256]{1,0:T(8,128)(2,1)S(1)}, bf16[48,256]{1,0:T(8,128)(2,1)S(1)}, u32[]{:S(2)}, u32[]{:S(2)}) %collective-permute-start.21) | collective-permute-done | bytes 24608 | tf_op jit(solution)/shard_map/ppermute | solution.py:237
  100.8 4.0 %collective-permute-done.23.refs_2_ = bf16[192,256]{1,0:T(8,128)(2,1)S(1)} collective-permute-done((bf16[192,256]{1,0:T(8,128)(2,1)S(1)}, bf16[192,256]{1,0:T(8,128)(2,1)S(1)}, u32[]{:S(2)}, u32[]{:S(2)}) %collective-permute-start.23) | collective-permute-done | bytes 98336 | tf_op jit(solution)/shard_map/ppermute | solution.py:237
  107.5 1.5 collective-permute-start.27
  109.3 1.8 %collective-permute-done.27 = f32[128]{0:T(128)S(1)} collective-permute-done((f32[128]{0:T(128)S(1)}, f32[128]{0:T(128)S(1)}, u32[]{:S(2)}, u32[]{:S(2)}) %collective-permute-start.27) | collective-permute-done | bytes 544 | tf_op jit(solution)/shard_map/ppermute | solution.py:240
  111.5 1.6 collective-permute-start.26
  114.1 6.6 %collective-permute-done.26 = f16[128,1024]{1,0:T(8,128)(2,1)S(1)} collective-permute-done((f16[128,1024]{1,0:T(8,128)(2,1)S(1)}, f16[128,1024]{1,0:T(8,128)(2,1)S(1)}, u32[]{:S(2)}, u32[]{:S(2)}) %collective-permute-start.26) | collective-permute-done | bytes 262176 | tf_op jit(solution)/shard_map/ppermute | solution.py:240
  121.1 3.7 %collective-permute-done.30 = f16[128,1024]{1,0:T(8,128)(2,1)S(1)} collective-permute-done((f16[128,1024]{1,0:T(8,128)(2,1)S(1)}, f16[128,1024]{1,0:T(8,128)(2,1)S(1)}, u32[]{:S(2)}, u32[]{:S(2)}) %collective-permute-start.30) | collective-permute-done | bytes 262176 | tf_op jit(solution)/shard_map/ppermute | solution.py:240
  125.1 1.5 collective-permute-done.31.refs_6_
  128.4 4.1 %collective-permute-done.32 = f16[208,256]{1,0:T(8,128)(2,1)S(1)} collective-permute-done((f16[208,256]{1,0:T(8,128)(2,1)S(1)}, f16[208,256]{1,0:T(8,128)(2,1)S(1)}, u32[]{:S(2)}, u32[]{:S(2)}) %collective-permute-start.32) | collective-permute-done | bytes 106528 | tf_op jit(solution)/shard_map/ppermute | solution.py:237
  132.6 1.7 %collective-permute-start.35 = (f16[64,256]{1,0:T(8,128)(2,1)S(1)}, f16[64,256]{1,0:T(8,128)(2,1)S(1)}, u32[]{:S(2)}, u32[]{:S(2)}) collective-permute-start(f16[64,256]{1,0:T(8,128)(2,1)S(1)} %concatenate.113), channel_id=1, source_target_pairs={{0,6},{1,7},{2,4},{3,5},{4,2},{5,3},{6,0},{7,1},{8,14},{9,15},{10,... | collective-permute-start | bytes 98312 | tf_op jit(solution)/shard_map/ppermute | solution.py:237
  134.8 2.3 %collective-permute-start.33 = (f16[64,256]{1,0:T(8,128)(2,1)S(1)}, f16[64,256]{1,0:T(8,128)(2,1)S(1)}, u32[]{:S(2)}, u32[]{:S(2)}) collective-permute-start(f16[64,256]{1,0:T(8,128)(2,1)S(1)} %get-tuple-element.101), channel_id=1, source_target_pairs={{0,2},{1,3},{2,0},{3,1},{4,6},{5,7},{6,4},{7,5},{8,10},{9,11},{10,... | collective-permute-start | bytes 98312 | tf_op jit(solution)/shard_map/ppermute | solution.py:237
  137.1 1.5 collective-permute-done.35
  139.4 2.4 %collective-permute-start.38 = (bf16[48,256]{1,0:T(8,128)(2,1)S(1)}, bf16[48,256]{1,0:T(8,128)(2,1)S(1)}, u32[]{:S(2)}, u32[]{:S(2)}) collective-permute-start(bf16[48,256]{1,0:T(8,128)(2,1)S(1)} %get-tuple-element.62), channel_id=1, source_target_pairs={{0,6},{1,7},{2,4},{3,5},{4,2},{5,3},{6,0},{7,1},{8,14},{9,15},{10,... | collective-permute-start | bytes 73736 | tf_op jit(solution)/shard_map/ppermute | solution.py:237
  142.6 1.3 collective-permute-start.36
  145.1 1.6 collective-permute-done.37
  147.7 3.8 %collective-permute-done.39 = bf16[192,256]{1,0:T(8,128)(2,1)S(1)} collective-permute-done((bf16[192,256]{1,0:T(8,128)(2,1)S(1)}, bf16[192,256]{1,0:T(8,128)(2,1)S(1)}, u32[]{:S(2)}, u32[]{:S(2)}) %collective-permute-start.39) | collective-permute-done | bytes 98336 | tf_op jit(solution)/shard_map/ppermute | solution.py:237
  154.1 0.9 collective-permute-done.42
  155.1 1.5 collective-permute-start.45
  156.8 1.8 %collective-permute-done.45 = f32[64]{0:T(128)S(1)} collective-permute-done((f32[64]{0:T(128)S(1)}, f32[64]{0:T(128)S(1)}, u32[]{:S(2)}, u32[]{:S(2)}) %collective-permute-start.45) | collective-permute-done | bytes 288 | tf_op jit(solution)/shard_map/ppermute | solution.py:240
  159.0 1.6 collective-permute-start.44
  161.6 3.6 %collective-permute-done.44 = f16[64,1024]{1,0:T(8,128)(2,1)S(1)} collective-permute-done((f16[64,1024]{1,0:T(8,128)(2,1)S(1)}, f16[64,1024]{1,0:T(8,128)(2,1)S(1)}, u32[]{:S(2)}, u32[]{:S(2)}) %collective-permute-start.44) | collective-permute-done | bytes 131104 | tf_op jit(solution)/shard_map/ppermute | solution.py:240
  165.3 1.3 collective-permute-done.43
  (145 shorter events, 20.3 us)
Async XLA Ops:
  0.6 15.2 %collective-permute-start.3 = (f32[64,2048]{1,0:T(8,128)}, f32[64,2048]{1,0:T(8,128)S(1)}, u32[]{:S(2)}, u32[]{:S(2)}) collective-permute-start(f32[64,2048]{1,0:T(8,128)} %param.9), channel_id=1, source_target_pairs={{0,16},{8,24},{16,0},{24,8},{1,17},{9,25},{17,1},{25,9},{2,18},{10... | collective-permute-start | bytes 1572872 | tf_op jit(solution)/shard_map/ppermute | solution.py:240
  15.9 29.4 %collective-permute-start.4 = (bf16[128,2048]{1,0:T(8,128)(2,1)S(1)}, bf16[128,2048]{1,0:T(8,128)(2,1)S(1)}, u32[]{:S(2)}, u32[]{:S(2)}) collective-permute-start(bf16[128,2048]{1,0:T(8,128)(2,1)S(1)} %convert_element_type.137.refs_4_.refs_8_), channel_id=1, source_target_pairs={{0,8},{8,0},{16,24},{24,16},{1,9},{9,1},{17,25},{25,17},{2,10},{10... | collective-permute-start | bytes 1572872 | tf_op jit(solution)/shard_map/ppermute | solution.py:240
  23.4 17.9 %collective-permute-start = (bf16[48,2304]{1,0:T(8,128)(2,1)}, bf16[48,2304]{1,0:T(8,128)(2,1)S(1)}, u32[]{:S(2)}, u32[]{:S(2)}) collective-permute-start(bf16[48,2304]{1,0:T(8,128)(2,1)} %get-tuple-element.32), channel_id=1, source_target_pairs={{0,1},{1,0},{2,3},{3,2},{4,5},{5,4},{6,7},{7,6},{8,9},{9,8},{10,11... | collective-permute-start | bytes 663560 | tf_op jit(solution)/shard_map/ppermute | solution.py:237
  25.2 16.2 %collective-permute-start.1 = (bf16[48,2304]{1,0:T(8,128)(2,1)}, bf16[48,2304]{1,0:T(8,128)(2,1)S(1)}, u32[]{:S(2)}, u32[]{:S(2)}) collective-permute-start(bf16[48,2304]{1,0:T(8,128)(2,1)} %get-tuple-element.33), channel_id=1, source_target_pairs={{0,2},{1,3},{2,0},{3,1},{4,6},{5,7},{6,4},{7,5},{8,10},{9,11},{10,... | collective-permute-start | bytes 663560 | tf_op jit(solution)/shard_map/ppermute | solution.py:237
  26.8 18.4 %collective-permute-start.2 = (bf16[48,2304]{1,0:T(8,128)(2,1)}, bf16[48,2304]{1,0:T(8,128)(2,1)S(1)}, u32[]{:S(2)}, u32[]{:S(2)}) collective-permute-start(bf16[48,2304]{1,0:T(8,128)(2,1)} %get-tuple-element.34), channel_id=1, source_target_pairs={{0,3},{1,2},{2,1},{3,0},{4,7},{5,6},{6,5},{7,4},{8,11},{9,10},{10,... | collective-permute-start | bytes 663560 | tf_op jit(solution)/shard_map/ppermute | solution.py:237
  32.5 26.8 %copy-start.2 = (bf16[32,2048]{1,0:T(8,128)(2,1)S(1)}, bf16[32,2048]{1,0:T(8,128)(2,1)}, u32[]{:S(2)}) copy-start(bf16[32,2048]{1,0:T(8,128)(2,1)} %get-tuple-element.46) | copy-start | bytes 393220
  32.5 43.6 %collective-permute-start.8 = (bf16[32,2048]{1,0:T(8,128)(2,1)}, bf16[32,2048]{1,0:T(8,128)(2,1)S(1)}, u32[]{:S(2)}, u32[]{:S(2)}) collective-permute-start(bf16[32,2048]{1,0:T(8,128)(2,1)} %get-tuple-element.40), channel_id=1, source_target_pairs={{0,7},{1,6},{2,5},{3,4},{4,3},{5,2},{6,1},{7,0},{8,15},{9,14},{10,... | collective-permute-start | bytes 393224 | tf_op jit(solution)/shard_map/ppermute | solution.py:237
  41.3 40.8 %copy-start.1 = (f32[48,256]{1,0:T(8,128)S(1)}, f32[48,256]{1,0:T(8,128)}, u32[]{:S(2)}) copy-start(f32[48,256]{1,0:T(8,128)} %refs_0_.3) | copy-start | bytes 147460
  41.3 8.5 %collective-permute-start.9 = (bf16[16,2816]{1,0:T(8,128)(2,1)}, bf16[16,2816]{1,0:T(8,128)(2,1)S(1)}, u32[]{:S(2)}, u32[]{:S(2)}) collective-permute-start(bf16[16,2816]{1,0:T(8,128)(2,1)} %get-tuple-element.41), channel_id=1, source_target_pairs={{0,7},{1,6},{2,5},{3,4},{4,3},{5,2},{6,1},{7,0},{8,15},{9,14},{10,... | collective-permute-start | bytes 270344 | tf_op jit(solution)/shard_map/ppermute | solution.py:237
  41.5 34.7 %collective-permute-start.10 = (bf16[32,2048]{1,0:T(8,128)(2,1)S(1)}, bf16[32,2048]{1,0:T(8,128)(2,1)S(1)}, u32[]{:S(2)}, u32[]{:S(2)}) collective-permute-start(bf16[32,2048]{1,0:T(8,128)(2,1)S(1)} %copy-done.4), channel_id=1, source_target_pairs={{0,6},{1,7},{2,4},{3,5},{4,2},{5,3},{6,0},{7,1},{8,14},{9,15},{10,... | collective-permute-start | bytes 393224 | tf_op jit(solution)/shard_map/ppermute | solution.py:237
  45.2 14.1 %collective-permute-start.11 = (bf16[16,2816]{1,0:T(8,128)(2,1)}, bf16[16,2816]{1,0:T(8,128)(2,1)S(1)}, u32[]{:S(2)}, u32[]{:S(2)}) collective-permute-start(bf16[16,2816]{1,0:T(8,128)(2,1)} %get-tuple-element.43), channel_id=1, source_target_pairs={{0,6},{1,7},{2,4},{3,5},{4,2},{5,3},{6,0},{7,1},{8,14},{9,15},{10,... | collective-permute-start | bytes 270344 | tf_op jit(solution)/shard_map/ppermute | solution.py:237
  45.3 30.8 %collective-permute-start.12 = (bf16[32,2048]{1,0:T(8,128)(2,1)S(1)}, bf16[32,2048]{1,0:T(8,128)(2,1)S(1)}, u32[]{:S(2)}, u32[]{:S(2)}) collective-permute-start(bf16[32,2048]{1,0:T(8,128)(2,1)S(1)} %copy-done.3), channel_id=1, source_target_pairs={{0,5},{1,4},{2,7},{3,6},{4,1},{5,0},{6,3},{7,2},{8,13},{9,12},{10,... | collective-permute-start | bytes 393224 | tf_op jit(solution)/shard_map/ppermute | solution.py:237
  49.8 20.7 %collective-permute-start.13 = (bf16[16,2816]{1,0:T(8,128)(2,1)}, bf16[16,2816]{1,0:T(8,128)(2,1)S(1)}, u32[]{:S(2)}, u32[]{:S(2)}) collective-permute-start(bf16[16,2816]{1,0:T(8,128)(2,1)} %get-tuple-element.45), channel_id=1, source_target_pairs={{0,5},{1,4},{2,7},{3,6},{4,1},{5,0},{6,3},{7,2},{8,13},{9,12},{10,... | collective-permute-start | bytes 270344 | tf_op jit(solution)/shard_map/ppermute | solution.py:237
  59.3 16.8 %collective-permute-start.14 = (bf16[32,2048]{1,0:T(8,128)(2,1)S(1)}, bf16[32,2048]{1,0:T(8,128)(2,1)S(1)}, u32[]{:S(2)}, u32[]{:S(2)}) collective-permute-start(bf16[32,2048]{1,0:T(8,128)(2,1)S(1)} %copy-done.2), channel_id=1, source_target_pairs={{0,4},{1,5},{2,6},{3,7},{4,0},{5,1},{6,2},{7,3},{8,12},{9,13},{10,... | collective-permute-start | bytes 393224 | tf_op jit(solution)/shard_map/ppermute | solution.py:237
  70.5 5.6 %collective-permute-start.15 = (bf16[16,2816]{1,0:T(8,128)(2,1)}, bf16[16,2816]{1,0:T(8,128)(2,1)S(1)}, u32[]{:S(2)}, u32[]{:S(2)}) collective-permute-start(bf16[16,2816]{1,0:T(8,128)(2,1)} %get-tuple-element.47), channel_id=1, source_target_pairs={{0,4},{1,5},{2,6},{3,7},{4,0},{5,1},{6,2},{7,3},{8,12},{9,13},{10,... | collective-permute-start | bytes 270344 | tf_op jit(solution)/shard_map/ppermute | solution.py:237
  77.1 9.7 %collective-permute-start.19 = (f16[64,256]{1,0:T(8,128)(2,1)S(1)}, f16[64,256]{1,0:T(8,128)(2,1)S(1)}, u32[]{:S(2)}, u32[]{:S(2)}) collective-permute-start(f16[64,256]{1,0:T(8,128)(2,1)S(1)} %get-tuple-element.51), channel_id=1, source_target_pairs={{0,7},{1,6},{2,5},{3,4},{4,3},{5,2},{6,1},{7,0},{8,15},{9,14},{10,... | collective-permute-start | bytes 98312 | tf_op jit(solution)/shard_map/ppermute | solution.py:237
  81.2 7.1 %collective-permute-start.18 = (f16[64,256]{1,0:T(8,128)(2,1)S(1)}, f16[64,256]{1,0:T(8,128)(2,1)S(1)}, u32[]{:S(2)}, u32[]{:S(2)}) collective-permute-start(f16[64,256]{1,0:T(8,128)(2,1)S(1)} %get-tuple-element.50), channel_id=1, source_target_pairs={{0,6},{1,7},{2,4},{3,5},{4,2},{5,3},{6,0},{7,1},{8,14},{9,15},{10,... | collective-permute-start | bytes 98312 | tf_op jit(solution)/shard_map/ppermute | solution.py:237
  82.3 6.3 %collective-permute-start.17 = (f16[64,256]{1,0:T(8,128)(2,1)S(1)}, f16[64,256]{1,0:T(8,128)(2,1)S(1)}, u32[]{:S(2)}, u32[]{:S(2)}) collective-permute-start(f16[64,256]{1,0:T(8,128)(2,1)S(1)} %get-tuple-element.49), channel_id=1, source_target_pairs={{0,5},{1,4},{2,7},{3,6},{4,1},{5,0},{6,3},{7,2},{8,13},{9,12},{10,... | collective-permute-start | bytes 98312 | tf_op jit(solution)/shard_map/ppermute | solution.py:237
  82.4 6.3 %collective-permute-start.16 = (f16[64,256]{1,0:T(8,128)(2,1)S(1)}, f16[64,256]{1,0:T(8,128)(2,1)S(1)}, u32[]{:S(2)}, u32[]{:S(2)}) collective-permute-start(f16[64,256]{1,0:T(8,128)(2,1)S(1)} %concatenate.112), channel_id=1, source_target_pairs={{0,4},{1,5},{2,6},{3,7},{4,0},{5,1},{6,2},{7,3},{8,12},{9,13},{10,... | collective-permute-start | bytes 98312 | tf_op jit(solution)/shard_map/ppermute | solution.py:237
  85.1 4.8 %collective-permute-start.7 = (f16[64,256]{1,0:T(8,128)(2,1)S(1)}, f16[64,256]{1,0:T(8,128)(2,1)S(1)}, u32[]{:S(2)}, u32[]{:S(2)}) collective-permute-start(f16[64,256]{1,0:T(8,128)(2,1)S(1)} %concatenate.111), channel_id=1, source_target_pairs={{0,3},{1,2},{2,1},{3,0},{4,7},{5,6},{6,5},{7,4},{8,11},{9,10},{10,... | collective-permute-start | bytes 98312 | tf_op jit(solution)/shard_map/ppermute | solution.py:237
  86.8 3.9 %collective-permute-start.6 = (f16[64,256]{1,0:T(8,128)(2,1)S(1)}, f16[64,256]{1,0:T(8,128)(2,1)S(1)}, u32[]{:S(2)}, u32[]{:S(2)}) collective-permute-start(f16[64,256]{1,0:T(8,128)(2,1)S(1)} %get-tuple-element.36), channel_id=1, source_target_pairs={{0,2},{1,3},{2,0},{3,1},{4,6},{5,7},{6,4},{7,5},{8,10},{9,11},{10,... | collective-permute-start | bytes 98312 | tf_op jit(solution)/shard_map/ppermute | solution.py:237
  88.3 3.9 %collective-permute-start.5 = (f16[64,256]{1,0:T(8,128)(2,1)S(1)}, f16[64,256]{1,0:T(8,128)(2,1)S(1)}, u32[]{:S(2)}, u32[]{:S(2)}) collective-permute-start(f16[64,256]{1,0:T(8,128)(2,1)S(1)} %get-tuple-element.35), channel_id=1, source_target_pairs={{0,1},{1,0},{2,3},{3,2},{4,5},{5,4},{6,7},{7,6},{8,9},{9,8},{10,11... | collective-permute-start | bytes 98312 | tf_op jit(solution)/shard_map/ppermute | solution.py:237
  92.3 5.7 %collective-permute-start.22 = (bf16[48,256]{1,0:T(8,128)(2,1)S(1)}, bf16[48,256]{1,0:T(8,128)(2,1)S(1)}, u32[]{:S(2)}, u32[]{:S(2)}) collective-permute-start(bf16[48,256]{1,0:T(8,128)(2,1)S(1)} %get-tuple-element.72), channel_id=1, source_target_pairs={{0,6},{1,7},{2,4},{3,5},{4,2},{5,3},{6,0},{7,1},{8,14},{9,15},{10,... | collective-permute-start | bytes 73736 | tf_op jit(solution)/shard_map/ppermute | solution.py:237
  95.3 4.7 %collective-permute-start.21 = (bf16[48,256]{1,0:T(8,128)(2,1)S(1)}, bf16[48,256]{1,0:T(8,128)(2,1)S(1)}, u32[]{:S(2)}, u32[]{:S(2)}) collective-permute-start(bf16[48,256]{1,0:T(8,128)(2,1)S(1)} %get-tuple-element.72), channel_id=1, source_target_pairs={{0,4},{1,5},{2,6},{3,7},{4,0},{5,1},{6,2},{7,3},{8,12},{9,13},{10,... | collective-permute-start | bytes 73736 | tf_op jit(solution)/shard_map/ppermute | solution.py:237
  95.3 4.7 %collective-permute-start.20 = (bf16[48,256]{1,0:T(8,128)(2,1)S(1)}, bf16[48,256]{1,0:T(8,128)(2,1)S(1)}, u32[]{:S(2)}, u32[]{:S(2)}) collective-permute-start(bf16[48,256]{1,0:T(8,128)(2,1)S(1)} %get-tuple-element.72), channel_id=1, source_target_pairs={{0,2},{1,3},{2,0},{3,1},{4,6},{5,7},{6,4},{7,5},{8,10},{9,11},{10,... | collective-permute-start | bytes 73736 | tf_op jit(solution)/shard_map/ppermute | solution.py:237
  100.0 4.7 %collective-permute-start.23 = (bf16[192,256]{1,0:T(8,128)(2,1)S(1)}, bf16[192,256]{1,0:T(8,128)(2,1)S(1)}, u32[]{:S(2)}, u32[]{:S(2)}) collective-permute-start(bf16[192,256]{1,0:T(8,128)(2,1)S(1)} %get-tuple-element.71.refs_2_), channel_id=1, source_target_pairs={{0,1},{1,0},{2,3},{3,2},{4,5},{5,4},{6,7},{7,6},{8,9},{9,8},{10,11... | collective-permute-start | bytes 294920 | tf_op jit(solution)/shard_map/ppermute | solution.py:237
  104.8 2.6 %collective-permute-start.25 = (f32[128]{0:T(128)S(1)}, f32[128]{0:T(128)S(1)}, u32[]{:S(2)}, u32[]{:S(2)}) collective-permute-start(f32[128]{0:T(128)S(1)} %slice.259), channel_id=1, source_target_pairs={{0,8},{8,0},{16,24},{24,16},{1,9},{9,1},{17,25},{25,17},{2,10},{10... | collective-permute-start | bytes 1544 | tf_op jit(solution)/shard_map/ppermute | solution.py:240
  105.7 5.4 %collective-permute-start.24 = (f32[128,1024]{1,0:T(8,128)S(1)}, f32[128,1024]{1,0:T(8,128)S(1)}, u32[]{:S(2)}, u32[]{:S(2)}) collective-permute-start(f32[128,1024]{1,0:T(8,128)S(1)} %convolution_add_fusion.6), channel_id=1, source_target_pairs={{0,8},{8,0},{16,24},{24,16},{1,9},{9,1},{17,25},{25,17},{2,10},{10... | collective-permute-start | bytes 1572872 | tf_op jit(solution)/shard_map/ppermute | solution.py:240
  107.3 5.8 %collective-permute-start.29 = (f32[128,1024]{1,0:T(8,128)S(1)}, f32[128,1024]{1,0:T(8,128)S(1)}, u32[]{:S(2)}, u32[]{:S(2)}) collective-permute-start(f32[128,1024]{1,0:T(8,128)S(1)} %convolution_add_fusion.4), channel_id=1, source_target_pairs={{0,8},{8,0},{16,24},{24,16},{1,9},{9,1},{17,25},{25,17},{2,10},{10... | collective-permute-start | bytes 1572872 | tf_op jit(solution)/shard_map/ppermute | solution.py:240
  107.5 3.6 %collective-permute-start.27 = (f32[128]{0:T(128)S(1)}, f32[128]{0:T(128)S(1)}, u32[]{:S(2)}, u32[]{:S(2)}) collective-permute-start(f32[128]{0:T(128)S(1)} %pad_maximum_fusion.23), channel_id=1, source_target_pairs={{0,16},{8,24},{16,0},{24,8},{1,17},{9,25},{17,1},{25,9},{2,18},{10... | collective-permute-start | bytes 1544 | tf_op jit(solution)/shard_map/ppermute | solution.py:240
  111.5 9.2 %collective-permute-start.26 = (f16[128,1024]{1,0:T(8,128)(2,1)S(1)}, f16[128,1024]{1,0:T(8,128)(2,1)S(1)}, u32[]{:S(2)}, u32[]{:S(2)}) collective-permute-start(f16[128,1024]{1,0:T(8,128)(2,1)S(1)} %fusion.15), channel_id=1, source_target_pairs={{0,16},{8,24},{16,0},{24,8},{1,17},{9,25},{17,1},{25,9},{2,18},{10... | collective-permute-start | bytes 786440 | tf_op jit(solution)/shard_map/ppermute | solution.py:240
  113.5 11.2 %collective-permute-start.30 = (f16[128,1024]{1,0:T(8,128)(2,1)S(1)}, f16[128,1024]{1,0:T(8,128)(2,1)S(1)}, u32[]{:S(2)}, u32[]{:S(2)}) collective-permute-start(f16[128,1024]{1,0:T(8,128)(2,1)S(1)} %fusion.17), channel_id=1, source_target_pairs={{0,16},{8,24},{16,0},{24,8},{1,17},{9,25},{17,1},{25,9},{2,18},{10... | collective-permute-start | bytes 786440 | tf_op jit(solution)/shard_map/ppermute | solution.py:240
  121.0 4.1 %collective-permute-start.28 = (bf16[128,1024]{1,0:T(8,128)(2,1)S(1)}, bf16[128,1024]{1,0:T(8,128)(2,1)S(1)}, u32[]{:S(2)}, u32[]{:S(2)}) collective-permute-start(bf16[128,1024]{1,0:T(8,128)(2,1)S(1)} %get-tuple-element.68.refs_3_), channel_id=1, source_target_pairs={{0,8},{8,0},{16,24},{24,16},{1,9},{9,1},{17,25},{25,17},{2,10},{10... | collective-permute-start | bytes 786440 | tf_op jit(solution)/shard_map/ppermute | solution.py:240
  125.0 1.6 collective-permute-start.31
  127.4 5.1 %collective-permute-start.32 = (f16[208,256]{1,0:T(8,128)(2,1)S(1)}, f16[208,256]{1,0:T(8,128)(2,1)S(1)}, u32[]{:S(2)}, u32[]{:S(2)}) collective-permute-start(f16[208,256]{1,0:T(8,128)(2,1)S(1)} %convert_element_type.162), channel_id=1, source_target_pairs={{0,1},{1,0},{2,3},{3,2},{4,5},{5,4},{6,7},{7,6},{8,9},{9,8},{10,11... | collective-permute-start | bytes 319496 | tf_op jit(solution)/shard_map/ppermute | solution.py:237
  132.6 6.1 %collective-permute-start.35 = (f16[64,256]{1,0:T(8,128)(2,1)S(1)}, f16[64,256]{1,0:T(8,128)(2,1)S(1)}, u32[]{:S(2)}, u32[]{:S(2)}) collective-permute-start(f16[64,256]{1,0:T(8,128)(2,1)S(1)} %concatenate.113), channel_id=1, source_target_pairs={{0,6},{1,7},{2,4},{3,5},{4,2},{5,3},{6,0},{7,1},{8,14},{9,15},{10,... | collective-permute-start | bytes 98312 | tf_op jit(solution)/shard_map/ppermute | solution.py:237
  134.4 5.0 %collective-permute-start.34 = (f16[64,256]{1,0:T(8,128)(2,1)S(1)}, f16[64,256]{1,0:T(8,128)(2,1)S(1)}, u32[]{:S(2)}, u32[]{:S(2)}) collective-permute-start(f16[64,256]{1,0:T(8,128)(2,1)S(1)} %get-tuple-element.102), channel_id=1, source_target_pairs={{0,4},{1,5},{2,6},{3,7},{4,0},{5,1},{6,2},{7,3},{8,12},{9,13},{10,... | collective-permute-start | bytes 98312 | tf_op jit(solution)/shard_map/ppermute | solution.py:237
  134.8 4.6 %collective-permute-start.33 = (f16[64,256]{1,0:T(8,128)(2,1)S(1)}, f16[64,256]{1,0:T(8,128)(2,1)S(1)}, u32[]{:S(2)}, u32[]{:S(2)}) collective-permute-start(f16[64,256]{1,0:T(8,128)(2,1)S(1)} %get-tuple-element.101), channel_id=1, source_target_pairs={{0,2},{1,3},{2,0},{3,1},{4,6},{5,7},{6,4},{7,5},{8,10},{9,11},{10,... | collective-permute-start | bytes 98312 | tf_op jit(solution)/shard_map/ppermute | solution.py:237
  139.4 5.7 %collective-permute-start.38 = (bf16[48,256]{1,0:T(8,128)(2,1)S(1)}, bf16[48,256]{1,0:T(8,128)(2,1)S(1)}, u32[]{:S(2)}, u32[]{:S(2)}) collective-permute-start(bf16[48,256]{1,0:T(8,128)(2,1)S(1)} %get-tuple-element.62), channel_id=1, source_target_pairs={{0,6},{1,7},{2,4},{3,5},{4,2},{5,3},{6,0},{7,1},{8,14},{9,15},{10,... | collective-permute-start | bytes 73736 | tf_op jit(solution)/shard_map/ppermute | solution.py:237
  141.9 4.8 %collective-permute-start.37 = (bf16[48,256]{1,0:T(8,128)(2,1)S(1)}, bf16[48,256]{1,0:T(8,128)(2,1)S(1)}, u32[]{:S(2)}, u32[]{:S(2)}) collective-permute-start(bf16[48,256]{1,0:T(8,128)(2,1)S(1)} %get-tuple-element.62), channel_id=1, source_target_pairs={{0,4},{1,5},{2,6},{3,7},{4,0},{5,1},{6,2},{7,3},{8,12},{9,13},{10,... | collective-permute-start | bytes 73736 | tf_op jit(solution)/shard_map/ppermute | solution.py:237
  142.6 4.1 %collective-permute-start.36 = (bf16[48,256]{1,0:T(8,128)(2,1)S(1)}, bf16[48,256]{1,0:T(8,128)(2,1)S(1)}, u32[]{:S(2)}, u32[]{:S(2)}) collective-permute-start(bf16[48,256]{1,0:T(8,128)(2,1)S(1)} %get-tuple-element.62), channel_id=1, source_target_pairs={{0,2},{1,3},{2,0},{3,1},{4,6},{5,7},{6,4},{7,5},{8,10},{9,11},{10,... | collective-permute-start | bytes 73736 | tf_op jit(solution)/shard_map/ppermute | solution.py:237
  146.8 4.7 %collective-permute-start.39 = (bf16[192,256]{1,0:T(8,128)(2,1)S(1)}, bf16[192,256]{1,0:T(8,128)(2,1)S(1)}, u32[]{:S(2)}, u32[]{:S(2)}) collective-permute-start(bf16[192,256]{1,0:T(8,128)(2,1)S(1)} %get-tuple-element.61), channel_id=1, source_target_pairs={{0,1},{1,0},{2,3},{3,2},{4,5},{5,4},{6,7},{7,6},{8,9},{9,8},{10,11... | collective-permute-start | bytes 294920 | tf_op jit(solution)/shard_map/ppermute | solution.py:237
  153.0 5.6 %collective-permute-start.41 = (f32[128,1024]{1,0:T(8,128)S(1)}, f32[128,1024]{1,0:T(8,128)S(1)}, u32[]{:S(2)}, u32[]{:S(2)}) collective-permute-start(f32[128,1024]{1,0:T(8,128)S(1)} %convolution_add_fusion.2), channel_id=1, source_target_pairs={{0,8},{8,0},{16,24},{24,16},{1,9},{9,1},{17,25},{25,17},{2,10},{10... | collective-permute-start | bytes 1572872 | tf_op jit(solution)/shard_map/ppermute | solution.py:240
  153.2 1.8 %collective-permute-start.42 = (f32[128]{0:T(128)S(1)}, f32[128]{0:T(128)S(1)}, u32[]{:S(2)}, u32[]{:S(2)}) collective-permute-start(f32[128]{0:T(128)S(1)} %slice.290), channel_id=1, source_target_pairs={{0,8},{8,0},{16,24},{24,16},{1,9},{9,1},{17,25},{25,17},{2,10},{10... | collective-permute-start | bytes 1544 | tf_op jit(solution)/shard_map/ppermute | solution.py:240
  154.0 6.6 %collective-permute-start.40 = (f32[128,1024]{1,0:T(8,128)S(1)}, f32[128,1024]{1,0:T(8,128)S(1)}, u32[]{:S(2)}, u32[]{:S(2)}) collective-permute-start(f32[128,1024]{1,0:T(8,128)S(1)} %convolution_add_fusion.1), channel_id=1, source_target_pairs={{0,8},{8,0},{16,24},{24,16},{1,9},{9,1},{17,25},{25,17},{2,10},{10... | collective-permute-start | bytes 1572872 | tf_op jit(solution)/shard_map/ppermute | solution.py:240
  155.1 3.6 %collective-permute-start.45 = (f32[64]{0:T(128)S(1)}, f32[64]{0:T(128)S(1)}, u32[]{:S(2)}, u32[]{:S(2)}) collective-permute-start(f32[64]{0:T(128)S(1)} %slice.291), channel_id=1, source_target_pairs={{0,16},{8,24},{16,0},{24,8},{1,17},{9,25},{17,1},{25,9},{2,18},{10... | collective-permute-start | bytes 776 | tf_op jit(solution)/shard_map/ppermute | solution.py:240
  159.0 6.1 %collective-permute-start.44 = (f16[64,1024]{1,0:T(8,128)(2,1)S(1)}, f16[64,1024]{1,0:T(8,128)(2,1)S(1)}, u32[]{:S(2)}, u32[]{:S(2)}) collective-permute-start(f16[64,1024]{1,0:T(8,128)(2,1)S(1)} %fusion.23), channel_id=1, source_target_pairs={{0,16},{8,24},{16,0},{24,8},{1,17},{9,25},{17,1},{25,9},{2,18},{10... | collective-permute-start | bytes 393224 | tf_op jit(solution)/shard_map/ppermute | solution.py:240
  161.0 5.6 %collective-permute-start.43 = (f16[64,1024]{1,0:T(8,128)(2,1)S(1)}, f16[64,1024]{1,0:T(8,128)(2,1)S(1)}, u32[]{:S(2)}, u32[]{:S(2)}) collective-permute-start(f16[64,1024]{1,0:T(8,128)(2,1)S(1)} %add_convert_fusion), channel_id=1, source_target_pairs={{0,16},{8,24},{16,0},{24,8},{1,17},{9,25},{17,1},{25,9},{2,18},{10... | collective-permute-start | bytes 393224 | tf_op jit(solution)/shard_map/ppermute | solution.py:240
  (3 other events, 40.4 us)
